TPU v7x, 32 devices: a whole 2x2x4 slice. The times are simulated.
32 devices in a mesh: wide: 8 (over y, x, core), narrow: 4 (over z).
Axes of the slice: x: 2, y: 2, z: 4, core: 2. Of those that a mesh axis runs over, the one named last changes fastest.
Arguments:
- tokens: bfloat16 [16, 1024, 768], P('wide', 'narrow'), may hold values from -6 to 6
- step_ids: int32 [16], P('wide'), may hold values from 0 to 999
- prefix: int32 [16], P('wide'), may hold values from 1 to 1024, as said below
- keep_bits: int32 [16, 1024], P('wide'), may hold values 0 or 1
- ada_weight: bfloat16 [4608, 128], replicated, may hold values from -0.5 to 0.5
- ada_bias: float32 [4608], replicated, may hold values from -3 to 3
- norm1_gain: float32 [768], replicated, may hold values from 0.5 to 1.5
- qkv_weight: bfloat16 [768, 2304], replicated, may hold values from -0.21875 to 0.21875
- out_weight: bfloat16 [768, 768], replicated, may hold values from -6 to 6
- norm2_gain: float32 [768], replicated, may hold values from 0.5 to 1.5
- up_weight: bfloat16 [768, 3072], replicated, may hold values from -0.21875 to 0.21875
- up_bias: float32 [3072], replicated, may hold values from -3 to 3
- down_weight: bfloat16 [3072, 768], replicated, may hold values from -0.21875 to 0.21875
- down_bias: float32 [768], replicated, may hold values from -3 to 3
- cotangent: bfloat16 [16, 1024, 768], P('wide', 'narrow'), may hold values from -6 to 6
Outputs:
- out_tokens: bfloat16 [16, 1024, 768], P('wide', 'narrow')
- input_grad: bfloat16 [16, 1024, 768], P('wide', 'narrow')
- ada_weight_grad: float32 [4608, 128], replicated
- ada_bias_grad: float32 [4608], replicated
- norm1_gain_grad: float32 [768], replicated
- qkv_weight_grad: float32 [768, 2304], replicated
- out_weight_grad: float32 [768, 768], replicated
- norm2_gain_grad: float32 [768], replicated
- up_weight_grad: float32 [768, 3072], replicated
- up_bias_grad: float32 [3072], replicated
- down_weight_grad: float32 [3072, 768], replicated
- down_bias_grad: float32 [768], replicated
Inputs may be any that keep to these rules, and one draw needn't show every extreme that they name: Every prefix keeps at least the first position visible; of the 2 consecutive sequences of each index of wide, one has the whole length 1024 as prefix.
All inputs are finite; a program needn't handle non-finite values. No bound on the sum of `keep_bits` on one device may be relied on, other than what follows from the above.
Results may differ from a plain program's by a relative error of at most 0.015.
Values may be sent and summed in bfloat16 or wider, within the bound.
A program may use at most 192 MiB of HBM per device.

v0:
```python
import functools
import math

import jax
import jax.numpy as jnp
from jax import lax
from jax.sharding import PartitionSpec as P

HEAD = 64
TEMB = 128
MICRO = 2


norm_epsilon = 1e-05
gelu_coeff = 0.7978845608028654
masked_score = -1e30


def shifted(block, axis, distance):
    devices = range(lax.axis_size(axis))
    route = [((i - distance) % len(devices), i) for i in devices]
    return lax.ppermute(block, axis, route)


def time_embed(step_ids):
    halfway = TEMB // 2
    frequency = jnp.exp(jnp.arange(halfway, dtype=jnp.float32) * (-math.log(10000.0) / halfway))
    angles = step_ids.astype(jnp.float32)[:, None] * frequency[None, :]
    return jnp.concatenate([jnp.cos(angles), jnp.sin(angles)], axis=-1)


def rope_tables(positions):
    halfway = HEAD // 2
    inverse = jnp.exp(jnp.arange(halfway, dtype=jnp.float32) * (-2.0 * math.log(10000.0) / HEAD))
    angles = positions[:, None] * inverse[None, :]
    return (jnp.cos(angles), jnp.sin(angles))


def rotate(values, cosine_rows, sine_rows):
    halfway = values.shape[-1] // 2
    former = values[..., :halfway]
    latter = values[..., halfway:]
    cos_wide = cosine_rows[:, None, :]
    sin_wide = sine_rows[:, None, :]
    return jnp.concatenate(
        [former * cos_wide - latter * sin_wide, latter * cos_wide + former * sin_wide], axis=-1
    )


def rotate_back(incoming, cosine_rows, sine_rows):
    halfway = incoming.shape[-1] // 2
    former = incoming[..., :halfway]
    latter = incoming[..., halfway:]
    cos_wide = cosine_rows[:, None, :]
    sin_wide = sine_rows[:, None, :]
    return jnp.concatenate(
        [former * cos_wide + latter * sin_wide, latter * cos_wide - former * sin_wide], axis=-1
    )


def layer_norm(values, scaling):
    center = values - jnp.mean(values, axis=-1, keepdims=True)
    spread = jnp.mean(center * center, axis=-1, keepdims=True)
    return center * lax.rsqrt(spread + norm_epsilon) * scaling


def modulate(values, scaling, shift_rows, scale_rows):
    return layer_norm(values, scaling) * (1.0 + scale_rows) + shift_rows


def gelu_tanh(values):
    inner_arg = gelu_coeff * (values + 0.044715 * values * values * values)
    return 0.5 * values * (1.0 + jnp.tanh(inner_arg))


def pass_pairs(pair_block):
    return shifted(pair_block, "narrow", 1)


def pass_pairs_again(pair_block):
    return shifted(pair_block, "narrow", 1)


def pass_grads(grad_block):
    return shifted(grad_block.astype(jnp.bfloat16), "narrow", 1).astype(grad_block.dtype)


def add_trees(former_tree, latter_tree):
    return jax.tree.map(jnp.add, former_tree, latter_tree)


def local(
    tokens,
    step_ids,
    prefix,
    keep_bits,
    ada_weight,
    ada_bias,
    norm1_gain,
    qkv_weight,
    out_weight,
    norm2_gain,
    up_weight,
    up_bias,
    down_weight,
    down_bias,
    cotangent,
):
    cycle_size = lax.axis_size("narrow")
    cycle_index = lax.axis_index("narrow")
    groups, span_size, width = tokens.shape
    per_micro = groups // MICRO
    head_count = width // HEAD
    score_scale = HEAD ** (-0.5)
    offsets = jnp.arange(span_size, dtype=jnp.int32)
    cosine_rows, sine_rows = rope_tables((cycle_index * span_size + offsets).astype(jnp.float32))
    condition = jax.nn.silu(time_embed(step_ids))
    modulation = (
        jnp.dot(
            condition,
            ada_weight.astype(jnp.float32).T,
            precision=lax.Precision.HIGHEST,
            preferred_element_type=jnp.float32,
        )
        + ada_bias
    )
    last_source = (cycle_index + 1) % cycle_size
    outputs = []
    input_grads = []
    collected = []
    for micro_index in range(MICRO):
        picked = slice(micro_index * per_micro, (micro_index + 1) * per_micro)
        inputs = tokens[picked].astype(jnp.float32)
        leading = prefix[picked]
        bits_here = keep_bits[picked]
        shift_one, scale_one, gate_one, shift_two, scale_two, gate_two = jnp.split(
            modulation[picked][:, None, :], 6, axis=-1
        )
        normed, norm_back = jax.vjp(modulate, inputs, norm1_gain, shift_one, scale_one)
        normed_low = normed.astype(jnp.bfloat16)
        projected = jnp.einsum(
            "bcd,de->bce", normed_low, qkv_weight, preferred_element_type=jnp.float32
        )
        shaped = projected.reshape(per_micro, span_size, 3, head_count, HEAD)
        queries = rotate(shaped[:, :, 0], cosine_rows, sine_rows).astype(jnp.bfloat16)
        key_rows = (
            rotate(shaped[:, :, 1], cosine_rows, sine_rows)
            .astype(jnp.bfloat16)
            .reshape(per_micro, span_size, width)
        )
        value_rows = shaped[:, :, 2].astype(jnp.bfloat16).reshape(per_micro, span_size, width)
        pair_rows = jnp.stack([key_rows, value_rows])

        def visible_keys(source):
            first_key = source * span_size
            window = lax.dynamic_slice_in_dim(bits_here, first_key, span_size, 1)
            allowed = ((first_key + offsets)[None, :] < leading[:, None]) | (window == 1)
            return allowed[:, None, None, :]

        def key_scores(key_block):
            shaped_keys = key_block.reshape(per_micro, span_size, head_count, HEAD)
            return (
                jnp.einsum(
                    "bqhe,bkhe->bhqk", queries, shaped_keys, preferred_element_type=jnp.float32
                )
                * score_scale
            )

        def add_online(pair_block, source, running):
            highest, total_sum, summed = running
            scores = key_scores(pair_block[0])
            allowed = visible_keys(source)
            block_high = jnp.max(jnp.where(allowed, scores, masked_score), axis=-1)
            new_high = jnp.maximum(highest, block_high)
            factor = jnp.exp(highest - new_high)
            exp_terms = jnp.where(allowed, jnp.exp(scores - new_high[..., None]), 0.0)
            total_sum = total_sum * factor + jnp.sum(exp_terms, axis=-1)
            shaped_values = pair_block[1].reshape(per_micro, span_size, head_count, HEAD)
            summed = summed * jnp.transpose(factor, (0, 2, 1))[..., None] + jnp.einsum(
                "bhqk,bkhe->bqhe",
                exp_terms.astype(jnp.bfloat16),
                shaped_values,
                preferred_element_type=jnp.float32,
            )
            return (new_high, total_sum, summed)

        start_stats = (
            jnp.full((per_micro, head_count, span_size), masked_score, jnp.float32),
            jnp.zeros((per_micro, head_count, span_size), jnp.float32),
        )
        start_sum = jnp.zeros((per_micro, span_size, head_count, HEAD), jnp.float32)

        def online_turn(turn_index, carried):
            pair_block, running = carried
            running = add_online(pair_block, (cycle_index - turn_index) % cycle_size, running)
            return (pass_pairs(pair_block), running)

        pair_block, running = lax.fori_loop(
            0, cycle_size - 1, online_turn, (pair_rows, (start_stats[0], start_stats[1], start_sum))
        )
        highest, total_sum, summed = add_online(pair_block, last_source, running)
        attended = summed / jnp.transpose(total_sum, (0, 2, 1))[..., None]
        log_total = highest + jnp.log(total_sum)
        attended_low = attended.reshape(per_micro, span_size, width).astype(jnp.bfloat16)
        branch_one = jnp.einsum(
            "bcd,de->bce", attended_low, out_weight, preferred_element_type=jnp.float32
        )
        middle = inputs + gate_one * branch_one
        normed_two, norm_back_two = jax.vjp(modulate, middle, norm2_gain, shift_two, scale_two)
        normed_two_low = normed_two.astype(jnp.bfloat16)
        hidden = (
            jnp.einsum("bcd,df->bcf", normed_two_low, up_weight, preferred_element_type=jnp.float32)
            + up_bias
        )
        active, gelu_back = jax.vjp(gelu_tanh, hidden)
        active_low = active.astype(jnp.bfloat16)
        branch_two = (
            jnp.einsum("bcf,fd->bcd", active_low, down_weight, preferred_element_type=jnp.float32)
            + down_bias
        )
        outputs.append((middle + gate_two * branch_two).astype(jnp.bfloat16))
        out_grad = cotangent[picked].astype(jnp.float32)
        gate_two_grad = jnp.sum(out_grad * branch_two, axis=1, keepdims=True)
        branch_two_grad = (gate_two * out_grad).astype(jnp.bfloat16)
        down_grad = jnp.einsum(
            "bcf,bcd->fd", active_low, branch_two_grad, preferred_element_type=jnp.float32
        )
        down_bias_grad = jnp.sum(branch_two_grad.astype(jnp.float32), axis=(0, 1))
        (hidden_grad,) = gelu_back(
            jnp.einsum(
                "bcd,fd->bcf", branch_two_grad, down_weight, preferred_element_type=jnp.float32
            )
        )
        hidden_low = hidden_grad.astype(jnp.bfloat16)
        up_grad = jnp.einsum(
            "bcd,bcf->df", normed_two_low, hidden_low, preferred_element_type=jnp.float32
        )
        up_bias_grad = jnp.sum(hidden_low.astype(jnp.float32), axis=(0, 1))
        middle_part, gain_two_grad, shift_two_grad, scale_two_grad = norm_back_two(
            jnp.einsum("bcf,df->bcd", hidden_low, up_weight, preferred_element_type=jnp.float32)
        )
        middle_grad = out_grad + middle_part
        gate_one_grad = jnp.sum(middle_grad * branch_one, axis=1, keepdims=True)
        branch_one_grad = (gate_one * middle_grad).astype(jnp.bfloat16)
        out_weight_part = jnp.einsum(
            "bcd,bce->de", attended_low, branch_one_grad, preferred_element_type=jnp.float32
        )
        attended_grad = (
            jnp.einsum(
                "bce,de->bcd", branch_one_grad, out_weight, preferred_element_type=jnp.float32
            )
            .astype(jnp.bfloat16)
            .reshape(per_micro, span_size, head_count, HEAD)
        )
        row_delta = jnp.einsum("bqhe,bqhe->bhq", attended_grad.astype(jnp.float32), attended)

        def add_grads(pair_block, source, query_grad):
            scores = key_scores(pair_block[0])
            prob_rows = jnp.where(visible_keys(source), jnp.exp(scores - log_total[..., None]), 0.0)
            shaped_keys = pair_block[0].reshape(per_micro, span_size, head_count, HEAD)
            shaped_values = pair_block[1].reshape(per_micro, span_size, head_count, HEAD)
            value_part = jnp.einsum(
                "bhqk,bqhe->bkhe",
                prob_rows.astype(jnp.bfloat16),
                attended_grad,
                preferred_element_type=jnp.float32,
            )
            prob_grad = jnp.einsum(
                "bqhe,bkhe->bhqk", attended_grad, shaped_values, preferred_element_type=jnp.float32
            )
            score_grad = (prob_rows * (prob_grad - row_delta[..., None])).astype(jnp.bfloat16)
            query_grad = (
                query_grad
                + jnp.einsum(
                    "bhqk,bkhe->bqhe", score_grad, shaped_keys, preferred_element_type=jnp.float32
                )
                * score_scale
            )
            key_part = (
                jnp.einsum(
                    "bhqk,bqhe->bkhe", score_grad, queries, preferred_element_type=jnp.float32
                )
                * score_scale
            )
            return (
                query_grad,
                jnp.stack(
                    [
                        key_part.reshape(per_micro, span_size, width),
                        value_part.reshape(per_micro, span_size, width),
                    ]
                ),
            )

        start_query = jnp.zeros((per_micro, span_size, head_count, HEAD), jnp.float32)

        def grads_turn(turn_index, carried):
            pair_block, grad_block, query_grad = carried
            query_grad, key_value_part = add_grads(
                pair_block, (cycle_index - turn_index) % cycle_size, query_grad
            )
            return (
                pass_pairs_again(pair_block),
                pass_grads(grad_block + key_value_part),
                query_grad,
            )

        start_grads = jnp.zeros((2, per_micro, span_size, width), jnp.float32)
        pair_block, grad_block, query_grad = lax.fori_loop(
            0, cycle_size - 1, grads_turn, (pair_rows, start_grads, start_query)
        )
        query_grad, key_value_part = add_grads(pair_block, last_source, query_grad)
        pair_grads = pass_grads(grad_block + key_value_part)
        query_pre = rotate_back(query_grad, cosine_rows, sine_rows).reshape(
            per_micro, span_size, width
        )
        key_pre = rotate_back(
            pair_grads[0].reshape(per_micro, span_size, head_count, HEAD), cosine_rows, sine_rows
        ).reshape(per_micro, span_size, width)
        joined = jnp.concatenate([query_pre, key_pre, pair_grads[1]], axis=-1).astype(jnp.bfloat16)
        qkv_grad = jnp.einsum("bcd,bce->de", normed_low, joined, preferred_element_type=jnp.float32)
        input_part, gain_one_grad, shift_one_grad, scale_one_grad = norm_back(
            jnp.einsum("bce,de->bcd", joined, qkv_weight, preferred_element_type=jnp.float32)
        )
        input_grads.append((middle_grad + input_part).astype(jnp.bfloat16))
        mod_grad = jnp.concatenate(
            [
                shift_one_grad,
                scale_one_grad,
                gate_one_grad,
                shift_two_grad,
                scale_two_grad,
                gate_two_grad,
            ],
            axis=-1,
        )[:, 0, :]
        ada_grad = jnp.dot(
            mod_grad.T,
            condition[picked],
            precision=lax.Precision.HIGHEST,
            preferred_element_type=jnp.float32,
        )
        ada_bias_grad = jnp.sum(mod_grad, axis=0)
        collected.append(
            (
                ada_grad,
                ada_bias_grad,
                gain_one_grad,
                qkv_grad,
                out_weight_part,
                gain_two_grad,
                up_grad,
                up_bias_grad,
                down_grad,
                down_bias_grad,
            )
        )
    summed = functools.reduce(add_trees, collected)
    finals = lax.psum(
        (
            summed[0],
            summed[1],
            summed[2],
            summed[3],
            summed[4],
            summed[5],
            summed[6],
            summed[7],
            summed[8],
            summed[9],
        ),
        ("wide", "narrow"),
    )
    return (
        jnp.concatenate(outputs, axis=0),
        jnp.concatenate(input_grads, axis=0),
        finals[0],
        finals[1],
        finals[2],
        finals[3],
        finals[4],
        finals[5],
        finals[6],
        finals[7],
        finals[8],
        finals[9],
    )


def solution(mesh):
    in_specs = (
        P("wide", "narrow", None),
        P("wide"),
        P("wide"),
        P("wide", None),
        P(),
        P(),
        P(),
        P(),
        P(),
        P(),
        P(),
        P(),
        P(),
        P(),
        P("wide", "narrow", None),
    )
    out_specs = (
        P("wide", "narrow", None),
        P("wide", "narrow", None),
        P(),
        P(),
        P(),
        P(),
        P(),
        P(),
        P(),
        P(),
        P(),
        P(),
    )
    return jax.shard_map(local, mesh=mesh, in_specs=in_specs, out_specs=out_specs, check_vma=False)
```

profile of v0, /device:TPU:1, one launch (start us, length us, event | category | flops | bytes accessed | tf_op | source)
XLA Modules:
  0.0 1060.8 jit_solution(13036474322672682413)
XLA Ops:
  39.6 63.4 %while.85 = (s32[]{:T(128)}, bf16[2,1,256,768]{2,3,1,0:T(8,128)(2,1)}, f32[1,12,256]{2,1,0:T(8,128)}, f32[1,12,256]{2,1,0:T(8,128)}, f32[1,256,12,64]{1,3,2,0:T(...) while((s32[]{:T(128)}, ...), condition=%wide.region_15.16_spmd.clone, body=%wide.region_12.15_spmd.clone.sunk | while | flops 210586640 | bytes 25119744 | solution.py:198
  47.8 14.4 %collective-permute-done.1 = bf16[2,1,256,768]{2,3,1,0:T(8,128)(2,1)} collective-permute-done((bf16[2,1,256,768]{2,3,1,0:T(8,128)(2,1)S(1)}, bf16[2,1,256,768]{2,3,1,0:T(8,128)(2,1)}, u32[]{:S(2)}, u32[]{:S(2)}) %collective-permute-start.1) | collective-permute-done | bytes 786464 | tf_op jit(solution)/shard_map/while/body/eval_jaxpr/ppermute | solution.py:22
  68.3 14.8 %collective-permute-done.1 = bf16[2,1,256,768]{2,3,1,0:T(8,128)(2,1)} collective-permute-done((bf16[2,1,256,768]{2,3,1,0:T(8,128)(2,1)S(1)}, bf16[2,1,256,768]{2,3,1,0:T(8,128)(2,1)}, u32[]{:S(2)}, u32[]{:S(2)}) %collective-permute-start.1) | collective-permute-done | bytes 786464 | tf_op jit(solution)/shard_map/while/body/eval_jaxpr/ppermute | solution.py:22
  89.2 13.9 %collective-permute-done.1 = bf16[2,1,256,768]{2,3,1,0:T(8,128)(2,1)} collective-permute-done((bf16[2,1,256,768]{2,3,1,0:T(8,128)(2,1)S(1)}, bf16[2,1,256,768]{2,3,1,0:T(8,128)(2,1)}, u32[]{:S(2)}, u32[]{:S(2)}) %collective-permute-start.1) | collective-permute-done | bytes 786464 | tf_op jit(solution)/shard_map/while/body/eval_jaxpr/ppermute | solution.py:22
  105.1 54.5 %while.84 = (s32[]{:T(128)}, bf16[2,1,256,768]{2,3,1,0:T(8,128)(2,1)}, f32[1,12,256]{2,1,0:T(8,128)S(1)}, f32[1,12,256]{2,1,0:T(8,128)}, f32[1,256,12,64]{1,3,2,...) while((s32[]{:T(128)}, ...), condition=%wide.region_5.6_spmd.clone, body=%wide.region_2.5_spmd.clone.sunk | while | flops 210586640 | bytes 25070564 | solution.py:198
  110.5 13.6 %collective-permute-done = bf16[2,1,256,768]{2,3,1,0:T(8,128)(2,1)} collective-permute-done((bf16[2,1,256,768]{2,3,1,0:T(8,128)(2,1)S(1)}, bf16[2,1,256,768]{2,3,1,0:T(8,128)(2,1)}, u32[]{:S(2)}, u32[]{:S(2)}) %collective-permute-start) | collective-permute-done | bytes 786464 | tf_op jit(solution)/shard_map/while/body/eval_jaxpr/ppermute | solution.py:22
  129.6 12.7 %collective-permute-done = bf16[2,1,256,768]{2,3,1,0:T(8,128)(2,1)} collective-permute-done((bf16[2,1,256,768]{2,3,1,0:T(8,128)(2,1)S(1)}, bf16[2,1,256,768]{2,3,1,0:T(8,128)(2,1)}, u32[]{:S(2)}, u32[]{:S(2)}) %collective-permute-start) | collective-permute-done | bytes 786464 | tf_op jit(solution)/shard_map/while/body/eval_jaxpr/ppermute | solution.py:22
  147.7 11.7 %collective-permute-done = bf16[2,1,256,768]{2,3,1,0:T(8,128)(2,1)} collective-permute-done((bf16[2,1,256,768]{2,3,1,0:T(8,128)(2,1)S(1)}, bf16[2,1,256,768]{2,3,1,0:T(8,128)(2,1)}, u32[]{:S(2)}, u32[]{:S(2)}) %collective-permute-start) | collective-permute-done | bytes 786464 | tf_op jit(solution)/shard_map/while/body/eval_jaxpr/ppermute | solution.py:22
  197.0 129.1 %while.86 = (s32[]{:T(128)}, bf16[2,1,256,768]{2,3,1,0:T(8,128)(2,1)}, f32[2,1,256,768]{2,3,1,0:T(8,128)}, f32[1,256,12,64]{1,3,2,0:T(8,128)}, s32[]{:T(128)}, /...) while((s32[]{:T(128)}, ...), condition=%wide.region_23.24_spmd.clone, body=%wide.region_22.23_spmd.clone.sunk | while | flops 513934336 | bytes 45259516 | solution.py:309
  211.3 12.8 %collective-permute-done.3 = bf16[2,1,256,768]{2,3,1,0:T(8,128)(2,1)} collective-permute-done((bf16[2,1,256,768]{2,3,1,0:T(8,128)(2,1)}, bf16[2,1,256,768]{2,3,1,0:T(8,128)(2,1)}, u32[]{:S(2)}, u32[]{:S(2)}) %collective-permute-start.3) | collective-permute-done | bytes 786464 | tf_op jit(solution)/shard_map/while/body/eval_jaxpr/ppermute | solution.py:22
  226.5 14.5 %collective-permute-done.2 = bf16[2,1,256,768]{2,3,1,0:T(8,128)(2,1)} collective-permute-done((bf16[2,1,256,768]{2,3,1,0:T(8,128)(2,1)}, bf16[2,1,256,768]{2,3,1,0:T(8,128)(2,1)}, u32[]{:S(2)}, u32[]{:S(2)}) %collective-permute-start.2) | collective-permute-done | bytes 786464 | tf_op jit(solution)/shard_map/while/body/eval_jaxpr/ppermute | solution.py:22
  255.5 11.6 %collective-permute-done.3 = bf16[2,1,256,768]{2,3,1,0:T(8,128)(2,1)} collective-permute-done((bf16[2,1,256,768]{2,3,1,0:T(8,128)(2,1)}, bf16[2,1,256,768]{2,3,1,0:T(8,128)(2,1)}, u32[]{:S(2)}, u32[]{:S(2)}) %collective-permute-start.3) | collective-permute-done | bytes 786464 | tf_op jit(solution)/shard_map/while/body/eval_jaxpr/ppermute | solution.py:22
  269.5 14.5 %collective-permute-done.2 = bf16[2,1,256,768]{2,3,1,0:T(8,128)(2,1)} collective-permute-done((bf16[2,1,256,768]{2,3,1,0:T(8,128)(2,1)}, bf16[2,1,256,768]{2,3,1,0:T(8,128)(2,1)}, u32[]{:S(2)}, u32[]{:S(2)}) %collective-permute-start.2) | collective-permute-done | bytes 786464 | tf_op jit(solution)/shard_map/while/body/eval_jaxpr/ppermute | solution.py:22
  298.6 10.7 %collective-permute-done.3 = bf16[2,1,256,768]{2,3,1,0:T(8,128)(2,1)} collective-permute-done((bf16[2,1,256,768]{2,3,1,0:T(8,128)(2,1)}, bf16[2,1,256,768]{2,3,1,0:T(8,128)(2,1)}, u32[]{:S(2)}, u32[]{:S(2)}) %collective-permute-start.3) | collective-permute-done | bytes 786464 | tf_op jit(solution)/shard_map/while/body/eval_jaxpr/ppermute | solution.py:22
  311.7 14.5 %collective-permute-done.2 = bf16[2,1,256,768]{2,3,1,0:T(8,128)(2,1)} collective-permute-done((bf16[2,1,256,768]{2,3,1,0:T(8,128)(2,1)}, bf16[2,1,256,768]{2,3,1,0:T(8,128)(2,1)}, u32[]{:S(2)}, u32[]{:S(2)}) %collective-permute-start.2) | collective-permute-done | bytes 786464 | tf_op jit(solution)/shard_map/while/body/eval_jaxpr/ppermute | solution.py:22
  340.2 127.0 %while.87 = (s32[]{:T(128)}, bf16[2,1,256,768]{2,3,1,0:T(8,128)(2,1)}, f32[2,1,256,768]{2,3,1,0:T(8,128)}, f32[1,256,12,64]{1,3,2,0:T(8,128)}, s32[]{:T(128)}, /...) while((s32[]{:T(128)}, ...), condition=%wide.region_29.30_spmd.clone, body=%wide.region_28.29_spmd.clone.sunk | while | flops 513934336 | bytes 42212092 | solution.py:309
  351.0 18.2 %collective-permute-done.5 = bf16[2,1,256,768]{2,3,1,0:T(8,128)(2,1)} collective-permute-done((bf16[2,1,256,768]{2,3,1,0:T(8,128)(2,1)}, bf16[2,1,256,768]{2,3,1,0:T(8,128)(2,1)}, u32[]{:S(2)}, u32[]{:S(2)}) %collective-permute-start.5) | collective-permute-done | bytes 786464 | tf_op jit(solution)/shard_map/while/body/eval_jaxpr/ppermute | solution.py:22
  371.6 14.5 %collective-permute-done.4 = bf16[2,1,256,768]{2,3,1,0:T(8,128)(2,1)} collective-permute-done((bf16[2,1,256,768]{2,3,1,0:T(8,128)(2,1)S(1)}, bf16[2,1,256,768]{2,3,1,0:T(8,128)(2,1)}, u32[]{:S(2)}, u32[]{:S(2)}) %collective-permute-start.4) | collective-permute-done | bytes 786464 | tf_op jit(solution)/shard_map/while/body/eval_jaxpr/ppermute | solution.py:22
  397.7 12.5 %collective-permute-done.5 = bf16[2,1,256,768]{2,3,1,0:T(8,128)(2,1)} collective-permute-done((bf16[2,1,256,768]{2,3,1,0:T(8,128)(2,1)}, bf16[2,1,256,768]{2,3,1,0:T(8,128)(2,1)}, u32[]{:S(2)}, u32[]{:S(2)}) %collective-permute-start.5) | collective-permute-done | bytes 786464 | tf_op jit(solution)/shard_map/while/body/eval_jaxpr/ppermute | solution.py:22
  412.7 14.5 %collective-permute-done.4 = bf16[2,1,256,768]{2,3,1,0:T(8,128)(2,1)} collective-permute-done((bf16[2,1,256,768]{2,3,1,0:T(8,128)(2,1)S(1)}, bf16[2,1,256,768]{2,3,1,0:T(8,128)(2,1)}, u32[]{:S(2)}, u32[]{:S(2)}) %collective-permute-start.4) | collective-permute-done | bytes 786464 | tf_op jit(solution)/shard_map/while/body/eval_jaxpr/ppermute | solution.py:22
  438.8 11.6 %collective-permute-done.5 = bf16[2,1,256,768]{2,3,1,0:T(8,128)(2,1)} collective-permute-done((bf16[2,1,256,768]{2,3,1,0:T(8,128)(2,1)}, bf16[2,1,256,768]{2,3,1,0:T(8,128)(2,1)}, u32[]{:S(2)}, u32[]{:S(2)}) %collective-permute-start.5) | collective-permute-done | bytes 786464 | tf_op jit(solution)/shard_map/while/body/eval_jaxpr/ppermute | solution.py:22
  452.8 14.5 %collective-permute-done.4 = bf16[2,1,256,768]{2,3,1,0:T(8,128)(2,1)} collective-permute-done((bf16[2,1,256,768]{2,3,1,0:T(8,128)(2,1)S(1)}, bf16[2,1,256,768]{2,3,1,0:T(8,128)(2,1)}, u32[]{:S(2)}, u32[]{:S(2)}) %collective-permute-start.4) | collective-permute-done | bytes 786464 | tf_op jit(solution)/shard_map/while/body/eval_jaxpr/ppermute | solution.py:22
  565.5 49.3 %all-reduce = (f32[4608]{0:T(1024)}, f32[768]{0:T(1024)}, f32[768]{0:T(1024)}, f32[3072]{0:T(1024)}, f32[768]{0:T(1024)}) all-reduce(f32[4608]{0:T(1024)S(1)} %add.737, f32[768]{0:T(1024)S(1)} %add.738, f32[768]{0:T(1024)} %add.741, f32[3072]{0:T(1024)} %add.743, f32[768]{0:T(1024)} %add.745), channel_id=1, replica_groups=mesh['wide'=8,'narrow'=4] {'wide','narrow'}, use_global_device_ids=true, to_apply=%region_45.46 | all-reduce | flops 9984 | bytes 79872 | tf_op jit(solution)/shard_map/psum | solution.py:359
  619.8 409.4 %all-reduce.4.cloned.1.call-done = (f32[4608,128]{1,0:T(8,128)}, f32[768,2304]{1,0:T(8,128)}, f32[768,768]{1,0:T(8,128)}, f32[768,3072]{1,0:T(8,128)}, f32[3072,768]{1,0:T(8,128)}) async-done(((f32[4608,128]{1,0:T(8,128)}, f32[768,2304]{1,0:T(8,128)}, f32[768,768]{1,0:T(8,128)}, f32[768,3072]{1,0:T(8,128)}, f32[3072,768]{1,0:T(8,128)}), (f32[4608,128]{1,0:T(8,128)}, f32[768,2304]{1,0:T(8,128)}, ...) | async-done | bytes 30670864 | tf_op jit(solution)/shard_map/psum | solution.py:359
  (693 shorter events, 338.9 us)
Async XLA Ops:
  7.2 162.6 %copy-start = (bf16[768,768]{1,0:T(8,128)(2,1)S(1)}, bf16[768,768]{1,0:T(8,128)(2,1)}, u32[]{:S(2)}) copy-start(bf16[768,768]{1,0:T(8,128)(2,1)} %param.31) | copy-start | bytes 3538948
  7.2 1022.0 %all-reduce.4.cloned.1.call-start = ((), (), s32[]{:S(2)}) async-start(), calls=%async_computation | async-start | bytes 61341696 | tf_op jit(solution)/shard_map/psum | solution.py:359
  33.4 71.7 %copy-start.47 = (bf16[1,256,12,32]{1,3,2,0:T(8,128)(2,1)}, bf16[1,256,12,32]{1,3,2,0:T(8,128)(2,1)S(1)}, u32[]{:S(2)}) copy-start(bf16[1,256,12,32]{1,3,2,0:T(8,128)(2,1)S(1)} %get-tuple-element.1423) | copy-start | bytes 589828
  33.4 71.7 %copy-start.49 = (bf16[1,256,12,32]{1,3,2,0:T(8,128)(2,1)}, bf16[1,256,12,32]{1,3,2,0:T(8,128)(2,1)S(1)}, u32[]{:S(2)}) copy-start(bf16[1,256,12,32]{1,3,2,0:T(8,128)(2,1)S(1)} %get-tuple-element.1424) | copy-start | bytes 589828
  40.8 21.5 %collective-permute-start.1 = (bf16[2,1,256,768]{2,3,1,0:T(8,128)(2,1)S(1)}, bf16[2,1,256,768]{2,3,1,0:T(8,128)(2,1)}, u32[]{:S(2)}, u32[]{:S(2)}) collective-permute-start(bf16[2,1,256,768]{2,3,1,0:T(8,128)(2,1)S(1)} %copy.108), channel_id=1, source_target_pairs={{3,0},{0,1},{1,2},{2,3},{7,4},{4,5},{5,6},{6,7},{11,8},{8,9},{9,10... | collective-permute-start | bytes 2359304 | tf_op jit(solution)/shard_map/while/body/eval_jaxpr/ppermute | solution.py:22
  63.4 19.7 %collective-permute-start.1 = (bf16[2,1,256,768]{2,3,1,0:T(8,128)(2,1)S(1)}, bf16[2,1,256,768]{2,3,1,0:T(8,128)(2,1)}, u32[]{:S(2)}, u32[]{:S(2)}) collective-permute-start(bf16[2,1,256,768]{2,3,1,0:T(8,128)(2,1)S(1)} %copy.108), channel_id=1, source_target_pairs={{3,0},{0,1},{1,2},{2,3},{7,4},{4,5},{5,6},{6,7},{11,8},{8,9},{9,10... | collective-permute-start | bytes 2359304 | tf_op jit(solution)/shard_map/while/body/eval_jaxpr/ppermute | solution.py:22
  84.3 18.8 %collective-permute-start.1 = (bf16[2,1,256,768]{2,3,1,0:T(8,128)(2,1)S(1)}, bf16[2,1,256,768]{2,3,1,0:T(8,128)(2,1)}, u32[]{:S(2)}, u32[]{:S(2)}) collective-permute-start(bf16[2,1,256,768]{2,3,1,0:T(8,128)(2,1)S(1)} %copy.108), channel_id=1, source_target_pairs={{3,0},{0,1},{1,2},{2,3},{7,4},{4,5},{5,6},{6,7},{11,8},{8,9},{9,10... | collective-permute-start | bytes 2359304 | tf_op jit(solution)/shard_map/while/body/eval_jaxpr/ppermute | solution.py:22
  106.3 17.9 %collective-permute-start = (bf16[2,1,256,768]{2,3,1,0:T(8,128)(2,1)S(1)}, bf16[2,1,256,768]{2,3,1,0:T(8,128)(2,1)}, u32[]{:S(2)}, u32[]{:S(2)}) collective-permute-start(bf16[2,1,256,768]{2,3,1,0:T(8,128)(2,1)S(1)} %copy.123), channel_id=1, source_target_pairs={{3,0},{0,1},{1,2},{2,3},{7,4},{4,5},{5,6},{6,7},{11,8},{8,9},{9,10... | collective-permute-start | bytes 2359304 | tf_op jit(solution)/shard_map/while/body/eval_jaxpr/ppermute | solution.py:22
  125.3 16.9 %collective-permute-start = (bf16[2,1,256,768]{2,3,1,0:T(8,128)(2,1)S(1)}, bf16[2,1,256,768]{2,3,1,0:T(8,128)(2,1)}, u32[]{:S(2)}, u32[]{:S(2)}) collective-permute-start(bf16[2,1,256,768]{2,3,1,0:T(8,128)(2,1)S(1)} %copy.123), channel_id=1, source_target_pairs={{3,0},{0,1},{1,2},{2,3},{7,4},{4,5},{5,6},{6,7},{11,8},{8,9},{9,10... | collective-permute-start | bytes 2359304 | tf_op jit(solution)/shard_map/while/body/eval_jaxpr/ppermute | solution.py:22
  143.4 16.0 %collective-permute-start = (bf16[2,1,256,768]{2,3,1,0:T(8,128)(2,1)S(1)}, bf16[2,1,256,768]{2,3,1,0:T(8,128)(2,1)}, u32[]{:S(2)}, u32[]{:S(2)}) collective-permute-start(bf16[2,1,256,768]{2,3,1,0:T(8,128)(2,1)S(1)} %copy.123), channel_id=1, source_target_pairs={{3,0},{0,1},{1,2},{2,3},{7,4},{4,5},{5,6},{6,7},{11,8},{8,9},{9,10... | collective-permute-start | bytes 2359304 | tf_op jit(solution)/shard_map/while/body/eval_jaxpr/ppermute | solution.py:22
  208.8 15.3 %collective-permute-start.3 = (bf16[2,1,256,768]{2,3,1,0:T(8,128)(2,1)}, bf16[2,1,256,768]{2,3,1,0:T(8,128)(2,1)}, u32[]{:S(2)}, u32[]{:S(2)}) collective-permute-start(bf16[2,1,256,768]{2,3,1,0:T(8,128)(2,1)} %fusion.436), channel_id=1, source_target_pairs={{3,0},{0,1},{1,2},{2,3},{7,4},{4,5},{5,6},{6,7},{11,8},{8,9},{9,10... | collective-permute-start | bytes 2359304 | tf_op jit(solution)/shard_map/while/body/eval_jaxpr/ppermute | solution.py:22
  208.8 32.2 %collective-permute-start.2 = (bf16[2,1,256,768]{2,3,1,0:T(8,128)(2,1)}, bf16[2,1,256,768]{2,3,1,0:T(8,128)(2,1)}, u32[]{:S(2)}, u32[]{:S(2)}) collective-permute-start(bf16[2,1,256,768]{2,3,1,0:T(8,128)(2,1)} %copy.149), channel_id=1, source_target_pairs={{3,0},{0,1},{1,2},{2,3},{7,4},{4,5},{5,6},{6,7},{11,8},{8,9},{9,10... | collective-permute-start | bytes 2359304 | tf_op jit(solution)/shard_map/while/body/eval_jaxpr/ppermute | solution.py:22
  252.8 14.4 %collective-permute-start.3 = (bf16[2,1,256,768]{2,3,1,0:T(8,128)(2,1)}, bf16[2,1,256,768]{2,3,1,0:T(8,128)(2,1)}, u32[]{:S(2)}, u32[]{:S(2)}) collective-permute-start(bf16[2,1,256,768]{2,3,1,0:T(8,128)(2,1)} %fusion.436), channel_id=1, source_target_pairs={{3,0},{0,1},{1,2},{2,3},{7,4},{4,5},{5,6},{6,7},{11,8},{8,9},{9,10... | collective-permute-start | bytes 2359304 | tf_op jit(solution)/shard_map/while/body/eval_jaxpr/ppermute | solution.py:22
  252.8 31.2 %collective-permute-start.2 = (bf16[2,1,256,768]{2,3,1,0:T(8,128)(2,1)}, bf16[2,1,256,768]{2,3,1,0:T(8,128)(2,1)}, u32[]{:S(2)}, u32[]{:S(2)}) collective-permute-start(bf16[2,1,256,768]{2,3,1,0:T(8,128)(2,1)} %copy.149), channel_id=1, source_target_pairs={{3,0},{0,1},{1,2},{2,3},{7,4},{4,5},{5,6},{6,7},{11,8},{8,9},{9,10... | collective-permute-start | bytes 2359304 | tf_op jit(solution)/shard_map/while/body/eval_jaxpr/ppermute | solution.py:22
  295.8 13.5 %collective-permute-start.3 = (bf16[2,1,256,768]{2,3,1,0:T(8,128)(2,1)}, bf16[2,1,256,768]{2,3,1,0:T(8,128)(2,1)}, u32[]{:S(2)}, u32[]{:S(2)}) collective-permute-start(bf16[2,1,256,768]{2,3,1,0:T(8,128)(2,1)} %fusion.436), channel_id=1, source_target_pairs={{3,0},{0,1},{1,2},{2,3},{7,4},{4,5},{5,6},{6,7},{11,8},{8,9},{9,10... | collective-permute-start | bytes 2359304 | tf_op jit(solution)/shard_map/while/body/eval_jaxpr/ppermute | solution.py:22
  295.8 30.3 %collective-permute-start.2 = (bf16[2,1,256,768]{2,3,1,0:T(8,128)(2,1)}, bf16[2,1,256,768]{2,3,1,0:T(8,128)(2,1)}, u32[]{:S(2)}, u32[]{:S(2)}) collective-permute-start(bf16[2,1,256,768]{2,3,1,0:T(8,128)(2,1)} %copy.149), channel_id=1, source_target_pairs={{3,0},{0,1},{1,2},{2,3},{7,4},{4,5},{5,6},{6,7},{11,8},{8,9},{9,10... | collective-permute-start | bytes 2359304 | tf_op jit(solution)/shard_map/while/body/eval_jaxpr/ppermute | solution.py:22
  335.5 178.8 %collective-permute-start.6 = (bf16[2,1,256,768]{2,3,1,0:T(8,128)(2,1)}, bf16[2,1,256,768]{2,3,1,0:T(8,128)(2,1)}, u32[]{:S(2)}, u32[]{:S(2)}) collective-permute-start(bf16[2,1,256,768]{2,3,1,0:T(8,128)(2,1)} %fusion.114), channel_id=1, source_target_pairs={{3,0},{0,1},{1,2},{2,3},{7,4},{4,5},{5,6},{6,7},{11,8},{8,9},{9,10... | collective-permute-start | bytes 2359304 | tf_op jit(solution)/shard_map/ppermute | solution.py:22
  349.4 19.8 %collective-permute-start.5 = (bf16[2,1,256,768]{2,3,1,0:T(8,128)(2,1)}, bf16[2,1,256,768]{2,3,1,0:T(8,128)(2,1)}, u32[]{:S(2)}, u32[]{:S(2)}) collective-permute-start(bf16[2,1,256,768]{2,3,1,0:T(8,128)(2,1)} %fusion.452), channel_id=1, source_target_pairs={{3,0},{0,1},{1,2},{2,3},{7,4},{4,5},{5,6},{6,7},{11,8},{8,9},{9,10... | collective-permute-start | bytes 2359304 | tf_op jit(solution)/shard_map/while/body/eval_jaxpr/ppermute | solution.py:22
  349.4 36.6 %collective-permute-start.4 = (bf16[2,1,256,768]{2,3,1,0:T(8,128)(2,1)S(1)}, bf16[2,1,256,768]{2,3,1,0:T(8,128)(2,1)}, u32[]{:S(2)}, u32[]{:S(2)}) collective-permute-start(bf16[2,1,256,768]{2,3,1,0:T(8,128)(2,1)S(1)} %copy.137), channel_id=1, source_target_pairs={{3,0},{0,1},{1,2},{2,3},{7,4},{4,5},{5,6},{6,7},{11,8},{8,9},{9,10... | collective-permute-start | bytes 2359304 | tf_op jit(solution)/shard_map/while/body/eval_jaxpr/ppermute | solution.py:22
  395.0 15.2 %collective-permute-start.5 = (bf16[2,1,256,768]{2,3,1,0:T(8,128)(2,1)}, bf16[2,1,256,768]{2,3,1,0:T(8,128)(2,1)}, u32[]{:S(2)}, u32[]{:S(2)}) collective-permute-start(bf16[2,1,256,768]{2,3,1,0:T(8,128)(2,1)} %fusion.452), channel_id=1, source_target_pairs={{3,0},{0,1},{1,2},{2,3},{7,4},{4,5},{5,6},{6,7},{11,8},{8,9},{9,10... | collective-permute-start | bytes 2359304 | tf_op jit(solution)/shard_map/while/body/eval_jaxpr/ppermute | solution.py:22
  395.0 32.1 %collective-permute-start.4 = (bf16[2,1,256,768]{2,3,1,0:T(8,128)(2,1)S(1)}, bf16[2,1,256,768]{2,3,1,0:T(8,128)(2,1)}, u32[]{:S(2)}, u32[]{:S(2)}) collective-permute-start(bf16[2,1,256,768]{2,3,1,0:T(8,128)(2,1)S(1)} %copy.137), channel_id=1, source_target_pairs={{3,0},{0,1},{1,2},{2,3},{7,4},{4,5},{5,6},{6,7},{11,8},{8,9},{9,10... | collective-permute-start | bytes 2359304 | tf_op jit(solution)/shard_map/while/body/eval_jaxpr/ppermute | solution.py:22
  436.1 14.3 %collective-permute-start.5 = (bf16[2,1,256,768]{2,3,1,0:T(8,128)(2,1)}, bf16[2,1,256,768]{2,3,1,0:T(8,128)(2,1)}, u32[]{:S(2)}, u32[]{:S(2)}) collective-permute-start(bf16[2,1,256,768]{2,3,1,0:T(8,128)(2,1)} %fusion.452), channel_id=1, source_target_pairs={{3,0},{0,1},{1,2},{2,3},{7,4},{4,5},{5,6},{6,7},{11,8},{8,9},{9,10... | collective-permute-start | bytes 2359304 | tf_op jit(solution)/shard_map/while/body/eval_jaxpr/ppermute | solution.py:22
  436.1 31.2 %collective-permute-start.4 = (bf16[2,1,256,768]{2,3,1,0:T(8,128)(2,1)S(1)}, bf16[2,1,256,768]{2,3,1,0:T(8,128)(2,1)}, u32[]{:S(2)}, u32[]{:S(2)}) collective-permute-start(bf16[2,1,256,768]{2,3,1,0:T(8,128)(2,1)S(1)} %copy.137), channel_id=1, source_target_pairs={{3,0},{0,1},{1,2},{2,3},{7,4},{4,5},{5,6},{6,7},{11,8},{8,9},{9,10... | collective-permute-start | bytes 2359304 | tf_op jit(solution)/shard_map/while/body/eval_jaxpr/ppermute | solution.py:22
  475.9 39.8 %collective-permute-start.7 = (bf16[2,1,256,768]{2,3,1,0:T(8,128)(2,1)}, bf16[2,1,256,768]{2,3,1,0:T(8,128)(2,1)}, u32[]{:S(2)}, u32[]{:S(2)}) collective-permute-start(bf16[2,1,256,768]{2,3,1,0:T(8,128)(2,1)} %fusion.115), channel_id=1, source_target_pairs={{3,0},{0,1},{1,2},{2,3},{7,4},{4,5},{5,6},{6,7},{11,8},{8,9},{9,10... | collective-permute-start | bytes 2359304 | tf_op jit(solution)/shard_map/ppermute | solution.py:22
  (190 other events, 1026.4 us)
Sparse Core Ops, SparseCore 0:
  558.2 470.9 all-reduce.3
where the time goes:
time: 1070 us; the launch traced here: 1060 us
  waiting for transfers between devices  655 us (61%)
  matrix products  149 us (14%)
  local copies, waits for them, and re-layouts  95.2 us (9%)
  other arithmetic  92.4 us (9%)
  blocking collectives  49.3 us (5%)
  between operations  16.4 us (2%)
    psum x1, waiting for transfers between devices, local(): lax.psum((summed[0], summed[1], summed[2], summed[3], summed[4], summed[5...  409 us
    ppermute x20, waiting for transfers between devices, shifted(): return lax.ppermute(block, axis, route)  245 us
    unnamed x314, local copies, waits for them, and re-layouts  53.2 us
    psum x1, blocking collectives, local(): lax.psum((summed[0], summed[1], summed[2], summed[3], summed[4], summed[5...  49.3 us
  transfers between devices with their start and end apart: 21, of which 19 were waited for; matrix products, arithmetic and copies ran while one was open for 14% of the time, Pallas kernels for 0%

commit v1 on v0

v1 whole, which is shorter than its diff:
```python
import functools
import math

import jax
import jax.numpy as jnp
from jax import lax
from jax.experimental import pallas as pl
from jax.experimental.pallas import tpu as pltpu
from jax.sharding import PartitionSpec as P

HEAD = 64
TEMB = 128
MESH = pl.DeviceIdType.MESH
BF = jnp.bfloat16
F32 = jnp.float32

norm_epsilon = 1e-05
gelu_coeff = 0.7978845608028654
masked_score = -1e30


def time_embed(step_ids):
    halfway = TEMB // 2
    frequency = jnp.exp(jnp.arange(halfway, dtype=F32) * (-math.log(10000.0) / halfway))
    angles = step_ids.astype(F32)[:, None] * frequency[None, :]
    return jnp.concatenate([jnp.cos(angles), jnp.sin(angles)], axis=-1)


def rope_tables(positions):
    halfway = HEAD // 2
    inverse = jnp.exp(jnp.arange(halfway, dtype=F32) * (-2.0 * math.log(10000.0) / HEAD))
    angles = positions[:, None] * inverse[None, :]
    return (jnp.cos(angles), jnp.sin(angles))


def rotate(values, cosine_rows, sine_rows, sign):
    former, latter = jnp.split(values, 2, axis=-1)
    cos_wide = cosine_rows[:, None, :]
    sin_wide = sine_rows[:, None, :] * sign
    return jnp.concatenate(
        [former * cos_wide - latter * sin_wide, latter * cos_wide + former * sin_wide], axis=-1
    )


def layer_norm(values, scaling):
    center = values - jnp.mean(values, axis=-1, keepdims=True)
    spread = jnp.mean(center * center, axis=-1, keepdims=True)
    return center * lax.rsqrt(spread + norm_epsilon) * scaling


def modulate(values, scaling, shift_rows, scale_rows):
    return layer_norm(values, scaling) * (1.0 + scale_rows) + shift_rows


def gelu_tanh(values):
    inner_arg = gelu_coeff * (values + 0.044715 * values * values * values)
    return 0.5 * values * (1.0 + jnp.tanh(inner_arg))


def dot(former, latter, dims):
    return lax.dot_general(former, latter, (dims, ((), ())), preferred_element_type=F32)


def attend_kernel(q_ref, ka_ref, va_ref, kb_ref, vb_ref, ba_ref, bb_ref, o_ref, lse_ref):
    count = q_ref.shape[0]
    copies = count // 128
    lane = lax.broadcasted_iota(jnp.int32, (1, 128), 1)
    q = q_ref[...]
    va_t = va_ref[...].T
    vb_t = vb_ref[...].T
    for h in range(2):
        qm = jnp.where((lane // HEAD) == h, q, jnp.zeros_like(q))
        sa = dot(ka_ref[...], qm, ((1,), (1,))) + jnp.concatenate([ba_ref[...]] * copies, axis=1)
        sb = dot(kb_ref[...], qm, ((1,), (1,))) + jnp.concatenate([bb_ref[...]] * copies, axis=1)
        top = jnp.maximum(jnp.max(sa, axis=0, keepdims=True), jnp.max(sb, axis=0, keepdims=True))
        pa = jnp.exp(sa - top)
        pb = jnp.exp(sb - top)
        total = jnp.sum(pa, axis=0, keepdims=True) + jnp.sum(pb, axis=0, keepdims=True)
        rows = slice(h * HEAD, (h + 1) * HEAD)
        out = dot(va_t[rows], pa.astype(BF), ((1,), (0,))) + dot(
            vb_t[rows], pb.astype(BF), ((1,), (0,))
        )
        o_ref[rows, :] = (out / total).astype(BF)
        lse_ref[0, h : h + 1, :] = top + jnp.log(total)


def attend(q, ka, va, kb, vb, bias_a, bias_b):
    count, width = q.shape
    pairs = width // 128
    col = pl.BlockSpec((count, 128), lambda p: (0, p))
    fixed = pl.BlockSpec((count, 128), lambda p: (0, 0))
    return pl.pallas_call(
        attend_kernel,
        grid=(pairs,),
        in_specs=[col] * 5 + [fixed] * 2,
        out_specs=[
            pl.BlockSpec((128, count), lambda p: (p, 0)),
            pl.BlockSpec((1, 8, count), lambda p: (p, 0, 0)),
        ],
        out_shape=[
            jax.ShapeDtypeStruct((width, count), BF),
            jax.ShapeDtypeStruct((pairs, 8, count), F32),
        ],
        compiler_params=pltpu.CompilerParams(vmem_limit_bytes=48 << 20),
        name="attend",
    )(q, ka, va, kb, vb, bias_a, bias_b)


def attend_back_kernel(
    q_ref, ka_ref, va_ref, kb_ref, vb_ref, ba_ref, bb_ref, o_ref, lse_ref, do_ref,
    dq_ref, dka_ref, dva_ref, dkb_ref, dvb_ref,
):
    count = q_ref.shape[0]
    copies = count // 128
    lane = lax.broadcasted_iota(jnp.int32, (1, 128), 1)
    q = q_ref[...]
    do = do_ref[...]
    do_t = do.astype(F32).T
    prod = o_ref[...].astype(F32) * do_t
    dq_parts = []
    for h in range(2):
        rows = slice(h * HEAD, (h + 1) * HEAD)
        picked = (lane // HEAD) == h
        qm = jnp.where(picked, q, jnp.zeros_like(q))
        dom = jnp.where(picked, do, jnp.zeros_like(do))
        delta = jnp.sum(prod[rows], axis=0, keepdims=True)
        lse = lse_ref[0, h : h + 1, :]
        dq_t = None
        for k_ref, v_ref, b_ref, dk_ref, dv_ref in (
            (ka_ref, va_ref, ba_ref, dka_ref, dva_ref),
            (kb_ref, vb_ref, bb_ref, dkb_ref, dvb_ref),
        ):
            k = k_ref[...]
            s = dot(k, qm, ((1,), (1,))) + jnp.concatenate([b_ref[...]] * copies, axis=1)
            p = jnp.exp(s - lse)
            dv = dot(p.astype(BF), dom, ((1,), (0,)))
            dp = dot(v_ref[...], dom, ((1,), (1,)))
            ds = (p * (dp - delta)).astype(BF)
            dk = dot(ds, qm, ((1,), (0,)))
            part = dot(k.T[rows], ds, ((1,), (0,)))
            dq_t = part if dq_t is None else dq_t + part
            if h == 0:
                dk_ref[...] = dk.astype(dk_ref.dtype)
                dv_ref[...] = dv.astype(dv_ref.dtype)
            else:
                dk_ref[...] = dk_ref[...] + dk.astype(dk_ref.dtype)
                dv_ref[...] = dv_ref[...] + dv.astype(dv_ref.dtype)
        dq_parts.append(dq_t)
    dq_ref[...] = (jnp.concatenate(dq_parts, axis=0) * (HEAD**-0.5)).T


def attend_back(q, ka, va, kb, vb, bias_a, bias_b, o_t, lse, do):
    count, width = q.shape
    pairs = width // 128
    col = pl.BlockSpec((count, 128), lambda p: (0, p))
    fixed = pl.BlockSpec((count, 128), lambda p: (0, 0))
    full = jax.ShapeDtypeStruct((count, width), F32)
    half = jax.ShapeDtypeStruct((count, width), BF)
    return pl.pallas_call(
        attend_back_kernel,
        grid=(pairs,),
        in_specs=[col] * 5
        + [fixed] * 2
        + [
            pl.BlockSpec((128, count), lambda p: (p, 0)),
            pl.BlockSpec((1, 8, count), lambda p: (p, 0, 0)),
            col,
        ],
        out_specs=[col] * 5,
        out_shape=[full, full, full, half, half],
        compiler_params=pltpu.CompilerParams(vmem_limit_bytes=48 << 20),
        name="attend_back",
    )(q, ka, va, kb, vb, bias_a, bias_b, o_t, lse, do)


def reduce_kernel(
    wide_size, ring,
    big_ref, small_ref, out_ref, sout_ref,
    acc, sacc, core_in, score_in, bit_in, sbit_in, ring_in, sring_in,
    copy_sem, send_sem, recv_sem, ring_send, ring_recv, gather_send, gather_recv,
):
    chunks, pieces = big_ref.shape[:2]
    nbits = (wide_size // 2).bit_length() - 1
    wide = lax.axis_index("wide")
    here = lax.axis_index("narrow")
    core = lax.rem(wide, 2)
    core_peer = (wide + 1 - 2 * core, here)
    bits = [lax.rem(wide // (2 << b), 2) for b in range(nbits)]
    bit_peers = [wide + (1 - 2 * bits[b]) * (2 << b) for b in range(nbits)]
    ring_peers = [(wide, lax.rem(here + d, ring)) for d in range(1, ring)]

    barrier = pltpu.get_barrier_semaphore()
    for peer in [core_peer] + [(w, here) for w in bit_peers] + ring_peers:
        pl.semaphore_signal(barrier, inc=1, device_id=peer, device_id_type=MESH)
    pl.semaphore_wait(barrier, 1 + nbits + ring - 1)

    def plan(parity):
        low = 0
        size = pieces
        steps = []
        for i in range(nbits):
            up, down = i, nbits - 1 - i
            bit = bits[up] + parity * (bits[down] - bits[up])
            peer = bit_peers[up] + parity * (bit_peers[down] - bit_peers[up])
            size //= 2
            before = low
            low = low + bit * size
            steps.append((before + (1 - bit) * size, low, size, (peer, here)))
        return steps, low

    def stage(step, chunk, parity, sem, big, out, total, core_slot, bit_slots, ring_slot):
        cols = out.shape[-1] // 2
        mine = pl.ds(pl.multiple_of(core * cols, 128), cols)
        other = pl.ds(pl.multiple_of((1 - core) * cols, 128), cols)
        steps, low = plan(parity)
        final = low + here

        def remote(src, dst, index, peer):
            return pltpu.make_async_remote_copy(
                src_ref=src,
                dst_ref=dst,
                send_sem=send_sem.at[index, sem],
                recv_sem=recv_sem.at[index, sem],
                device_id=peer,
                device_id_type=MESH,
            )

        def core_copy():
            return remote(big.at[:, :, other], core_slot, 0, core_peer)

        def own_copy():
            return pltpu.make_async_copy(big.at[:, :, mine], total, copy_sem.at[sem])

        def bit_copy(i):
            away, _, size, peer = steps[i]
            return remote(total.at[pl.ds(away, size)], bit_slots[i], 1 + i, peer)

        def ring_copy(d):
            target = lax.rem(here + d, ring)
            return pltpu.make_async_remote_copy(
                src_ref=total.at[low + target],
                dst_ref=ring_slot.at[d - 1],
                send_sem=ring_send.at[d - 1, sem],
                recv_sem=ring_recv.at[d - 1, sem],
                device_id=(wide, target),
                device_id_type=MESH,
            )

        def spread_copy(d):
            target = lax.rem(here + d, ring)
            place = out.at[final, :, mine]
            return pltpu.make_async_remote_copy(
                src_ref=place,
                dst_ref=place,
                send_sem=gather_send.at[d - 1, sem],
                recv_sem=gather_recv.at[d - 1, sem],
                device_id=(wide, target),
                device_id_type=MESH,
            )

        def back_copy(i):
            _, keep, size, peer = steps[i]
            place = out.at[pl.ds(keep, size), :, mine]
            return remote(place, place, 1 + nbits + i, peer)

        def core_back():
            place = out.at[:, :, mine]
            return remote(place, place, 1 + 2 * nbits, core_peer)

        def add(start, size, slot):
            @pl.loop(0, size)
            def _(j):
                total[start + j] = (total[start + j].astype(F32) + slot[j].astype(F32)).astype(BF)

        if step == 0:
            core_copy().start()
            own_copy().start()
        elif step == 1:
            own_copy().wait()
            core_copy().wait()
            add(0, pieces, core_slot)
            bit_copy(0).start()
        elif step <= nbits:
            bit_copy(step - 2).wait()
            add(steps[step - 2][1], steps[step - 2][2], bit_slots[step - 2])
            bit_copy(step - 1).start()
        elif step == nbits + 1:
            bit_copy(nbits - 1).wait()
            add(steps[nbits - 1][1], steps[nbits - 1][2], bit_slots[nbits - 1])
            for d in range(1, ring):
                ring_copy(d).start()
        elif step == nbits + 2:
            for d in range(1, ring):
                ring_copy(d).wait()
            value = total[final].astype(F32)
            for d in range(1, ring):
                value = value + ring_slot[d - 1].astype(F32)
            out[final, :, mine] = value.astype(BF)
            for d in range(1, ring):
                spread_copy(d).start()
        elif step == nbits + 3:
            for d in range(1, ring):
                spread_copy(d).wait()
            back_copy(nbits - 1).start()
        elif step <= 2 * nbits + 2:
            i = nbits - 1 - (step - nbits - 3)
            back_copy(i + 1).wait()
            back_copy(i).start()
        elif step == 2 * nbits + 3:
            back_copy(0).wait()
            core_back().start()
        else:
            core_back().wait()

    last = 2 * nbits + 4

    @pl.loop(0, chunks + 1 + last)
    def _(tick):
        for step in range(last, -1, -1):
            chunk = tick - step

            @pl.when((chunk >= 0) & (chunk < chunks))
            def _():
                stage(
                    step, chunk, lax.rem(chunk, 2), chunk,
                    big_ref.at[chunk], out_ref.at[chunk], acc.at[chunk], core_in.at[chunk],
                    [ref.at[chunk] for ref in bit_in], ring_in.at[chunk],
                )

            @pl.when(chunk == chunks)
            def _():
                stage(
                    step, chunks, 0, chunks,
                    small_ref, sout_ref, sacc, score_in, sbit_in, sring_in,
                )


def reduce_all(big, small, wide_size, ring):
    chunks, pieces, rows, cols = big.shape
    srows = small.shape[1]
    half = cols // 2
    nbits = (wide_size // 2).bit_length() - 1
    sizes = [pieces >> (i + 1) for i in range(nbits)]
    any_space = pl.BlockSpec(memory_space=pl.ANY)
    vmem = pl.BlockSpec(memory_space=pltpu.VMEM)
    dma = pltpu.SemaphoreType.DMA
    return pl.pallas_call(
        functools.partial(reduce_kernel, wide_size, ring),
        in_specs=[any_space, any_space],
        out_specs=[vmem, vmem],
        out_shape=[
            jax.ShapeDtypeStruct(big.shape, BF),
            jax.ShapeDtypeStruct(small.shape, BF),
        ],
        scratch_shapes=[
            pltpu.VMEM((chunks, pieces, rows, half), BF),
            pltpu.VMEM((pieces, srows, half), BF),
            pltpu.VMEM((chunks, pieces, rows, half), BF),
            pltpu.VMEM((pieces, srows, half), BF),
            [pltpu.VMEM((chunks, n, rows, half), BF) for n in sizes],
            [pltpu.VMEM((n, srows, half), BF) for n in sizes],
            pltpu.VMEM((chunks, ring - 1, rows, half), BF),
            pltpu.VMEM((ring - 1, srows, half), BF),
            dma((chunks + 1,)),
            dma((2 + 2 * nbits, chunks + 1)),
            dma((2 + 2 * nbits, chunks + 1)),
            dma((ring - 1, chunks + 1)),
            dma((ring - 1, chunks + 1)),
            dma((ring - 1, chunks + 1)),
            dma((ring - 1, chunks + 1)),
        ],
        compiler_params=pltpu.CompilerParams(
            collective_id=0, has_side_effects=True, vmem_limit_bytes=60 << 20
        ),
        name="reduce_all",
    )(big, small)


def local(
    tokens, step_ids, prefix, keep_bits, ada_weight, ada_bias, norm1_gain, qkv_weight, out_weight,
    norm2_gain, up_weight, up_bias, down_weight, down_bias, cotangent,
):
    wide_size = lax.axis_size("wide")
    ring = lax.axis_size("narrow")
    wide = lax.axis_index("wide")
    chip = lax.axis_index("narrow")
    core = wide % 2
    groups, span, width = tokens.shape
    assert ring == 2 * groups and wide_size % 2 == 0
    count = groups * span
    length = ring * span
    hidden_width = up_weight.shape[1]
    head_count = width // HEAD
    both = ("wide", "narrow")

    routes = []
    for step in range(groups):
        route = []
        for outer in range(wide_size // 2):
            for c in range(2):
                for z in range(ring):
                    seq = c * groups + (step + z) % groups
                    source = (2 * outer + c) * ring + z
                    target = (2 * outer + z // groups) * ring + seq
                    route.append((source, target))
        routes.append(route)

    def bring(array):
        got = jnp.stack(
            [
                lax.ppermute(
                    lax.dynamic_index_in_dim(array, (step + chip) % groups, 0, keepdims=False),
                    both,
                    routes[step],
                )
                for step in range(groups)
            ]
        )
        blocks = [
            lax.dynamic_index_in_dim(got, (chip - j) % groups, 0, keepdims=False)
            for j in range(groups)
        ]
        return jnp.concatenate(blocks, axis=0)

    def give_back(rows):
        blocks = rows.reshape(groups, span, width)
        got = jnp.stack(
            [
                lax.ppermute(
                    lax.dynamic_index_in_dim(blocks, (chip - step) % groups, 0, keepdims=False),
                    both,
                    [(b, a) for a, b in routes[step]],
                )
                for step in range(groups)
            ]
        )
        return jnp.stack(
            [
                lax.dynamic_index_in_dim(got, (g - chip) % groups, 0, keepdims=False)
                for g in range(groups)
            ]
        )

    swap = [(w, w + 1 - 2 * (w % 2)) for w in range(wide_size)]

    inputs_low = bring(tokens)
    table = jnp.concatenate([prefix[:, None], step_ids[:, None], keep_bits], axis=1)
    table = jnp.where(chip // groups == core, table, lax.ppermute(table, "wide", swap))
    row = lax.dynamic_index_in_dim(table, chip % groups, 0, keepdims=False)
    inputs_low, cotangent = lax.optimization_barrier((inputs_low, cotangent))
    out_grad = bring(cotangent).astype(F32)

    bits_here = row[2:]
    allowed = (jnp.arange(length, dtype=jnp.int32) < row[0]) | (bits_here == 1)
    bias = jnp.where(allowed, 0.0, masked_score).astype(F32)
    bias_wide = jnp.broadcast_to(bias.reshape(2, count, 1), (2, count, 128))
    bias_a = lax.dynamic_index_in_dim(bias_wide, core, 0, keepdims=False)
    bias_b = lax.dynamic_index_in_dim(bias_wide, 1 - core, 0, keepdims=False)

    condition = jax.nn.silu(time_embed(row[1:2]))
    modulation = (
        jnp.dot(
            condition, ada_weight.astype(F32).T, precision=lax.Precision.HIGHEST,
            preferred_element_type=F32,
        )
        + ada_bias
    )
    shift_one, scale_one, gate_one, shift_two, scale_two, gate_two = jnp.split(
        modulation, 6, axis=-1
    )
    cosine_rows, sine_rows = rope_tables(
        (core * count + jnp.arange(count, dtype=jnp.int32)).astype(F32)
    )

    inputs = inputs_low.astype(F32)
    normed, norm_back = jax.vjp(modulate, inputs, norm1_gain, shift_one, scale_one)
    normed_low = normed.astype(BF)
    projected = dot(normed_low, qkv_weight, ((1,), (0,)))
    shaped = projected.reshape(count, 3, head_count, HEAD)
    queries = (
        (rotate(shaped[:, 0], cosine_rows, sine_rows, 1.0) * HEAD**-0.5)
        .astype(BF)
        .reshape(count, width)
    )
    keys = rotate(shaped[:, 1], cosine_rows, sine_rows, 1.0).astype(BF).reshape(count, width)
    values = shaped[:, 2].astype(BF).reshape(count, width)
    keys_b = lax.ppermute(keys, "wide", swap)
    values_b = lax.ppermute(values, "wide", swap)

    attended_t, lse = attend(queries, keys, values, keys_b, values_b, bias_a, bias_b)
    branch_one = dot(attended_t, out_weight, ((0,), (0,)))
    middle = inputs + gate_one * branch_one
    normed_two, norm_back_two = jax.vjp(modulate, middle, norm2_gain, shift_two, scale_two)
    normed_two_low = normed_two.astype(BF)
    hidden = dot(normed_two_low, up_weight, ((1,), (0,))) + up_bias
    active, gelu_back = jax.vjp(gelu_tanh, hidden)
    active_low = active.astype(BF)
    branch_two = dot(active_low, down_weight, ((1,), (0,))) + down_bias
    outputs = give_back((middle + gate_two * branch_two).astype(BF))

    gate_two_grad = jnp.sum(out_grad * branch_two, axis=0)
    branch_two_grad = (gate_two * out_grad).astype(BF)
    down_grad = dot(active_low, branch_two_grad, ((0,), (0,))).astype(BF)
    down_bias_grad = jnp.sum(branch_two_grad.astype(F32), axis=0)
    (hidden_grad,) = gelu_back(dot(branch_two_grad, down_weight, ((1,), (1,))))
    hidden_low = hidden_grad.astype(BF)
    up_grad = dot(normed_two_low, hidden_low, ((0,), (0,))).astype(BF)
    up_bias_grad = jnp.sum(hidden_low.astype(F32), axis=0)
    middle_part, gain_two_grad, shift_two_grad, scale_two_grad = norm_back_two(
        dot(hidden_low, up_weight, ((1,), (1,)))
    )
    middle_grad = out_grad + middle_part
    gate_one_grad = jnp.sum(middle_grad * branch_one, axis=0)
    branch_one_grad = (gate_one * middle_grad).astype(BF)
    out_weight_grad = dot(attended_t, branch_one_grad, ((1,), (0,))).astype(BF)
    attended_grad = dot(branch_one_grad, out_weight, ((1,), (1,))).astype(BF)

    dq, dk, dv, dk_b, dv_b = attend_back(
        queries, keys, values, keys_b, values_b, bias_a, bias_b, attended_t, lse, attended_grad
    )
    dk = dk + lax.ppermute(dk_b, "wide", swap).astype(F32)
    dv = dv + lax.ppermute(dv_b, "wide", swap).astype(F32)

    def unrotate(values):
        return rotate(
            values.reshape(count, head_count, HEAD), cosine_rows, sine_rows, -1.0
        ).reshape(count, width)

    joined = jnp.concatenate([unrotate(dq), unrotate(dk), dv], axis=-1).astype(BF)
    qkv_grad = dot(normed_low, joined, ((0,), (0,))).astype(BF)
    input_part, gain_one_grad, shift_one_grad, scale_one_grad = norm_back(
        dot(joined, qkv_weight, ((1,), (1,)))
    )
    input_grad = give_back((middle_grad + input_part).astype(BF))

    pieces = wide_size // 2 * ring
    rows = width // pieces
    folds = hidden_width // width

    def tiles(array):
        return jnp.transpose(array.reshape(width, -1, width), (1, 0, 2))

    big = jnp.concatenate(
        [
            down_grad.reshape(folds, width, width),
            tiles(up_grad),
            out_weight_grad[None],
            tiles(qkv_grad),
        ]
    ).reshape(-1, pieces, rows, width)
    mod_grad = jnp.concatenate(
        [
            shift_one_grad[0], scale_one_grad[0], gate_one_grad,
            shift_two_grad[0], scale_two_grad[0], gate_two_grad,
        ]
    )
    total_seqs = wide_size * groups
    mod_size = 6 * width
    seq = (wide // 2) * ring + chip
    mod_rows = jnp.where(jnp.arange(total_seqs)[:, None] == seq, mod_grad[None, :], 0.0)
    small = jnp.concatenate(
        [mod_rows.reshape(-1), gain_one_grad, gain_two_grad, down_bias_grad, up_bias_grad]
    )
    srows = -(-small.shape[0] // (width * pieces * 8)) * 8
    small = jnp.pad(small, (0, srows * width * pieces - small.shape[0]))
    small = small.astype(BF).reshape(pieces, srows, width)

    summed, small_sum = reduce_all(big, small, wide_size, ring)
    summed = summed.reshape(-1, width, width)
    flat = small_sum.reshape(-1)
    at = total_seqs * mod_size
    mod_all = flat[:at].reshape(total_seqs, mod_size).astype(F32)
    rest = flat[at : at + 3 * width + hidden_width].astype(F32)
    steps_all = lax.all_gather(step_ids, "wide", axis=0, tiled=True)
    condition_all = jax.nn.silu(time_embed(steps_all))
    ada_grad = jnp.dot(
        mod_all.T, condition_all, precision=lax.Precision.HIGHEST, preferred_element_type=F32
    )

    def untile(array):
        return jnp.concatenate([array[i] for i in range(array.shape[0])], axis=1).astype(F32)

    return (
        outputs,
        input_grad,
        ada_grad,
        jnp.sum(mod_all, axis=0),
        rest[:width],
        untile(summed[2 * folds + 1 :]),
        summed[2 * folds].astype(F32),
        rest[width : 2 * width],
        untile(summed[folds : 2 * folds]),
        rest[3 * width :],
        summed[:folds].reshape(hidden_width, width).astype(F32),
        rest[2 * width : 3 * width],
    )


def solution(mesh):
    split = P("wide", "narrow", None)
    in_specs = (
        (split, P("wide"), P("wide"), P("wide", None)) + (P(),) * 10 + (split,)
    )
    out_specs = (split, split) + (P(),) * 10
    return jax.shard_map(local, mesh=mesh, in_specs=in_specs, out_specs=out_specs, check_vma=False)
```

time: 1070 us -> 464 us (0.43)
  waiting for transfers between devices: 655 us -> 19.7 us
  Pallas kernels: 0 us -> 214 us
  matrix products: 149 us -> 59.2 us
  blocking collectives: 49.3 us -> 6.69 us
  other arithmetic: 92.4 us -> 59.4 us
  local copies, waits for them, and re-layouts: 95.2 us -> 69.9 us
  starting transfers between devices: 2.2 us -> 23 us
  between operations: 16.4 us -> 3.19 us
    psum x1 -> x0, waiting for transfers between devices: 409 us -> none  [local(): lax.psum((summed[0], summed[1], summed[2], summed[3], summed[4], summed[5...]
    ppermute x20 -> x13, waiting for transfers between devices: 245 us -> 19.7 us  [the longest x4 11.8 us: bring(): lax.ppermute(lax.dynamic_index_in_dim(array, (step + chip) % groups, 0, k...]
    pallas_call x0 -> x3, Pallas kernels: none -> 214 us  [the longest x1 181 us: reduce_all(): pl.pallas_call(functools.partial(reduce_kernel, wide_size, ring), in_spec...]
    dot_general x81 -> x14, matrix products: 149 us -> 59.2 us  [the longest x12 54 us: dot(): lax.dot_general(former, latter, (dims, ((), ())), preferred_element_type=...]
    psum x1 -> x0, blocking collectives: 49.3 us -> none  [local(): lax.psum((summed[0], summed[1], summed[2], summed[3], summed[4], summed[5...]
    unnamed x314 -> x178, local copies, waits for them, and re-layouts: 53.2 us -> 6.64 us
    ppermute x20 -> x13, starting transfers between devices: 2.16 us -> 23 us  [the longest x4 10.8 us: bring(): lax.ppermute(lax.dynamic_index_in_dim(array, (step + chip) % groups, 0, k...]
    while x108 -> x0, local copies, waits for them, and re-layouts: 18.5 us -> none
  transfers between devices with their start and end apart: 21 -> 13, of which waited for: 19 -> 3; matrix products, arithmetic and copies ran while one was open for 14% -> 16% of each run, Pallas kernels for 0% -> 0%
where the time goes in v1:
time: 464 us; the launch traced here: 455 us
  Pallas kernels  214 us (46%)
  local copies, waits for them, and re-layouts  69.9 us (15%)
  other arithmetic  59.4 us (13%)
  matrix products  59.2 us (13%)
  starting transfers between devices  23 us (5%)
  waiting for transfers between devices  19.7 us (4%)
  blocking collectives  6.69 us (1%)
    pallas_call x1, Pallas kernels, reduce_all(): pl.pallas_call(functools.partial(reduce_kernel, wide_size, ring), in_spec...  181 us
    dot_general x12, matrix products, dot(): lax.dot_general(former, latter, (dims, ((), ())), preferred_element_type=...  54 us
    pallas_call x1, Pallas kernels, attend_back(): pl.pallas_call(attend_back_kernel, grid=(pairs,), in_specs=[col] * 5 + [f...  19.7 us
    pallas_call x1, Pallas kernels, attend(): pl.pallas_call(attend_kernel, grid=(pairs,), in_specs=[col] * 5 + [fixed]...  13.9 us
    ppermute x4, waiting for transfers between devices, bring(): lax.ppermute(lax.dynamic_index_in_dim(array, (step + chip) % groups, 0, k...  11.8 us
    concatenate x1, other arithmetic, local(): jnp.concatenate([down_grad.reshape(folds, width, width), tiles(up_grad),...  11.2 us
    ppermute x4, starting transfers between devices, bring(): lax.ppermute(lax.dynamic_index_in_dim(array, (step + chip) % groups, 0, k...  10.8 us
    ppermute x4, starting transfers between devices, give_back(): lax.ppermute(lax.dynamic_index_in_dim(blocks, (chip - step) % groups, 0,...  9.34 us
  transfers between devices with their start and end apart: 13, of which 3 were waited for; matrix products, arithmetic and copies ran while one was open for 16% of the time, Pallas kernels for 0%

profile of v1, /device:TPU:1, one launch (start us, length us, event | category | flops | bytes accessed | tf_op | source)
XLA Modules:
  0.0 455.5 jit_solution(17984838654067043025)
XLA Ops:
  6.0 4.7 %collective-permute-start.1 = (bf16[256,768]{1,0:T(8,128)(2,1)}, bf16[256,768]{1,0:T(8,128)(2,1)}, u32[]{:S(2)}, u32[]{:S(2)}) collective-permute-start(bf16[256,768]{1,0:T(8,128)(2,1)} %get-tuple-element.88), channel_id=1, source_target_pairs={{0,1},{1,0},{2,5},{3,4},{4,3},{5,2},{6,7},{7,6},{8,9},{9,8},{10,13... | collective-permute-start | bytes 1179656 | tf_op jit(solution)/shard_map/ppermute | solution.py:411
  15.1 6.7 %all-reduce.1 = s32[16]{0:T(128)S(1)} all-reduce(s32[16]{0:T(128)S(1)} %dynamic-update-slice), channel_id=1, replica_groups=mesh['wide'=8,'narrow'=4] {'wide'}, use_global_device_ids=true, to_apply=%add.1 | all-reduce | flops 16 | bytes 128
  60.9 4.0 collective-permute-done.8
  64.9 7.9 %collective-permute-done.7 = bf16[256,768]{1,0:T(8,128)(2,1)} collective-permute-done((bf16[256,768]{1,0:T(8,128)(2,1)}, bf16[256,768]{1,0:T(8,128)(2,1)}, u32[]{:S(2)}, u32[]{:S(2)}) %collective-permute-start.7) | collective-permute-done | bytes 393248 | tf_op jit(solution)/shard_map/ppermute | solution.py:411
  76.0 13.9 %attend.1 = (bf16[768,512]{1,0:T(8,128)(2,1)S(1)}, f32[6,8,512]{2,1,0:T(8,128)S(1)}) custom-call(bf16[512,768]{1,0:T(8,128)(2,1)S(1)} %copy-done.4, bf16[512,768]{1,0:T(8,128)(2,1)S(1)} %copy-done.2, bf16[512,768]{1,0:T(8,128)(2,1)S(1)} %copy-done.3, bf16[512,768]{1,0:T(8,128)(2,1)} %collective-permute-done.3.kb_ref, ...), custom_call_target="tpu_custom_call" | custom-call | tf_op jit(solution)/shard_map/attend/pallas_call | solution.py:92
  92.8 5.5 %fusion.69 = f32[512,3072]{1,0:T(8,128)S(1)} fusion(bf16[768,3072]{1,0:T(8,128)(2,1)} %param.25, f32[512,768]{1,0:T(8,128)S(1)} %get-tuple-element.53, f32[768]{0:T(1024)S(1)} %copy-done.63, f32[768]{0:T(1024)S(1)} %copy-done.47, f32[768]{0:T(1024)S(1)} %copy-done.56, f32[512]{0:T(512)S(1)} %fusion.54, f32[512]{0:T(512)S(1)} %broadcast_multiply_fusion.1), kind=kOutput, calls=%fused_computation.187 | convolution fusion | flops 2418278400 | bytes 12596224 | tf_op jit(solution)/shard_map/dot_general | solution.py:61
  98.4 10.3 %fusion.78 = (bf16[3072]{0:T(1024)(128)(2,1)}, bf16[512,3072]{1,0:T(8,128)(2,1)S(1)}) fusion(f32[512,3072]{1,0:T(8,128)S(1)} %fusion.69, f32[3072]{0:T(1024)S(1)} %copy-done.68, bf16[3072,768]{1,0:T(8,128)(2,1)S(1)} %bitcast.129, f32[768]{0:T(1024)S(1)} %copy-done.42, bf16[256,768]{1,0:T(8,128)(2,1)S(1)} %get-tuple-element.79, ...), kind=kOutput, calls=%fused_computation.194 | convolution fusion | flops 2459169792 | bytes 14963712 | tf_op jit(solution)/shard_map/dot_general | solution.py:61
  108.7 3.7 multiply_reduce_fusion
  116.9 4.6 %convolution_convert_fusion.1 = bf16[768,3072]{1,0:T(8,128)(2,1)} fusion(bf16[512,3072]{1,0:T(8,128)(2,1)S(1)} %get-tuple-element.111, f32[512,768]{1,0:T(8,128)S(1)} %get-tuple-element.53, f32[768]{0:T(1024)S(1)} %copy-done.63, f32[768]{0:T(1024)S(1)} %copy-done.47, f32[768]{0:T(1024)S(1)} %copy-done.56, f32[512]{0:T(512)S(1)} %fusion.54, ...), kind=kOutput, calls=%fused_computation.14 | convolution fusion | flops 2420637696 | bytes 9450496 | tf_op jit(solution)/shard_map/dot_general | solution.py:61
  121.6 19.7 %attend_back.1 = (f32[512,768]{1,0:T(8,128)}, f32[512,768]{1,0:T(8,128)}, f32[512,768]{1,0:T(8,128)}, bf16[512,768]{1,0:T(8,128)(2,1)S(1)}, bf16[512,768]{1,0:T(8,128)(2,1)S(1)}) custom-call(bf16[512,768]{1,0:T(8,128)(2,1)S(1)} %copy-done.4, bf16[512,768]{1,0:T(8,128)(2,1)S(1)} %copy-done.2, bf16[512,768]{1,0:T(8,128)(2,1)S(1)} %copy-done.3, ...), custom_call_target="tpu_custom_call" | custom-call | tf_op jit(solution)/shard_map/attend_back/pallas_call | solution.py:159
  146.6 4.9 %copy.55 = bf16[96,4,8,768]{3,2,0,1:T(8,128)(2,1)} copy(bf16[96,4,8,768]{3,2,1,0:T(8,128)(2,1)} %bitcast.109) | data formatting | bytes 9437184 | tf_op jit(solution)/shard_map/reshape | solution.py:541
  151.5 9.2 %convolution_convert_fusion.2 = bf16[3072,768]{1,0:T(8,128)(2,1)} fusion(f32[768]{0:T(1024)S(1)} %copy-done.43, bf16[256,768]{1,0:T(8,128)(2,1)S(1)} %copy-done.24, bf16[256,768]{1,0:T(8,128)(2,1)S(1)} %copy-done.21, f32[512,3072]{1,0:T(8,128)} %copy-done.74, f32[3072]{0:T(1024)S(1)} %copy-done.69), kind=kOutput, calls=%fused_computation.15 | convolution fusion | flops 2436366336 | bytes 11811840 | tf_op jit(solution)/shard_map/dot_general | solution.py:61
  180.7 4.0 convolution_convert_fusion
  186.4 6.5 %fusion.23 = (f32[768]{0:T(1024)S(1)}, f32[768]{0:T(1024)S(1)}, bf16[512,768]{1,0:T(8,128)(2,1)}, bf16[512,768]{1,0:T(8,128)(2,1)}) fusion(f32[768]{0:T(1024)S(1)} %copy-done.71, bf16[256,768]{1,0:T(8,128)(2,1)S(1)} %copy-done.25, bf16[256,768]{1,0:T(8,128)(2,1)S(1)} %copy-done.22, f32[512,768]{1,0:T(8,128)S(1)} %copy-done.26, ...), kind=kOutput, calls=%fused_computation.44 | convolution fusion | flops 2441476608 | bytes 20488192 | tf_op jit(solution)/shard_map/dot_general | solution.py:61
  195.1 5.7 %copy.50 = bf16[768,2304]{0,1:T(8,128)(2,1)} copy(bf16[768,2304]{1,0:T(8,128)(2,1)} %convolution_convert_fusion) | data formatting | bytes 7077888 | tf_op jit(solution)/shard_map/convert_element_type | solution.py:530
  200.8 4.3 copy.51
  205.1 11.2 %pad_maximum_fusion.big_ref = bf16[12,16,48,768]{3,2,1,0:T(8,128)(2,1)} fusion(bf16[3,16,48,768]{3,2,1,0:T(8,128)(2,1)S(1)} %bitcast.97, bf16[1,16,48,768]{3,2,1,0:T(8,128)(2,1)} %bitcast.117, bf16[4,16,48,768]{3,2,1,0:T(8,128)(2,1)} %bitcast.96, bf16[4,16,48,768]{3,2,1,0:T(8,128)(2,1)} %bitcast.105), kind=kLoop, calls=%fused_computation | loop fusion | flops 21233664 | bytes 28311552 | tf_op jit(solution)/shard_map/concatenate | solution.py:543
  216.3 180.8 %reduce_all.1 = (bf16[12,16,48,768]{3,2,1,0:T(8,128)(2,1)}, bf16[16,8,768]{2,1,0:T(8,128)(2,1)}) custom-call(bf16[12,16,48,768]{3,2,1,0:T(8,128)(2,1)} %pad_maximum_fusion.big_ref, bf16[16,8,768]{2,1,0:T(8,128)(2,1)} %reshape.354.small_ref), custom_call_target="tpu_custom_call" | custom-call | tf_op jit(solution)/shard_map/reduce_all/pallas_call | solution.py:347
  401.0 4.8 %slice.107 = bf16[4,16,48,768]{3,2,1,0:T(8,128)(2,1)} slice(bf16[12,16,48,768]{3,2,1,0:T(8,128)(2,1)} %get-tuple-element.33), slice={[0:4], [0:16], [0:48], [0:768]} | slice | bytes 9437184 | tf_op jit(solution)/shard_map/slice | solution.py:594
  405.8 6.4 %fusion.75 = (bf16[1,16,48,768]{3,2,1,0:T(8,128)(2,1)S(1)}, bf16[1,16,48,768]{3,2,1,0:T(8,128)(2,1)S(1)}, bf16[1,16,48,768]{3,2,1,0:T(8,128)(2,1)S(1)}, bf16[1,1...) fusion(bf16[12,16,48,768]{3,2,1,0:T(8,128)(2,1)} %get-tuple-ele, ...), kind=kLoop, calls=%fused_computation.191 | loop fusion | bytes 18874368 | tf_op jit(solution)/shard_map/slice | solution.py:581
  420.9 3.8 collective-permute-start.5
  424.7 6.9 %bitcast_convert_fusion = f32[3072,768]{1,0:T(8,128)} fusion(bf16[4,16,48,768]{3,2,1,0:T(8,128)(2,1)} %slice.107), kind=kLoop, calls=%fused_computation.18 | loop fusion | flops 2359296 | bytes 14155776 | tf_op jit(solution)/shard_map/convert_element_type | solution.py:594
  437.6 4.3 maximum_convert_fusion
  444.3 7.9 %collective-permute-done.5 = bf16[256,768]{1,0:T(8,128)(2,1)S(1)} collective-permute-done((bf16[256,768]{1,0:T(8,128)(2,1)S(1)}, bf16[256,768]{1,0:T(8,128)(2,1)S(1)}, u32[]{:S(2)}, u32[]{:S(2)}) %collective-permute-start.5) | collective-permute-done | bytes 393248 | tf_op jit(solution)/shard_map/ppermute | solution.py:429
  (290 shorter events, 110.7 us)
Async XLA Ops:
  0.6 35.7 %copy-start = (bf16[768,2304]{1,0:T(8,128)(2,1)S(1)}, bf16[768,2304]{1,0:T(8,128)(2,1)}, u32[]{:S(2)}) copy-start(bf16[768,2304]{1,0:T(8,128)(2,1)} %param.22) | copy-start | bytes 10616836
  3.9 21.5 %collective-permute-start.2 = (s32[2,1026]{1,0:T(2,128)}, s32[2,1026]{1,0:T(2,128)}, u32[]{:S(2)}, u32[]{:S(2)}) collective-permute-start(s32[2,1026]{1,0:T(2,128)} %concatenate.66), channel_id=1, source_target_pairs={{0,4},{4,0},{8,12},{12,8},{16,20},{20,16},{24,28},{28,24},{1,5},{5... | collective-permute-start | bytes 24632 | tf_op jit(solution)/shard_map/ppermute | solution.py:448
  6.0 27.7 %collective-permute-start.1 = (bf16[256,768]{1,0:T(8,128)(2,1)}, bf16[256,768]{1,0:T(8,128)(2,1)}, u32[]{:S(2)}, u32[]{:S(2)}) collective-permute-start(bf16[256,768]{1,0:T(8,128)(2,1)} %get-tuple-element.88), channel_id=1, source_target_pairs={{0,1},{1,0},{2,5},{3,4},{4,3},{5,2},{6,7},{7,6},{8,9},{9,8},{10,13... | collective-permute-start | bytes 1179656 | tf_op jit(solution)/shard_map/ppermute | solution.py:411
  10.7 23.0 %collective-permute-start = (bf16[256,768]{1,0:T(8,128)(2,1)}, bf16[256,768]{1,0:T(8,128)(2,1)}, u32[]{:S(2)}, u32[]{:S(2)}) collective-permute-start(bf16[256,768]{1,0:T(8,128)(2,1)} %get-tuple-element.89), channel_id=1, source_target_pairs={{0,0},{1,1},{2,4},{3,5},{4,2},{5,3},{6,6},{7,7},{8,8},{9,9},{10,12... | collective-permute-start | bytes 1179656 | tf_op jit(solution)/shard_map/ppermute | solution.py:411
  47.6 28.0 %collective-permute-start.4 = (bf16[512,768]{1,0:T(8,128)(2,1)}, bf16[512,768]{1,0:T(8,128)(2,1)}, u32[]{:S(2)}, u32[]{:S(2)}) collective-permute-start(bf16[512,768]{1,0:T(8,128)(2,1)} %copy.41.va_ref), channel_id=1, source_target_pairs={{0,4},{4,0},{8,12},{12,8},{16,20},{20,16},{24,28},{28,24},{1,5},{5... | collective-permute-start | bytes 2359304 | tf_op jit(solution)/shard_map/ppermute | solution.py:488
  49.9 25.8 %collective-permute-start.3 = (bf16[512,768]{1,0:T(8,128)(2,1)}, bf16[512,768]{1,0:T(8,128)(2,1)}, u32[]{:S(2)}, u32[]{:S(2)}) collective-permute-start(bf16[512,768]{1,0:T(8,128)(2,1)} %copy.40.ka_ref), channel_id=1, source_target_pairs={{0,4},{4,0},{8,12},{12,8},{16,20},{20,16},{24,28},{28,24},{1,5},{5... | collective-permute-start | bytes 2359304 | tf_op jit(solution)/shard_map/ppermute | solution.py:487
  52.0 12.9 %collective-permute-start.8 = (bf16[256,768]{1,0:T(8,128)(2,1)}, bf16[256,768]{1,0:T(8,128)(2,1)}, u32[]{:S(2)}, u32[]{:S(2)}) collective-permute-start(bf16[256,768]{1,0:T(8,128)(2,1)} %get-tuple-element.80), channel_id=1, source_target_pairs={{0,1},{1,0},{2,5},{3,4},{4,3},{5,2},{6,7},{7,6},{8,9},{9,8},{10,13... | collective-permute-start | bytes 1179656 | tf_op jit(solution)/shard_map/ppermute | solution.py:411
  54.2 18.5 %collective-permute-start.7 = (bf16[256,768]{1,0:T(8,128)(2,1)}, bf16[256,768]{1,0:T(8,128)(2,1)}, u32[]{:S(2)}, u32[]{:S(2)}) collective-permute-start(bf16[256,768]{1,0:T(8,128)(2,1)} %get-tuple-element.81), channel_id=1, source_target_pairs={{0,0},{1,1},{2,4},{3,5},{4,2},{5,3},{6,6},{7,7},{8,8},{9,9},{10,12... | collective-permute-start | bytes 1179656 | tf_op jit(solution)/shard_map/ppermute | solution.py:411
  60.9 14.8 %copy-start.51 = (f32[1,512,1]{1,0,2:T(1,128)S(1)}, f32[1,512,1]{1,0,2:T(1,128)}, u32[]{:S(2)}) copy-start(f32[1,512,1]{1,0,2:T(1,128)} %get-tuple-element.100) | copy-start | bytes 6148
  60.9 14.9 %copy-start.50 = (f32[1,512,1]{1,0,2:T(1,128)S(1)}, f32[1,512,1]{1,0,2:T(1,128)}, u32[]{:S(2)}) copy-start(f32[1,512,1]{1,0,2:T(1,128)} %get-tuple-element.99) | copy-start | bytes 6148
  60.9 15.0 %copy-start.2 = (bf16[512,768]{1,0:T(8,128)(2,1)S(1)}, bf16[512,768]{1,0:T(8,128)(2,1)}, u32[]{:S(2)}) copy-start(bf16[512,768]{1,0:T(8,128)(2,1)} %copy.40.ka_ref) | copy-start | bytes 2359300
  60.9 15.0 %copy-start.3 = (bf16[512,768]{1,0:T(8,128)(2,1)S(1)}, bf16[512,768]{1,0:T(8,128)(2,1)}, u32[]{:S(2)}) copy-start(bf16[512,768]{1,0:T(8,128)(2,1)} %copy.41.va_ref) | copy-start | bytes 2359300
  60.9 15.0 %copy-start.4 = (bf16[512,768]{1,0:T(8,128)(2,1)S(1)}, bf16[512,768]{1,0:T(8,128)(2,1)}, u32[]{:S(2)}) copy-start(bf16[512,768]{1,0:T(8,128)(2,1)} %copy.39.q_ref) | copy-start | bytes 2359300
  74.2 40.8 %copy-start.20 = (bf16[256,768]{1,0:T(8,128)(2,1)}, bf16[256,768]{1,0:T(8,128)(2,1)S(1)}, u32[]{:S(2)}) copy-start(bf16[256,768]{1,0:T(8,128)(2,1)S(1)} %get-tuple-element.78) | copy-start | bytes 1179652
  74.2 40.8 %copy-start.23 = (bf16[256,768]{1,0:T(8,128)(2,1)}, bf16[256,768]{1,0:T(8,128)(2,1)S(1)}, u32[]{:S(2)}) copy-start(bf16[256,768]{1,0:T(8,128)(2,1)S(1)} %get-tuple-element.79) | copy-start | bytes 1179652
  89.9 25.0 %copy-start.5 = (bf16[768,512]{1,0:T(8,128)(2,1)}, bf16[768,512]{1,0:T(8,128)(2,1)S(1)}, u32[]{:S(2)}) copy-start(bf16[768,512]{1,0:T(8,128)(2,1)S(1)} %get-tuple-element.24.o_ref) | copy-start | bytes 2359300
  92.0 25.0 %copy-start.11 = (f32[512,768]{1,0:T(8,128)}, f32[512,768]{1,0:T(8,128)S(1)}, u32[]{:S(2)}) copy-start(f32[512,768]{1,0:T(8,128)S(1)} %get-tuple-element.53) | copy-start | bytes 4718596
  92.8 15.9 %slice-start = ((s8[4718592]{0:T(1024)(128)(4,1)}), s8[4194304]{0:T(1024)(128)(4,1)S(1)}, s32[]{:S(2)}) async-start(s8[4718592]{0:T(1024)(128)(4,1)} %bitcast.126), calls=%async_computation | async-start | bytes 8388608
  146.1 14.6 %collective-permute-start.9 = (bf16[512,768]{1,0:T(8,128)(2,1)}, bf16[512,768]{1,0:T(8,128)(2,1)S(1)}, u32[]{:S(2)}, u32[]{:S(2)}) collective-permute-start(bf16[512,768]{1,0:T(8,128)(2,1)} %copy-done.7), channel_id=1, source_target_pairs={{0,4},{4,0},{8,12},{12,8},{16,20},{20,16},{24,28},{28,24},{1,5},{5... | collective-permute-start | bytes 2359304 | tf_op jit(solution)/shard_map/ppermute | solution.py:521
  146.1 30.0 %collective-permute-start.10 = (bf16[512,768]{1,0:T(8,128)(2,1)}, bf16[512,768]{1,0:T(8,128)(2,1)}, u32[]{:S(2)}, u32[]{:S(2)}) collective-permute-start(bf16[512,768]{1,0:T(8,128)(2,1)} %copy-done.6), channel_id=1, source_target_pairs={{0,4},{4,0},{8,12},{12,8},{16,20},{20,16},{24,28},{28,24},{1,5},{5... | collective-permute-start | bytes 2359304 | tf_op jit(solution)/shard_map/ppermute | solution.py:522
  415.3 28.9 %collective-permute-start.12 = (bf16[256,768]{1,0:T(8,128)(2,1)S(1)}, bf16[256,768]{1,0:T(8,128)(2,1)S(1)}, u32[]{:S(2)}, u32[]{:S(2)}) collective-permute-start(bf16[256,768]{1,0:T(8,128)(2,1)S(1)} %get-tuple-element.76), channel_id=1, source_target_pairs={{1,0},{0,1},{5,2},{4,3},{3,4},{2,5},{7,6},{6,7},{9,8},{8,9},{13,10... | collective-permute-start | bytes 1179656 | tf_op jit(solution)/shard_map/ppermute | solution.py:429
  416.5 27.7 %collective-permute-start.11 = (bf16[256,768]{1,0:T(8,128)(2,1)S(1)}, bf16[256,768]{1,0:T(8,128)(2,1)S(1)}, u32[]{:S(2)}, u32[]{:S(2)}) collective-permute-start(bf16[256,768]{1,0:T(8,128)(2,1)S(1)} %get-tuple-element.77), channel_id=1, source_target_pairs={{0,0},{1,1},{4,2},{5,3},{2,4},{3,5},{6,6},{7,7},{8,8},{9,9},{12,10... | collective-permute-start | bytes 1179656 | tf_op jit(solution)/shard_map/ppermute | solution.py:429
  419.1 25.2 %collective-permute-start.6 = (bf16[256,768]{1,0:T(8,128)(2,1)S(1)}, bf16[256,768]{1,0:T(8,128)(2,1)S(1)}, u32[]{:S(2)}, u32[]{:S(2)}) collective-permute-start(bf16[256,768]{1,0:T(8,128)(2,1)S(1)} %get-tuple-element.84), channel_id=1, source_target_pairs={{1,0},{0,1},{5,2},{4,3},{3,4},{2,5},{7,6},{6,7},{9,8},{8,9},{13,10... | collective-permute-start | bytes 1179656 | tf_op jit(solution)/shard_map/ppermute | solution.py:429
  420.9 31.2 %collective-permute-start.5 = (bf16[256,768]{1,0:T(8,128)(2,1)S(1)}, bf16[256,768]{1,0:T(8,128)(2,1)S(1)}, u32[]{:S(2)}, u32[]{:S(2)}) collective-permute-start(bf16[256,768]{1,0:T(8,128)(2,1)S(1)} %get-tuple-element.85), channel_id=1, source_target_pairs={{0,0},{1,1},{4,2},{5,3},{2,4},{3,5},{6,6},{7,7},{8,8},{9,9},{12,10... | collective-permute-start | bytes 1179656 | tf_op jit(solution)/shard_map/ppermute | solution.py:429
  (72 other events, 354.9 us)

commit v2 on v1

v2 whole, which is shorter than its diff:
```python
import functools
import math

import jax
import jax.numpy as jnp
import numpy as np
from jax import lax
from jax.experimental import pallas as pl
from jax.experimental.pallas import tpu as pltpu
from jax.sharding import PartitionSpec as P

HEAD = 64
TEMB = 128
MESH = pl.DeviceIdType.MESH
BF = jnp.bfloat16
F32 = jnp.float32
DMA = pltpu.SemaphoreType.DMA

norm_epsilon = 1e-05
gelu_coeff = 0.7978845608028654
masked_score = -1e30


def time_embed(step_ids):
    halfway = TEMB // 2
    frequency = jnp.exp(jnp.arange(halfway, dtype=F32) * (-math.log(10000.0) / halfway))
    angles = step_ids.astype(F32)[:, None] * frequency[None, :]
    return jnp.concatenate([jnp.cos(angles), jnp.sin(angles)], axis=-1)


def rope_tables(length):
    halfway = HEAD // 2
    inverse = 10000.0 ** (-2.0 * np.arange(halfway) / HEAD)
    angles = np.arange(length)[:, None] * inverse[None, :]
    sines = np.sin(angles)
    return (
        np.tile(np.cos(angles), (1, 4)).astype(np.float32),
        np.concatenate([-sines, sines, -sines, sines], axis=1).astype(np.float32),
    )


def dot(former, latter, dims):
    return lax.dot_general(former, latter, (dims, ((), ())), preferred_element_type=F32)


def rotate(values, cosines, sines, sign):
    lane = lax.broadcasted_iota(jnp.int32, (1, 128), 1)
    first = (lane % HEAD) < HEAD // 2
    parts = []
    for n in range(values.shape[1] // 128):
        part = values[:, n * 128 : (n + 1) * 128]
        partner = jnp.where(first, pltpu.roll(part, 128 - HEAD // 2, 1), pltpu.roll(part, HEAD // 2, 1))
        turned = partner * sines
        parts.append(part * cosines + (turned if sign > 0 else -turned))
    return parts[0] if len(parts) == 1 else jnp.concatenate(parts, axis=1)


def normed_rows(values):
    center = values - jnp.mean(values, axis=-1, keepdims=True)
    spread = jnp.mean(center * center, axis=-1, keepdims=True)
    scale = lax.rsqrt(spread + norm_epsilon)
    return center * scale, scale


def part_of(mod_ref, index, width):
    return mod_ref[:, index * width : (index + 1) * width]


def wide_of(block, copies):
    return jnp.concatenate([block] * copies, axis=1)
LAG = 2


def front_kernel(
    groups, ring,
    tok_ref, cot_ref, wqkv_ref, ada_ref, info_ref, ada_bias_ref, gain_ref, cos_ref, sin_ref,
    x_ref, dy_ref, h_ref, q_ref, ka_ref, va_ref, kb_ref, vb_ref, o_ref, ot_ref, lse_ref,
    mod_ref, ba_ref, bb_ref, misc_ref,
    wqkv, ada, table,
    load_sem, self_sem, info_send, info_recv, send_sem, recv_sem, kv_send, kv_recv,
):
    span, width = tok_ref.shape[1:]
    count = groups * span
    wide = lax.axis_index("wide")
    chip = lax.axis_index("narrow")
    core = lax.rem(wide, 2)
    base = wide - core
    peer = (base + 1 - core, chip)

    load_w = pltpu.make_async_copy(wqkv_ref, wqkv, load_sem.at[0])
    load_a = pltpu.make_async_copy(ada_ref, ada, load_sem.at[1])
    load_a.start()
    load_w.start()

    barrier = pltpu.get_barrier_semaphore()
    for c in range(2):
        for d in range(ring):
            if c or d:
                other = (base + lax.rem(core + c, 2), lax.rem(chip + d, ring))
                pl.semaphore_signal(barrier, inc=1, device_id=other, device_id_type=MESH)
    pl.semaphore_wait(barrier, 2 * ring - 1)

    slot = lax.rem(chip, groups)
    to_core = chip // groups
    rows_out = pl.ds(pl.multiple_of(slot * span, span), span)

    def move(src, dst, kind, g):
        remote = pltpu.make_async_remote_copy(
            src_ref=src.at[g],
            dst_ref=dst.at[rows_out],
            send_sem=send_sem.at[kind, g],
            recv_sem=recv_sem.at[kind, slot],
            device_id=(base + to_core, core * groups + g),
            device_id_type=MESH,
        )
        here = pltpu.make_async_copy(src.at[g], dst.at[rows_out], self_sem.at[kind])
        own = (to_core == core) & (slot == g)
        return remote, here, own

    def send(src, dst, kind):
        for g in range(groups):
            remote, here, own = move(src, dst, kind, g)

            @pl.when(own)
            def _():
                here.start()

            @pl.when(jnp.logical_not(own))
            def _():
                remote.start()

    def sent(src, dst, kind):
        for g in range(groups):
            remote, here, own = move(src, dst, kind, g)

            @pl.when(jnp.logical_not(own))
            def _():
                remote.wait_send()

    def arrive(src, dst, kind, j):
        rows = pl.ds(j * span, span)
        own = (to_core == core) & (slot == j)

        @pl.when(own)
        def _():
            pltpu.make_async_copy(src.at[0], dst.at[rows], self_sem.at[kind]).wait()

        @pl.when(jnp.logical_not(own))
        def _():
            pltpu.make_async_remote_copy(
                src_ref=src.at[0],
                dst_ref=dst.at[rows],
                send_sem=send_sem.at[kind, 0],
                recv_sem=recv_sem.at[kind, j],
                device_id=peer,
                device_id_type=MESH,
            ).wait_recv()

    send(tok_ref, x_ref, 0)
    table[core] = info_ref[...]
    swap_info = pltpu.make_async_remote_copy(
        src_ref=info_ref,
        dst_ref=table.at[core],
        send_sem=info_send,
        recv_sem=info_recv,
        device_id=peer,
        device_id_type=MESH,
    )
    swap_info.start()
    swap_info.wait()
    row = table[chip // groups, lax.rem(chip, groups)]
    length = row.shape[1] - 2 * TEMB
    misc_ref[...] = row[:, TEMB + length :]
    bias = jnp.where(core == 0, row[:, TEMB : TEMB + count], row[:, TEMB + count : TEMB + length])
    ba_ref[...] = jnp.broadcast_to(bias, (128, count)).T
    bias = jnp.where(core == 1, row[:, TEMB : TEMB + count], row[:, TEMB + count : TEMB + length])
    bb_ref[...] = jnp.broadcast_to(bias, (128, count)).T

    cond = jnp.broadcast_to(row[:, :TEMB], (16, TEMB))
    high = cond.astype(BF).astype(F32)
    middle = (cond - high).astype(BF).astype(F32)
    low = cond - high - middle
    line = lax.broadcasted_iota(jnp.int32, (16, TEMB), 0)
    three = jnp.where(
        line == 0, high, jnp.where(line == 1, middle, jnp.where(line == 2, low, 0.0))
    ).astype(BF)
    load_a.wait()
    for i in range(6):
        cols = slice(i * width, (i + 1) * width)
        mod_ref[:, cols] = (
            jnp.sum(dot(three, ada[cols, :], ((1,), (1,))), axis=0, keepdims=True)
            + ada_bias_ref[:, cols]
        )
    shift = part_of(mod_ref, 0, width)
    scale = gain_ref[...] * (1.0 + part_of(mod_ref, 1, width))

    load_w.wait()
    swaps = []
    for j in range(groups):
        rows = pl.ds(j * span, span)
        arrive(tok_ref, x_ref, 0, j)
        if j == groups - 1:
            send(cot_ref, dy_ref, 1)
        normed, _ = normed_rows(x_ref[rows, :].astype(F32))
        h_ref[rows, :] = (normed * scale + shift).astype(BF)
        place = pl.ds(pl.multiple_of(core * count + j * span, span), span)
        cosines = cos_ref[place, :]
        sines = sin_ref[place, :]
        step = 256
        for n in (2, 1, 0):
            target = (q_ref, ka_ref, va_ref)[n]
            for m in range(width // step):
                cols = pl.ds(n * width + m * step, step)
                block = dot(h_ref[rows, :], wqkv[:, cols], ((1,), (0,)))
                if n < 2:
                    block = rotate(block, cosines, sines, 1)
                if n == 0:
                    block = block * HEAD**-0.5
                target[rows, m * step : (m + 1) * step] = block.astype(BF)
            if n > 0:
                swap = pltpu.make_async_remote_copy(
                    src_ref=target.at[rows],
                    dst_ref=(kb_ref, vb_ref)[n - 1].at[rows],
                    send_sem=kv_send.at[n - 1, j],
                    recv_sem=kv_recv.at[n - 1, j],
                    device_id=peer,
                    device_id_type=MESH,
                )
                swap.start()
                swaps.append(swap)
    for swap in swaps:
        swap.wait()

    copies = count // 128
    lane = lax.broadcasted_iota(jnp.int32, (1, 128), 1)

    @pl.loop(0, width // 128)
    def _(p):
        cols = pl.ds(pl.multiple_of(p * 128, 128), 128)
        q = q_ref[:, cols]
        ka = ka_ref[:, cols]
        kb = kb_ref[:, cols]
        va_t = va_ref[:, cols].T
        vb_t = vb_ref[:, cols].T
        outs = []
        for h in range(2):
            qm = jnp.where((lane // HEAD) == h, q, jnp.zeros_like(q))
            sa = dot(ka, qm, ((1,), (1,))) + wide_of(ba_ref[...], copies)
            sb = dot(kb, qm, ((1,), (1,))) + wide_of(bb_ref[...], copies)
            top = jnp.maximum(jnp.max(sa, axis=0, keepdims=True), jnp.max(sb, axis=0, keepdims=True))
            pa = jnp.exp(sa - top)
            pb = jnp.exp(sb - top)
            total = jnp.sum(pa, axis=0, keepdims=True) + jnp.sum(pb, axis=0, keepdims=True)
            part = slice(h * HEAD, (h + 1) * HEAD)
            out = dot(va_t[part], pa.astype(BF), ((1,), (0,))) + dot(
                vb_t[part], pb.astype(BF), ((1,), (0,))
            )
            outs.append(out / total)
            lse_ref[p, h : h + 1, :] = top + jnp.log(total)
        both = jnp.concatenate(outs, axis=0)
        ot_ref[cols, :] = both.astype(BF)
        o_ref[:, cols] = both.T.astype(BF)

    sent(tok_ref, x_ref, 0)
    for j in range(groups):
        arrive(cot_ref, dy_ref, 1, j)
    sent(cot_ref, dy_ref, 1)


def front(tokens, cotangent, wqkv, ada, info, ada_bias, gain, cosines, sines, ring):
    groups, span, width = tokens.shape
    count = groups * span
    any_space = pl.BlockSpec(memory_space=pl.ANY)
    vmem = pl.BlockSpec(memory_space=pltpu.VMEM)
    rows = jax.ShapeDtypeStruct((count, width), BF)
    return pl.pallas_call(
        functools.partial(front_kernel, groups, ring),
        in_specs=[any_space] * 4 + [vmem] * 5,
        out_specs=[vmem] * 15,
        out_shape=[rows] * 9
        + [
            jax.ShapeDtypeStruct((width, count), BF),
            jax.ShapeDtypeStruct((width // 128, 8, count), F32),
            jax.ShapeDtypeStruct((1, 6 * width), F32),
            jax.ShapeDtypeStruct((count, 128), F32),
            jax.ShapeDtypeStruct((count, 128), F32),
            jax.ShapeDtypeStruct((1, TEMB), F32),
        ],
        scratch_shapes=[
            pltpu.VMEM(wqkv.shape, BF),
            pltpu.VMEM(ada.shape, BF),
            pltpu.VMEM((2,) + info.shape, F32),
            DMA((2,)),
            DMA((2,)),
            DMA,
            DMA,
            DMA((2, groups)),
            DMA((2, groups)),
            DMA((2, groups)),
            DMA((2, groups)),
        ],
        compiler_params=pltpu.CompilerParams(
            collective_id=1, has_side_effects=True, vmem_limit_bytes=56 << 20
        ),
        name="front",
    )(tokens, cotangent, wqkv, ada, info, ada_bias, gain, cosines, sines)


def ffn_kernel(
    x_ref, o_ref, ot_ref, dy_ref, mod_ref, gain_ref, wout_ref, up_ref, up_bias_ref, down_ref,
    down_bias_ref,
    out_ref, do_ref, dx_ref, vec_ref, dup_bias_ref, ddown_ref, dup_ref, dout_ref,
    middle, branch, h, h_t, dm, acc, dacc,
):
    f = pl.program_id(0)
    count, width = x_ref.shape
    tile = min(256, count)
    shift, scale, gate_one, gate_two = (
        part_of(mod_ref, i, width) for i in (3, 4, 2, 5)
    )

    @pl.when(f == 0)
    def _():
        for r in range(0, count, tile):
            rows = slice(r, r + tile)
            a = dot(o_ref[rows, :], wout_ref[...], ((1,), (0,)))
            branch[rows, :] = a
            x1 = x_ref[rows, :].astype(F32) + gate_one * a
            middle[rows, :] = x1
            normed, _ = normed_rows(x1)
            h2 = (normed * (gain_ref[...] * (1.0 + scale)) + shift).astype(BF)
            h[rows, :] = h2
            h_t[:, rows] = h2.T
            dm_rows = (dy_ref[rows, :].astype(F32) * gate_two).astype(BF)
            dm[rows, :] = dm_rows
            part = jnp.sum(dm_rows.astype(F32), axis=0, keepdims=True)
            vec_ref[5:6, :] = part if r == 0 else vec_ref[5:6, :] + part

    u = dot(h[...], up_ref[...], ((1,), (0,))) + up_bias_ref[...]
    square = u * u
    tanh = jnp.tanh(gelu_coeff * (u + 0.044715 * u * square))
    g = (0.5 * u * (1.0 + tanh)).astype(BF)
    slope = 0.5 * (1.0 + tanh) + (0.5 * gelu_coeff) * u * (1.0 - tanh * tanh) * (
        1.0 + (3 * 0.044715) * square
    )
    part = dot(g, down_ref[...], ((1,), (0,)))
    ddown_ref[...] = dot(g, dm[...], ((0,), (0,))).astype(BF)
    du = (dot(dm[...], down_ref[...], ((1,), (1,))) * slope).astype(BF)
    dup_bias_ref[...] = jnp.sum(du.astype(F32), axis=0, keepdims=True)
    dup_ref[0] = dot(h_t[...], du, ((1,), (0,))).astype(BF)
    dpart = dot(du, up_ref[...], ((1,), (1,)))

    @pl.when(f == 0)
    def _():
        acc[...] = part
        dacc[...] = dpart

    @pl.when(f > 0)
    def _():
        acc[...] += part
        dacc[...] += dpart

    @pl.when(f == pl.num_programs(0) - 1)
    def _():
        sums = [0.0] * 5
        for r in range(0, count, tile):
            rows = slice(r, r + tile)
            m = acc[rows, :] + down_bias_ref[...]
            x1 = middle[rows, :]
            out_ref[rows, :] = (x1 + gate_two * m).astype(BF)
            dy = dy_ref[rows, :].astype(F32)
            dh = dacc[rows, :]
            n2, rscale = normed_rows(x1)
            dhn = dh * n2
            e = dh * ((1.0 + scale) * gain_ref[...])
            dx1 = dy + rscale * (
                e
                - jnp.mean(e, axis=-1, keepdims=True)
                - n2 * jnp.mean(e * n2, axis=-1, keepdims=True)
            )
            dx_ref[rows, :] = dx1
            da = (gate_one * dx1).astype(BF)
            h[rows, :] = da
            for i, value in enumerate((dx1 * branch[rows, :], dh, dhn, dy * m)):
                sums[i] = sums[i] + jnp.sum(value, axis=0, keepdims=True)
            do_ref[rows, :] = dot(da, wout_ref[...], ((1,), (1,))).astype(BF)
        vec_ref[0:1, :] = sums[0]
        vec_ref[1:2, :] = sums[1]
        vec_ref[2:3, :] = sums[2] * gain_ref[...]
        vec_ref[3:4, :] = sums[3]
        vec_ref[4:5, :] = sums[2] * (1.0 + scale)
        dout_ref[...] = dot(ot_ref[...], h[...], ((1,), (0,))).astype(BF)


def ffn(x, o, ot, dy, mod, gain, wout, up, up_bias, down, down_bias):
    count, width = x.shape
    hidden = up.shape[1]
    step = 256
    folds = width // step

    def full(array):
        return pl.BlockSpec(array.shape, lambda f: (0,) * array.ndim)

    rows = jax.ShapeDtypeStruct((count, width), BF)
    outs = [
        rows,
        rows,
        jax.ShapeDtypeStruct((count, width), F32),
        jax.ShapeDtypeStruct((8, width), F32),
        jax.ShapeDtypeStruct((1, hidden), F32),
        jax.ShapeDtypeStruct((hidden, width), BF),
        jax.ShapeDtypeStruct((hidden // width, width, width), BF),
        jax.ShapeDtypeStruct((width, width), BF),
    ]
    up_bias_spec = pl.BlockSpec((1, step), lambda f: (0, f))
    down_spec = pl.BlockSpec((step, width), lambda f: (f, 0))
    return pl.pallas_call(
        ffn_kernel,
        grid=(hidden // step,),
        in_specs=[
            full(x), full(o), full(ot), full(dy), full(mod), full(gain), full(wout),
            pl.BlockSpec((width, step), lambda f: (0, f)), up_bias_spec, down_spec,
            full(down_bias),
        ],
        out_specs=[full(s) for s in outs[:4]]
        + [
            up_bias_spec,
            down_spec,
            pl.BlockSpec((1, width, step), lambda f: (f // folds, 0, f % folds)),
            full(outs[7]),
        ],
        out_shape=outs,
        scratch_shapes=[
            pltpu.VMEM((count, width), F32),
            pltpu.VMEM((count, width), F32),
            pltpu.VMEM((count, width), BF),
            pltpu.VMEM((width, count), BF),
            pltpu.VMEM((count, width), BF),
            pltpu.VMEM((count, width), F32),
            pltpu.VMEM((count, width), F32),
        ],
        compiler_params=pltpu.CompilerParams(vmem_limit_bytes=56 << 20),
        name="ffn",
    )(x, o, ot, dy, mod, gain, wout, up, up_bias, down, down_bias)


def back_kernel(
    groups, wide_size, ring, lag,
    q_ref, ka_ref, va_ref, kb_ref, vb_ref, ba_ref, bb_ref, ot_ref, lse_ref, do_ref, x_ref, h_ref,
    dx_ref, mod_ref, gain_ref, cos_ref, sin_ref, misc_ref, vec_ref, dup_bias_ref,
    wqkv_ref, ddown_ref, dup_ref, dout_ref, rows_ref,
    sum_ref, ssum_ref, tokens_ref, grad_ref,
    wqkv, dqkv, dk_own, dv_own, dk_away, dv_away, dk_in, dv_in, dq_big, dsmall, drows,
    acc, sacc, core_in, score_in, bit_in, sbit_in,
    load_sem, copy_sem, send_sem, recv_sem, kv_send, kv_recv, self_sem, row_send, row_recv,
):
    chunks, pieces, piece_rows = acc.shape[:3]
    outer = (wide_size // 2).bit_length() - 1
    inner = ring.bit_length() - 1
    total_bits = outer + inner
    count, width = x_ref.shape
    span = count // groups
    pairs = width // 128
    folds = ddown_ref.shape[0]
    wide = lax.axis_index("wide")
    chip = lax.axis_index("narrow")
    core = lax.rem(wide, 2)
    base = wide - core
    core_peer = (base + 1 - core, chip)
    dims = []
    for b in range(outer):
        bit = lax.rem(wide // (2 << b), 2)
        dims.append((bit, wide + (1 - 2 * bit) * (2 << b), chip))
    for b in range(inner):
        bit = lax.rem(chip // (1 << b), 2)
        dims.append((bit, wide, chip + (1 - 2 * bit) * (1 << b)))
    up = list(range(outer))
    rest = list(range(outer, total_bits))
    orders = (up + rest, up[::-1] + rest, rest + up)

    load_w = pltpu.make_async_copy(wqkv_ref, wqkv, load_sem)
    load_w.start()
    barrier = pltpu.get_barrier_semaphore()
    for d in dims[:outer]:
        pl.semaphore_signal(barrier, inc=1, device_id=d[1:], device_id_type=MESH)
    for c in range(2):
        for d in range(ring):
            if c or d:
                other = (base + lax.rem(core + c, 2), lax.rem(chip + d, ring))
                pl.semaphore_signal(barrier, inc=1, device_id=other, device_id_type=MESH)
    pl.semaphore_wait(barrier, outer + 2 * ring - 1)

    slot = lax.rem(chip, groups)
    home = chip // groups

    def row_move(src, dst, kind, j):
        rows = pl.ds(j * span, span)
        remote = pltpu.make_async_remote_copy(
            src_ref=src.at[rows],
            dst_ref=dst.at[slot],
            send_sem=row_send.at[kind, j],
            recv_sem=row_recv.at[kind, slot],
            device_id=(base + home, core * groups + j),
            device_id_type=MESH,
        )
        here = pltpu.make_async_copy(src.at[rows], dst.at[slot], self_sem.at[kind])
        own = (home == core) & (slot == j)
        return remote, here, own

    def row_send_all(src, dst, kind):
        for j in range(groups):
            remote, here, own = row_move(src, dst, kind, j)

            @pl.when(own)
            def _():
                here.start()

            @pl.when(jnp.logical_not(own))
            def _():
                remote.start()

    def row_wait_all(src, dst, kind):
        for j in range(groups):
            remote, here, own = row_move(src, dst, kind, j)

            @pl.when(own)
            def _():
                here.wait()

            @pl.when(jnp.logical_not(own))
            def _():
                remote.wait_send()

        for g in range(groups):
            own = (home == core) & (slot == g)

            @pl.when(jnp.logical_not(own))
            def _():
                pltpu.make_async_remote_copy(
                    src_ref=src.at[pl.ds(0, span)],
                    dst_ref=dst.at[g],
                    send_sem=row_send.at[kind, 0],
                    recv_sem=row_recv.at[kind, g],
                    device_id=core_peer,
                    device_id_type=MESH,
                ).wait_recv()

    def plan(kind):
        late = kind // 4
        odd = lax.rem(kind, 2) * (1 - late)
        low = 0
        size = pieces
        steps = []
        for i in range(total_bits):
            bit, peer_wide, peer_here = (
                a + odd * (b - a) + late * (c - a)
                for a, b, c in zip(*(dims[order[i]] for order in orders))
            )
            size //= 2
            before = low
            low = low + bit * size
            steps.append((before + (1 - bit) * size, low, size, (peer_wide, peer_here)))
        return steps

    def stage(step, kind, sem, big, out, total, core_slot, bit_slots):
        cols = total.shape[-1]
        mine = pl.ds(pl.multiple_of(core * cols, 128), cols)
        other = pl.ds(pl.multiple_of((1 - core) * cols, 128), cols)
        steps = plan(kind)

        def remote(src, dst, index, peer):
            return pltpu.make_async_remote_copy(
                src_ref=src,
                dst_ref=dst,
                send_sem=send_sem.at[index, sem],
                recv_sem=recv_sem.at[index, sem],
                device_id=peer,
                device_id_type=MESH,
            )

        def core_copy():
            return remote(big.at[:, :, other], core_slot, 0, core_peer)

        def own_copy():
            return pltpu.make_async_copy(big.at[:, :, mine], total, copy_sem.at[sem])

        def bit_copy(i):
            away, _, size, peer = steps[i]
            return remote(total.at[pl.ds(away, size)], bit_slots[i], 1 + i, peer)

        def back_copy(i):
            _, keep, size, peer = steps[i]
            place = out.at[pl.ds(keep, size), :, mine]
            if i == total_bits - 1:
                return remote(total.at[pl.ds(keep, size)], place, 1 + total_bits + i, peer)
            return remote(place, place, 1 + total_bits + i, peer)

        def keep_copy():
            _, keep, size, _ = steps[-1]
            return pltpu.make_async_copy(
                total.at[pl.ds(keep, size)], out.at[pl.ds(keep, size), :, mine], copy_sem.at[sem]
            )

        def core_back():
            place = out.at[:, :, mine]
            return remote(place, place, 1 + 2 * total_bits, core_peer)

        def add(start, size, from_slot):
            @pl.loop(0, size)
            def _(j):
                total[start + j] = (total[start + j].astype(F32) + from_slot[j].astype(F32)).astype(BF)

        if step == 0:
            core_copy().start()
            own_copy().start()
        elif step == 1:
            own_copy().wait()
            core_copy().wait()
            add(0, pieces, core_slot)
            bit_copy(0).start()
        elif step <= total_bits + 1:
            i = step - 2
            bit_copy(i).wait()
            add(steps[i][1], steps[i][2], bit_slots[i])
            if step <= total_bits:
                bit_copy(i + 1).start()
            else:
                keep_copy().start()
                back_copy(i).start()
        elif step <= 2 * total_bits:
            i = 2 * total_bits + 1 - step
            if i == total_bits - 1:
                keep_copy().wait()
            back_copy(i).wait()
            back_copy(i - 1).start()
        elif step == 2 * total_bits + 1:
            back_copy(0).wait()
            core_back().start()
        else:
            core_back().wait()

    last = 2 * total_bits + 2

    def communicate(tick):
        for step in range(last, -1, -1):
            chunk = tick - lag * step

            def at_chunk(source):
                stage(
                    step, lax.rem(chunk, 5), chunk,
                    source, sum_ref.at[chunk], acc.at[chunk], core_in.at[chunk],
                    [ref.at[chunk] for ref in bit_in],
                )

            if step < 2:
                for source, first, size in (
                    (ddown_ref, 0, folds),
                    (dup_ref, folds, folds),
                    (dout_ref, 2 * folds, 1),
                    (dq_big, 2 * folds + 1, 3),
                ):

                    @pl.when((chunk >= first) & (chunk < first + size))
                    def _():
                        at_chunk(source.at[chunk - first])
            else:

                @pl.when((chunk >= 0) & (chunk < chunks))
                def _():
                    at_chunk(sum_ref.at[chunk])

            @pl.when(chunk == chunks)
            def _():
                stage(step, 0, chunks, dsmall, ssum_ref, sacc, score_in, sbit_in)

    copies = count // 128
    lane = lax.broadcasted_iota(jnp.int32, (1, 128), 1)
    place = pl.ds(pl.multiple_of(core * count, count), count)

    def kv_copies(p):
        cols = pl.ds(pl.multiple_of(p * 128, 128), 128)
        return [
            pltpu.make_async_remote_copy(
                src_ref=away.at[:, cols],
                dst_ref=landing.at[:, cols],
                send_sem=kv_send.at[i, p],
                recv_sem=kv_recv.at[i, p],
                device_id=core_peer,
                device_id_type=MESH,
            )
            for i, (away, landing) in enumerate(((dk_away, dk_in), (dv_away, dv_in)))
        ]

    def attention(p):
        cols = pl.ds(pl.multiple_of(p * 128, 128), 128)
        q = q_ref[:, cols]
        do = do_ref[:, cols]
        prod = ot_ref[cols, :].astype(F32) * do.astype(F32).T
        qs, dos, deltas, lses = [], [], [], []
        for h in range(2):
            picked = (lane // HEAD) == h
            qs.append(jnp.where(picked, q, jnp.zeros_like(q)))
            dos.append(jnp.where(picked, do, jnp.zeros_like(do)))
            deltas.append(jnp.sum(prod[h * HEAD : (h + 1) * HEAD], axis=0, keepdims=True))
            lses.append(lse_ref[p, h : h + 1, :])
        dq = [None, None]
        for k_ref, v_ref, b_ref, dk_ref, dv_ref in (
            (kb_ref, vb_ref, bb_ref, dk_away, dv_away),
            (ka_ref, va_ref, ba_ref, dk_own, dv_own),
        ):
            k = k_ref[:, cols]
            v = v_ref[:, cols]
            k_t = k.T
            dk = dv = None
            for h in range(2):
                s = dot(k, qs[h], ((1,), (1,))) + wide_of(b_ref[...], copies)
                prob = jnp.exp(s - lses[h])
                dv_h = dot(prob.astype(BF), dos[h], ((1,), (0,)))
                dprob = dot(v, dos[h], ((1,), (1,)))
                ds = (prob * (dprob - deltas[h])).astype(BF)
                dk_h = dot(ds, qs[h], ((1,), (0,)))
                part = dot(k_t[h * HEAD : (h + 1) * HEAD], ds, ((1,), (0,)))
                dq[h] = part if dq[h] is None else dq[h] + part
                dk = dk_h if dk is None else dk + dk_h
                dv = dv_h if dv is None else dv + dv_h
            dk_ref[:, cols] = dk.astype(dk_ref.dtype)
            dv_ref[:, cols] = dv.astype(dv_ref.dtype)
        dq_both = (jnp.concatenate(dq, axis=0) * (HEAD**-0.5)).T
        dqkv[:, cols] = rotate(dq_both, cos_ref[place, :], sin_ref[place, :], -1).astype(BF)
        for copy in kv_copies(p):
            copy.start()

    def join():
        @pl.loop(0, pairs)
        def _(p):
            for copy in kv_copies(p):
                copy.wait()
            cols = pl.ds(pl.multiple_of(p * 128, 128), 128)
            dk = dk_own[:, cols] + dk_in[:, cols].astype(F32)
            dv = dv_own[:, cols] + dv_in[:, cols].astype(F32)
            k_cols = pl.ds(pl.multiple_of(width + p * 128, 128), 128)
            v_cols = pl.ds(pl.multiple_of(2 * width + p * 128, 128), 128)
            dqkv[:, k_cols] = rotate(dk, cos_ref[place, :], sin_ref[place, :], -1).astype(BF)
            dqkv[:, v_cols] = dv.astype(BF)

    def weights():
        h_t = h_ref[...].T
        step = 256
        for n in range(3):
            for m in range(width // step):
                cols = pl.ds(n * width + m * step, step)
                block = dot(h_t, dqkv[:, cols], ((1,), (0,))).astype(BF)
                for i in range(pieces):
                    dq_big[n, i, :, m * step : (m + 1) * step] = block[
                        i * piece_rows : (i + 1) * piece_rows
                    ]

    def finish():
        load_w.wait()
        tile = min(256, count)
        scale = 1.0 + part_of(mod_ref, 1, width)
        sums = [0.0, 0.0]
        for r in range(0, count, tile):
            rows = slice(r, r + tile)
            dh = dot(dqkv[rows, :], wqkv[...], ((1,), (1,)))
            n1, rscale = normed_rows(x_ref[rows, :].astype(F32))
            e = dh * (scale * gain_ref[...])
            drows[rows, :] = (
                dx_ref[rows, :]
                + rscale
                * (
                    e
                    - jnp.mean(e, axis=-1, keepdims=True)
                    - n1 * jnp.mean(e * n1, axis=-1, keepdims=True)
                )
            ).astype(BF)
            sums[0] = sums[0] + jnp.sum(dh, axis=0, keepdims=True)
            sums[1] = sums[1] + jnp.sum(dh * n1, axis=0, keepdims=True)
        row_send_all(drows, grad_ref, 1)
        srows = dsmall.shape[1]
        seq = (wide // 2) * ring + chip
        seqs = wide_size * groups
        line = lax.broadcasted_iota(jnp.int32, (pieces * srows, width), 0)
        line_lane = lax.broadcasted_iota(jnp.int32, (1, width), 1)
        held = jnp.where((line_lane == seq) & (core == 0), 1.0, 0.0)
        fixed = seqs * 6
        entries = [
            (seq * 6, sums[0]),
            (seq * 6 + 1, sums[1] * gain_ref[...]),
            (seq * 6 + 2, vec_ref[0:1, :]),
            (seq * 6 + 3, vec_ref[1:2, :]),
            (seq * 6 + 4, vec_ref[2:3, :]),
            (seq * 6 + 5, vec_ref[3:4, :]),
            (fixed, sums[1] * scale),
            (fixed + 1, vec_ref[4:5, :]),
            (fixed + 2, vec_ref[5:6, :]),
            (fixed + 3, held * misc_ref[:, 0:1]),
            (fixed + 4, held * misc_ref[:, 1:2]),
        ] + [(fixed + 5 + i, dup_bias_ref[i : i + 1, :]) for i in range(folds)]
        value = jnp.zeros((pieces * srows, width), F32)
        for at, entry in entries:
            value = jnp.where(line == at, entry, value)
        dsmall[...] = value.reshape(pieces, srows, width).astype(BF)

    row_send_all(rows_ref, tokens_ref, 0)

    @pl.loop(0, chunks + 1 + lag * last)
    def _(tick):
        communicate(tick)

        @pl.when(tick < pairs)
        def _():
            attention(tick)

        @pl.when(tick == pairs)
        def _():
            join()
            weights()

        @pl.when(tick == pairs + 1)
        def _():
            finish()

    row_wait_all(rows_ref, tokens_ref, 0)
    row_wait_all(drows, grad_ref, 1)


def back(
    q, ka, va, kb, vb, ba, bb, ot, lse, do, x, h, dx, mod, gain, cosines, sines, misc, vec,
    dup_bias, wqkv, ddown, dup, dout, out_rows, groups, wide_size, ring, lag,
):
    count, width = x.shape
    pieces = wide_size // 2 * ring
    rows = width // pieces
    half = width // 2
    folds = ddown.shape[0] // width
    chunks = 2 * folds + 4
    pairs = width // 128
    total_bits = pieces.bit_length() - 1
    assert width // 256 * 256 == width and chunks > pairs + 2
    srows = -(-(wide_size * groups * 6 + 5 + folds) // (pieces * 8)) * 8
    sizes = [pieces >> (i + 1) for i in range(total_bits)]
    any_space = pl.BlockSpec(memory_space=pl.ANY)
    vmem = pl.BlockSpec(memory_space=pltpu.VMEM)
    block = jax.ShapeDtypeStruct((groups, count // groups, width), BF)
    return pl.pallas_call(
        functools.partial(back_kernel, groups, wide_size, ring, lag),
        in_specs=[vmem] * 20 + [any_space] * 5,
        out_specs=[any_space] * 4,
        out_shape=[
            jax.ShapeDtypeStruct((chunks, pieces, rows, width), BF),
            jax.ShapeDtypeStruct((pieces, srows, width), BF),
            block,
            block,
        ],
        scratch_shapes=[
            pltpu.VMEM(wqkv.shape, BF),
            pltpu.VMEM((count, 3 * width), BF),
            pltpu.VMEM((count, width), F32),
            pltpu.VMEM((count, width), F32),
            pltpu.VMEM((count, width), BF),
            pltpu.VMEM((count, width), BF),
            pltpu.VMEM((count, width), BF),
            pltpu.VMEM((count, width), BF),
            pltpu.VMEM((3, pieces, rows, width), BF),
            pltpu.VMEM((pieces, srows, width), BF),
            pltpu.VMEM((count, width), BF),
            pltpu.VMEM((chunks, pieces, rows, half), BF),
            pltpu.VMEM((pieces, srows, half), BF),
            pltpu.VMEM((chunks, pieces, rows, half), BF),
            pltpu.VMEM((pieces, srows, half), BF),
            [pltpu.VMEM((chunks, n, rows, half), BF) for n in sizes],
            [pltpu.VMEM((n, srows, half), BF) for n in sizes],
            DMA,
            DMA((chunks + 1,)),
            DMA((2 + 2 * total_bits, chunks + 1)),
            DMA((2 + 2 * total_bits, chunks + 1)),
            DMA((2, pairs)),
            DMA((2, pairs)),
            DMA((2,)),
            DMA((2, groups)),
            DMA((2, groups)),
        ],
        compiler_params=pltpu.CompilerParams(
            collective_id=0, has_side_effects=True, vmem_limit_bytes=62 << 20
        ),
        name="back",
    )(
        q, ka, va, kb, vb, ba, bb, ot, lse, do, x, h, dx, mod, gain, cosines, sines, misc, vec,
        dup_bias, wqkv,
        ddown.reshape(folds, pieces, rows, width),
        dup.reshape(folds, pieces, rows, width),
        dout.reshape(1, pieces, rows, width),
        out_rows,
    )


def local(
    tokens, step_ids, prefix, keep_bits, ada_weight, ada_bias, norm1_gain, qkv_weight, out_weight,
    norm2_gain, up_weight, up_bias, down_weight, down_bias, cotangent,
):
    wide_size = lax.axis_size("wide")
    ring = lax.axis_size("narrow")
    groups, span, width = tokens.shape
    assert ring == 2 * groups and wide_size % 2 == 0
    length = ring * span
    hidden = up_weight.shape[1]
    folds = hidden // width
    seqs = wide_size * groups

    allowed = (jnp.arange(length, dtype=jnp.int32)[None, :] < prefix[:, None]) | (keep_bits == 1)
    lanes = jnp.arange(TEMB, dtype=jnp.int32)[None, :]
    steps = step_ids[:, None]
    info = jnp.concatenate(
        [
            jax.nn.silu(time_embed(step_ids)),
            jnp.where(allowed, 0.0, masked_score),
            jnp.where(lanes == 0, steps // 32, jnp.where(lanes == 1, steps % 32, 0)).astype(F32),
        ],
        axis=1,
    )[:, None, :]
    cosines, sines = rope_tables(length)
    x, dy, h, q, ka, va, kb, vb, o, ot, lse, mod, ba, bb, misc = front(
        tokens, cotangent, qkv_weight, ada_weight, info, ada_bias[None], norm1_gain[None],
        cosines, sines, ring,
    )
    out_rows, do, dx, vec, dup_bias, ddown, dup, dout = ffn(
        x, o, ot, dy, mod, norm2_gain[None], out_weight, up_weight, up_bias[None], down_weight,
        down_bias[None],
    )
    summed, small, outputs, input_grad = back(
        q, ka, va, kb, vb, ba, bb, ot, lse, do, x, h, dx, mod, norm1_gain[None], cosines, sines,
        misc, vec, dup_bias.reshape(folds, width), qkv_weight, ddown, dup, dout, out_rows,
        groups, wide_size, ring, LAG,
    )
    summed = summed.reshape(-1, width, width)
    small = small.reshape(-1, width).astype(F32)
    at = seqs * 6
    mod_all = small[:at].reshape(seqs, 6 * width)
    steps_all = small[at + 3, :seqs] * 32 + small[at + 4, :seqs]
    ada_grad = jnp.dot(
        mod_all.T, jax.nn.silu(time_embed(steps_all)), precision=lax.Precision.HIGHEST,
        preferred_element_type=F32,
    )

    def untile(array):
        return jnp.concatenate([array[i] for i in range(array.shape[0])], axis=1).astype(F32)

    return (
        outputs,
        input_grad,
        ada_grad,
        jnp.sum(mod_all, axis=0),
        small[at],
        untile(summed[2 * folds + 1 :]),
        summed[2 * folds].astype(F32),
        small[at + 1],
        untile(summed[folds : 2 * folds]),
        small[at + 5 : at + 5 + folds].reshape(-1),
        summed[:folds].reshape(hidden, width).astype(F32),
        small[at + 2],
    )


def solution(mesh):
    split = P("wide", "narrow", None)
    in_specs = (
        (split, P("wide"), P("wide"), P("wide", None)) + (P(),) * 10 + (split,)
    )
    out_specs = (split, split) + (P(),) * 10
    return jax.shard_map(local, mesh=mesh, in_specs=in_specs, out_specs=out_specs, check_vma=False)
```

time: 464 us -> 289 us (0.62); the launches traced: 455 us -> 288 us
  matrix products: 59.2 us -> 2.75 us
  local copies, waits for them, and re-layouts: 69.9 us -> 18.8 us
  other arithmetic: 59.4 us -> 18.9 us
  Pallas kernels: 214 us -> 247 us
  starting transfers between devices: 23 us -> 0 us
  waiting for transfers between devices: 19.7 us -> 0 us
  blocking collectives: 6.69 us -> 0 us
    dot_general x14 -> x1, matrix products: 59.2 us -> 2.75 us  [local(): jnp.dot(mod_all.T, jax.nn.silu(time_embed(steps_all)), precision=lax.Prec...]
    pallas_call x3, Pallas kernels: 214 us -> 247 us  [the longest x1 168 us: back(): pl.pallas_call(functools.partial(back_kernel, groups, wide_size, ring, la...]
    ppermute x13 -> x0, starting transfers between devices: 23 us -> none  [the longest x4 10.8 us: bring(): lax.ppermute(lax.dynamic_index_in_dim(array, (step + chip) % groups, 0, k...]
    ppermute x13 -> x0, waiting for transfers between devices: 19.7 us -> none  [the longest x4 11.8 us: bring(): lax.ppermute(lax.dynamic_index_in_dim(array, (step + chip) % groups, 0, k...]
    concatenate x5 -> x1, other arithmetic: 15.2 us -> 0.01 us  [local(): jnp.concatenate([jax.nn.silu(time_embed(step_ids)), jnp.where(allowed, 0....]
    convert_element_type x4 -> x0, local copies, waits for them, and re-layouts: 12.6 us -> none  [the longest x1 5.75 us: local(): qkv_grad = dot(normed_low, joined, ((0,), (0,))).astype(BF)]
    reshape x6 -> x4, local copies, waits for them, and re-layouts: 13.2 us -> 1.46 us  [the longest x1 0.61 us: local(): dup_bias.reshape(folds, width)]
    another operation x7 -> x0, other arithmetic: 9.38 us -> none
  transfers between devices with their start and end apart: 13 -> 0, of which waited for: 3 -> 0; matrix products, arithmetic and copies ran while one was open for 16% -> 0% of each run, Pallas kernels for 0% -> 0%
where the time goes in v2:
time: 289 us; the launch traced here: 288 us
  Pallas kernels  247 us (85%)
  other arithmetic  18.9 us (7%)
  local copies, waits for them, and re-layouts  18.8 us (7%)
    pallas_call x1, Pallas kernels, back(): pl.pallas_call(functools.partial(back_kernel, groups, wide_size, ring, la...  168 us
    pallas_call x1, Pallas kernels, front(): pl.pallas_call(functools.partial(front_kernel, groups, ring), in_specs=[a...  40 us
    pallas_call x1, Pallas kernels, ffn(): pl.pallas_call(ffn_kernel, grid=(hidden // step,), in_specs=[full(x), ful...  39.8 us
    convert_element_type x2, other arithmetic, untile(): jnp.concatenate([array[i] for i in range(array.shape[0])], axis=1)  7.51 us

profile of v2, /device:TPU:1, one launch (start us, length us, event | category | flops | bytes accessed | tf_op | source)
XLA Modules:
  0.0 288.5 jit_solution(15135321988113012657)
XLA Ops:
  0.7 0.7 fusion.11
  1.7 1.3 broadcast_in_dim.80.gain_ref
  3.0 1.3 broadcast_in_dim.81.gain_ref
  4.2 1.3 broadcast_in_dim.83.down_bias_ref
  5.5 0.8 or_select_fusion
  6.9 1.3 broadcast_in_dim.79.ada_bias_ref
  8.2 40.0 %front.1 = (bf16[512,768]{1,0:T(8,128)(2,1)}, bf16[512,768]{1,0:T(8,128)(2,1)}, bf16[512,768]{1,0:T(8,128)(2,1)}, bf16[512,768]{1,0:T(8,128)(2,1)}, bf16[512,768...) custom-call(bf16[2,256,768]{2,1,0:T(8,128)(2,1)} %tok_ref.1, ...), custom_call_target="tpu_custom_call" | custom-call | tf_op jit(solution)/shard_map/front/pallas_call | solution.py:276
  48.2 39.8 %ffn.1 = (bf16[512,768]{1,0:T(8,128)(2,1)}, bf16[512,768]{1,0:T(8,128)(2,1)}, f32[512,768]{1,0:T(8,128)}, f32[8,768]{1,0:T(8,128)}, f32[1,3072]{1,0:T(1,128)}, /...) custom-call(bf16[512,768]{1,0:T(8,128)(2,1)} %get-tuple-element.48.x_ref, ...), custom_call_target="tpu_custom_call" | custom-call | tf_op jit(solution)/shard_map/ffn/pallas_call | solution.py:417
  88.5 1.4 reduce.9
  90.5 167.6 %back.1 = (bf16[12,16,48,768]{3,2,1,0:T(8,128)(2,1)}, bf16[16,8,768]{2,1,0:T(8,128)(2,1)}, bf16[2,256,768]{2,1,0:T(8,128)(2,1)}, bf16[2,256,768]{2,1,0:T(8,128)(2,1)}) custom-call(bf16[512,768]{1,0:T(8,128)(2,1)} %get-tuple-element.39.q_ref, bf16[512,768]{1,0:T(8,128)(2,1)} %get-tuple-element.40.ka_ref, bf16[512,768]{1,0:T(8,128)(2,1)} %get-tuple-element.41.va_ref, ...), custom_call_target="tpu_custom_call" | custom-call | tf_op jit(solution)/shard_map/back/pallas_call | solution.py:846
  258.1 0.9 slice.72
  259.2 0.9 slice.91
  260.2 0.7 reduce_sum.9
  260.9 1.0 convert_bitcast_fusion
  261.9 0.6 slice_reduce_fusion
  263.2 2.8 fusion
  266.0 2.6 slice.87
  268.6 4.1 %fusion.10 = (bf16[1,16,48,768]{3,2,1,0:T(8,128)(2,1)S(1)}, bf16[1,16,48,768]{3,2,1,0:T(8,128)(2,1)S(1)}, bf16[1,16,48,768]{3,2,1,0:T(8,128)(2,1)S(1)}, bf16[1,1...) fusion(bf16[12,16,48,768]{3,2,1,0:T(8,128)(2,1)} %get-tuple-ele, ...), kind=kLoop, calls=%fused_computation.38 | loop fusion | bytes 18874368 | tf_op jit(solution)/shard_map/slice | solution.py:947
  272.8 1.7 bitcast_convert_fusion.1
  274.4 4.3 %maximum_convert_fusion = f32[768,3072]{1,0:T(8,128)} fusion(bf16[768,768]{1,0:T(8,128)(2,1)S(1)} %bitcast.23, bf16[768,768]{1,0:T(8,128)(2,1)S(1)} %bitcast.24, bf16[768,768]{1,0:T(8,128)(2,1)S(1)} %bitcast.25, bf16[768,768]{1,0:T(8,128)(2,1)S(1)} %bitcast.22), kind=kLoop, calls=%fused_computation | loop fusion | flops 18874368 | bytes 14155776 | tf_op jit(solution)/shard_map/convert_element_type | solution.py:947
  278.7 4.8 %bitcast_convert_fusion = f32[3072,768]{1,0:T(8,128)} fusion(bf16[4,16,48,768]{3,2,1,0:T(8,128)(2,1)S(1)} %slice.87), kind=kLoop, calls=%fused_computation.1 | loop fusion | flops 2359296 | bytes 14155776 | tf_op jit(solution)/shard_map/convert_element_type | solution.py:960
  283.5 3.2 %maximum_convert_fusion.1 = f32[768,2304]{1,0:T(8,128)} fusion(bf16[768,768]{1,0:T(8,128)(2,1)S(1)} %bitcast.26, bf16[768,768]{1,0:T(8,128)(2,1)S(1)} %bitcast.27, bf16[768,768]{1,0:T(8,128)(2,1)S(1)} %bitcast.28), kind=kLoop, calls=%fused_computation.2 | loop fusion | flops 10616832 | bytes 10616832 | tf_op jit(solution)/shard_map/convert_element_type | solution.py:947
  286.7 0.9 copy.31
  287.6 0.9 copy.32
  (19 shorter events, 3.0 us)
Async XLA Ops:
  283.5 3.2 %copy-start.1 = (bf16[2,256,768]{2,1,0:T(8,128)(2,1)S(1)}, bf16[2,256,768]{2,1,0:T(8,128)(2,1)}, u32[]{:S(2)}) copy-start(bf16[2,256,768]{2,1,0:T(8,128)(2,1)} %get-tuple-element.98) | copy-start | bytes 2359300
  283.5 4.1 %copy-start = (bf16[2,256,768]{2,1,0:T(8,128)(2,1)S(1)}, bf16[2,256,768]{2,1,0:T(8,128)(2,1)}, u32[]{:S(2)}) copy-start(bf16[2,256,768]{2,1,0:T(8,128)(2,1)} %get-tuple-element.99) | copy-start | bytes 2359300

commit v3 on v2

v3 whole, which is shorter than its diff:
```python
import functools
import math

import jax
import jax.numpy as jnp
import numpy as np
from jax import lax
from jax.experimental import pallas as pl
from jax.experimental.pallas import tpu as pltpu
from jax.sharding import PartitionSpec as P

HEAD = 64
TEMB = 128
MESH = pl.DeviceIdType.MESH
BF = jnp.bfloat16
F32 = jnp.float32
DMA = pltpu.SemaphoreType.DMA

norm_epsilon = 1e-05
gelu_coeff = 0.7978845608028654
masked_score = -1e30


def time_embed(step_ids):
    halfway = TEMB // 2
    frequency = jnp.exp(jnp.arange(halfway, dtype=F32) * (-math.log(10000.0) / halfway))
    angles = step_ids.astype(F32)[:, None] * frequency[None, :]
    return jnp.concatenate([jnp.cos(angles), jnp.sin(angles)], axis=-1)


def rope_tables(length):
    halfway = HEAD // 2
    inverse = 10000.0 ** (-2.0 * np.arange(halfway) / HEAD)
    angles = np.arange(length)[:, None] * inverse[None, :]
    sines = np.sin(angles)
    return (
        np.tile(np.cos(angles), (1, 4)).astype(np.float32),
        np.concatenate([-sines, sines, -sines, sines], axis=1).astype(np.float32),
    )


def dot(former, latter, dims):
    return lax.dot_general(former, latter, (dims, ((), ())), preferred_element_type=F32)


def rotate(values, cosines, sines, sign):
    lane = lax.broadcasted_iota(jnp.int32, (1, 128), 1)
    first = (lane % HEAD) < HEAD // 2
    parts = []
    for n in range(values.shape[1] // 128):
        part = values[:, n * 128 : (n + 1) * 128]
        partner = jnp.where(first, pltpu.roll(part, 128 - HEAD // 2, 1), pltpu.roll(part, HEAD // 2, 1))
        turned = partner * sines
        parts.append(part * cosines + (turned if sign > 0 else -turned))
    return parts[0] if len(parts) == 1 else jnp.concatenate(parts, axis=1)


def normed_rows(values):
    center = values - jnp.mean(values, axis=-1, keepdims=True)
    spread = jnp.mean(center * center, axis=-1, keepdims=True)
    scale = lax.rsqrt(spread + norm_epsilon)
    return center * scale, scale


def part_of(mod_ref, index, width):
    return mod_ref[:, index * width : (index + 1) * width]


def wide_of(block, copies):
    return jnp.concatenate([block] * copies, axis=1)


def front_kernel(
    groups, ring,
    tok_ref, cot_ref, wqkv_ref, ada_ref, info_ref, par_ref, cos_ref, sin_ref,
    x_ref, dy_ref, h_ref, q_ref, ka_ref, va_ref, kb_ref, vb_ref, o_ref, ot_ref, lse_ref,
    mod_ref, ba_ref, bb_ref, cond_ref,
    wqkv, ada, table,
    load_sem, self_sem, info_send, info_recv, send_sem, recv_sem, kv_send, kv_recv,
):
    span, width = tok_ref.shape[1:]
    count = groups * span
    wide = lax.axis_index("wide")
    chip = lax.axis_index("narrow")
    core = lax.rem(wide, 2)
    base = wide - core
    peer = (base + 1 - core, chip)

    load_w = pltpu.make_async_copy(wqkv_ref, wqkv, load_sem.at[0])
    load_a = pltpu.make_async_copy(ada_ref, ada, load_sem.at[1])
    load_a.start()
    load_w.start()

    barrier = pltpu.get_barrier_semaphore()
    for c in range(2):
        for d in range(ring):
            if c or d:
                other = (base + lax.rem(core + c, 2), lax.rem(chip + d, ring))
                pl.semaphore_signal(barrier, inc=1, device_id=other, device_id_type=MESH)
    pl.semaphore_wait(barrier, 2 * ring - 1)

    slot = lax.rem(chip, groups)
    to_core = chip // groups
    rows_out = pl.ds(pl.multiple_of(slot * span, span), span)

    def move(src, dst, kind, g):
        remote = pltpu.make_async_remote_copy(
            src_ref=src.at[g],
            dst_ref=dst.at[rows_out],
            send_sem=send_sem.at[kind, g],
            recv_sem=recv_sem.at[kind, slot],
            device_id=(base + to_core, core * groups + g),
            device_id_type=MESH,
        )
        here = pltpu.make_async_copy(src.at[g], dst.at[rows_out], self_sem.at[kind])
        own = (to_core == core) & (slot == g)
        return remote, here, own

    def send(src, dst, kind):
        for g in range(groups):
            remote, here, own = move(src, dst, kind, g)

            @pl.when(own)
            def _():
                here.start()

            @pl.when(jnp.logical_not(own))
            def _():
                remote.start()

    def sent(src, dst, kind):
        for g in range(groups):
            remote, here, own = move(src, dst, kind, g)

            @pl.when(jnp.logical_not(own))
            def _():
                remote.wait_send()

    def arrive(src, dst, kind, j):
        rows = pl.ds(j * span, span)
        own = (to_core == core) & (slot == j)

        @pl.when(own)
        def _():
            pltpu.make_async_copy(src.at[0], dst.at[rows], self_sem.at[kind]).wait()

        @pl.when(jnp.logical_not(own))
        def _():
            pltpu.make_async_remote_copy(
                src_ref=src.at[0],
                dst_ref=dst.at[rows],
                send_sem=send_sem.at[kind, 0],
                recv_sem=recv_sem.at[kind, j],
                device_id=peer,
                device_id_type=MESH,
            ).wait_recv()

    send(tok_ref, x_ref, 0)
    table[core] = info_ref[...]
    swap_info = pltpu.make_async_remote_copy(
        src_ref=info_ref,
        dst_ref=table.at[core],
        send_sem=info_send,
        recv_sem=info_recv,
        device_id=peer,
        device_id_type=MESH,
    )
    swap_info.start()
    swap_info.wait()
    row = table[chip // groups, lax.rem(chip, groups)]
    length = row.shape[1] - TEMB
    cond_ref[...] = row[:, :TEMB]
    bias = jnp.where(core == 0, row[:, TEMB : TEMB + count], row[:, TEMB + count : TEMB + length])
    ba_ref[...] = jnp.broadcast_to(bias, (128, count)).T
    bias = jnp.where(core == 1, row[:, TEMB : TEMB + count], row[:, TEMB + count : TEMB + length])
    bb_ref[...] = jnp.broadcast_to(bias, (128, count)).T

    cond = jnp.broadcast_to(row[:, :TEMB], (16, TEMB))
    high = cond.astype(BF).astype(F32)
    middle = (cond - high).astype(BF).astype(F32)
    low = cond - high - middle
    line = lax.broadcasted_iota(jnp.int32, (16, TEMB), 0)
    three = jnp.where(
        line == 0, high, jnp.where(line == 1, middle, jnp.where(line == 2, low, 0.0))
    ).astype(BF)
    load_a.wait()
    for i in range(6):
        cols = slice(i * width, (i + 1) * width)
        mod_ref[:, cols] = (
            jnp.sum(dot(three, ada[cols, :], ((1,), (1,))), axis=0, keepdims=True)
            + par_ref[3 + i : 4 + i, :]
        )
    shift = part_of(mod_ref, 0, width)
    scale = par_ref[0:1, :] * (1.0 + part_of(mod_ref, 1, width))

    load_w.wait()
    swaps = []
    for j in range(groups):
        rows = pl.ds(j * span, span)
        arrive(tok_ref, x_ref, 0, j)
        if j == groups - 1:
            send(cot_ref, dy_ref, 1)
        normed, _ = normed_rows(x_ref[rows, :].astype(F32))
        h_ref[rows, :] = (normed * scale + shift).astype(BF)
        place = pl.ds(pl.multiple_of(core * count + j * span, span), span)
        cosines = cos_ref[place, :]
        sines = sin_ref[place, :]
        step = 256
        for n in (2, 1, 0):
            target = (q_ref, ka_ref, va_ref)[n]
            for m in range(width // step):
                cols = pl.ds(n * width + m * step, step)
                block = dot(h_ref[rows, :], wqkv[:, cols], ((1,), (0,)))
                if n < 2:
                    block = rotate(block, cosines, sines, 1)
                if n == 0:
                    block = block * HEAD**-0.5
                target[rows, m * step : (m + 1) * step] = block.astype(BF)
            if n > 0:
                swap = pltpu.make_async_remote_copy(
                    src_ref=target.at[rows],
                    dst_ref=(kb_ref, vb_ref)[n - 1].at[rows],
                    send_sem=kv_send.at[n - 1, j],
                    recv_sem=kv_recv.at[n - 1, j],
                    device_id=peer,
                    device_id_type=MESH,
                )
                swap.start()
                swaps.append(swap)
    for swap in swaps:
        swap.wait()

    copies = count // 128
    lane = lax.broadcasted_iota(jnp.int32, (1, 128), 1)

    @pl.loop(0, width // 128)
    def _(p):
        cols = pl.ds(pl.multiple_of(p * 128, 128), 128)
        q = q_ref[:, cols]
        ka = ka_ref[:, cols]
        kb = kb_ref[:, cols]
        va_t = va_ref[:, cols].T
        vb_t = vb_ref[:, cols].T
        outs = []
        for h in range(2):
            qm = jnp.where((lane // HEAD) == h, q, jnp.zeros_like(q))
            sa = dot(ka, qm, ((1,), (1,))) + wide_of(ba_ref[...], copies)
            sb = dot(kb, qm, ((1,), (1,))) + wide_of(bb_ref[...], copies)
            top = jnp.maximum(jnp.max(sa, axis=0, keepdims=True), jnp.max(sb, axis=0, keepdims=True))
            pa = jnp.exp(sa - top)
            pb = jnp.exp(sb - top)
            total = jnp.sum(pa, axis=0, keepdims=True) + jnp.sum(pb, axis=0, keepdims=True)
            part = slice(h * HEAD, (h + 1) * HEAD)
            out = dot(va_t[part], pa.astype(BF), ((1,), (0,))) + dot(
                vb_t[part], pb.astype(BF), ((1,), (0,))
            )
            outs.append(out / total)
            lse_ref[p, h : h + 1, :] = top + jnp.log(total)
        both = jnp.concatenate(outs, axis=0)
        ot_ref[cols, :] = both.astype(BF)
        o_ref[:, cols] = both.T.astype(BF)

    sent(tok_ref, x_ref, 0)
    for j in range(groups):
        arrive(cot_ref, dy_ref, 1, j)
    sent(cot_ref, dy_ref, 1)


def front(tokens, cotangent, wqkv, ada, info, params, cosines, sines, ring):
    groups, span, width = tokens.shape
    count = groups * span
    any_space = pl.BlockSpec(memory_space=pl.ANY)
    vmem = pl.BlockSpec(memory_space=pltpu.VMEM)
    rows = jax.ShapeDtypeStruct((count, width), BF)
    return pl.pallas_call(
        functools.partial(front_kernel, groups, ring),
        in_specs=[any_space] * 4 + [vmem] * 4,
        out_specs=[vmem] * 15,
        out_shape=[rows] * 9
        + [
            jax.ShapeDtypeStruct((width, count), BF),
            jax.ShapeDtypeStruct((width // 128, 8, count), F32),
            jax.ShapeDtypeStruct((1, 6 * width), F32),
            jax.ShapeDtypeStruct((count, 128), F32),
            jax.ShapeDtypeStruct((count, 128), F32),
            jax.ShapeDtypeStruct((1, TEMB), F32),
        ],
        scratch_shapes=[
            pltpu.VMEM(wqkv.shape, BF),
            pltpu.VMEM(ada.shape, BF),
            pltpu.VMEM((2,) + info.shape, F32),
            DMA((2,)),
            DMA((2,)),
            DMA,
            DMA,
            DMA((2, groups)),
            DMA((2, groups)),
            DMA((2, groups)),
            DMA((2, groups)),
        ],
        compiler_params=pltpu.CompilerParams(
            collective_id=1, has_side_effects=True, vmem_limit_bytes=56 << 20
        ),
        name="front",
    )(tokens, cotangent, wqkv, ada, info, params, cosines, sines)


def rest_kernel(
    groups, wide_size, ring, lags,
    x_ref, o_ref, ot_ref, dy_ref, mod_ref, par_ref, cos_ref, sin_ref, cond_ref, lse_ref, wout_ref,
    q_in, ka_in, va_in, kb_in, vb_in, h_in, ba_in, bb_in, up_ref, down_ref, wqkv_ref,
    sum_ref, ssum_ref, tokens_ref, grad_ref,
    q_ref, ka_ref, va_ref, kb_ref, vb_ref, h_ref, ba_ref, bb_ref,
    weights, staging, dsmall, middle, branch, normed_low, normed_t, dm, total_a, total_b, active,
    slope, dq_t, vec, dup_bias, out_rows, drows, dqkv, dk_in, dv_in,
    acc, sacc, core_in, score_in, bit_in, sbit_in,
    load_sem, weight_sem, copy_sem, send_sem, recv_sem, kv_send, kv_recv, self_sem, row_send,
    row_recv,
):
    chunks, pieces, piece_rows = acc.shape[:3]
    slots = core_in.shape[0]
    subs = x_ref.shape[1] // (2 * acc.shape[-1])
    stages = staging.shape[0]
    outer = (wide_size // 2).bit_length() - 1
    inner = ring.bit_length() - 1
    total_bits = outer + inner
    count, width = x_ref.shape
    span = count // groups
    pairs = width // 128
    folds = up_ref.shape[1] // width
    early = (2 * folds + 1) * subs
    gap = 2 * pairs - subs + 2
    wide = lax.axis_index("wide")
    chip = lax.axis_index("narrow")
    core = lax.rem(wide, 2)
    base = wide - core
    core_peer = (base + 1 - core, chip)
    dims = []
    for b in range(outer):
        bit = lax.rem(wide // (2 << b), 2)
        dims.append((bit, wide + (1 - 2 * bit) * (2 << b), chip))
    for b in range(inner):
        bit = lax.rem(chip // (1 << b), 2)
        dims.append((bit, wide, chip + (1 - 2 * bit) * (1 << b)))
    up = list(range(outer))
    rest = list(range(outer, total_bits))
    orders = (up + rest, up[::-1] + rest, rest + up)

    def load_up(i, slot):
        cols = pl.ds(pl.multiple_of(i * width, width), width)
        return pltpu.make_async_copy(up_ref.at[:, cols], weights.at[slot], weight_sem.at[slot])

    def load_down(i, slot):
        rows = pl.ds(pl.multiple_of(i * width, width), width)
        return pltpu.make_async_copy(down_ref.at[rows], weights.at[slot], weight_sem.at[slot])

    def load_qkv(n):
        cols = pl.ds(n * width, width)
        return pltpu.make_async_copy(wqkv_ref.at[:, cols], weights.at[n], weight_sem.at[n])

    for i in range(2):
        load_up(i, 2 * i).start()
        load_down(i, 2 * i + 1).start()
    loads = [
        pltpu.make_async_copy(src, dst, load_sem.at[i])
        for i, (src, dst) in enumerate(
            (
                (q_in, q_ref), (ka_in, ka_ref), (va_in, va_ref), (kb_in, kb_ref), (vb_in, vb_ref),
                (h_in, h_ref), (ba_in, ba_ref), (bb_in, bb_ref),
            )
        )
    ]
    for load in loads:
        load.start()
    barrier = pltpu.get_barrier_semaphore()
    for d in dims[:outer]:
        pl.semaphore_signal(barrier, inc=1, device_id=d[1:], device_id_type=MESH)
    for c in range(2):
        for d in range(ring):
            if c or d:
                other = (base + lax.rem(core + c, 2), lax.rem(chip + d, ring))
                pl.semaphore_signal(barrier, inc=1, device_id=other, device_id_type=MESH)
    pl.semaphore_wait(barrier, outer + 2 * ring - 1)

    slot = lax.rem(chip, groups)
    home = chip // groups

    def row_move(src, dst, kind, j):
        rows = pl.ds(j * span, span)
        remote = pltpu.make_async_remote_copy(
            src_ref=src.at[rows],
            dst_ref=dst.at[slot],
            send_sem=row_send.at[kind, j],
            recv_sem=row_recv.at[kind, slot],
            device_id=(base + home, core * groups + j),
            device_id_type=MESH,
        )
        here = pltpu.make_async_copy(src.at[rows], dst.at[slot], self_sem.at[kind])
        own = (home == core) & (slot == j)
        return remote, here, own

    def row_send_all(src, dst, kind):
        for j in range(groups):
            remote, here, own = row_move(src, dst, kind, j)

            @pl.when(own)
            def _():
                here.start()

            @pl.when(jnp.logical_not(own))
            def _():
                remote.start()

    def row_wait_all(src, dst, kind):
        for j in range(groups):
            remote, here, own = row_move(src, dst, kind, j)

            @pl.when(own)
            def _():
                here.wait()

            @pl.when(jnp.logical_not(own))
            def _():
                remote.wait_send()

        for g in range(groups):
            own = (home == core) & (slot == g)

            @pl.when(jnp.logical_not(own))
            def _():
                pltpu.make_async_remote_copy(
                    src_ref=src.at[pl.ds(0, span)],
                    dst_ref=dst.at[g],
                    send_sem=row_send.at[kind, 0],
                    recv_sem=row_recv.at[kind, g],
                    device_id=core_peer,
                    device_id_type=MESH,
                ).wait_recv()

    def plan(kind):
        late = kind // 4
        odd = lax.rem(kind, 2) * (1 - late)
        low = 0
        size = pieces
        steps = []
        for i in range(total_bits):
            bit, peer_wide, peer_here = (
                a + odd * (b - a) + late * (c - a)
                for a, b, c in zip(*(dims[order[i]] for order in orders))
            )
            size //= 2
            before = low
            low = low + bit * size
            steps.append((before + (1 - bit) * size, low, size, (peer_wide, peer_here)))
        return steps

    def stage(step, kind, sem, lane_base, big, out, total, core_slot, bit_slots):
        cols = total.shape[-1]
        mine = pl.ds(pl.multiple_of(lane_base + core * cols, 128), cols)
        other = pl.ds(pl.multiple_of(lane_base + (1 - core) * cols, 128), cols)
        steps = plan(kind)

        def remote(src, dst, index, peer):
            return pltpu.make_async_remote_copy(
                src_ref=src,
                dst_ref=dst,
                send_sem=send_sem.at[index, sem],
                recv_sem=recv_sem.at[index, sem],
                device_id=peer,
                device_id_type=MESH,
            )

        def core_copy():
            return remote(big.at[:, :, other], core_slot, 0, core_peer)

        def own_copy():
            return pltpu.make_async_copy(big.at[:, :, mine], total, copy_sem.at[sem])

        def bit_copy(i):
            away, _, size, peer = steps[i]
            return remote(total.at[pl.ds(away, size)], bit_slots[i], 1 + i, peer)

        def back_copy(i):
            _, keep, size, peer = steps[i]
            place = out.at[pl.ds(keep, size), :, mine]
            if i == total_bits - 1:
                return remote(total.at[pl.ds(keep, size)], place, 1 + total_bits + i, peer)
            return remote(place, place, 1 + total_bits + i, peer)

        def keep_copy():
            _, keep, size, _ = steps[-1]
            return pltpu.make_async_copy(
                total.at[pl.ds(keep, size)], out.at[pl.ds(keep, size), :, mine], copy_sem.at[sem]
            )

        def core_back():
            place = out.at[:, :, mine]
            return remote(place, place, 1 + 2 * total_bits, core_peer)

        def add(start, size, from_slot):
            @pl.loop(0, size)
            def _(j):
                total[start + j] = (total[start + j].astype(F32) + from_slot[j].astype(F32)).astype(BF)

        if step == 0:
            core_copy().start()
            own_copy().start()
        elif step == 1:
            own_copy().wait()
            core_copy().wait()
            add(0, pieces, core_slot)
            bit_copy(0).start()
        elif step <= total_bits + 1:
            i = step - 2
            bit_copy(i).wait()
            add(steps[i][1], steps[i][2], bit_slots[i])
            if step <= total_bits:
                bit_copy(i + 1).start()
            else:
                keep_copy().start()
                back_copy(i).start()
        elif step <= 2 * total_bits:
            i = 2 * total_bits + 1 - step
            if i == total_bits - 1:
                keep_copy().wait()
            back_copy(i).wait()
            back_copy(i - 1).start()
        elif step == 2 * total_bits + 1:
            back_copy(0).wait()
            core_back().start()
        else:
            core_back().wait()

    last = 2 * total_bits + 2

    offsets = [sum(lags[:step]) for step in range(last + 1)]

    def communicate(tick):
        for step in range(last, -1, -1):
            entry = tick - offsets[step] - 2
            chunk = entry - gap * (entry // (early + gap))

            @pl.when(
                ((entry >= 0) & (entry < early))
                | ((entry >= early + gap) & (entry < chunks + gap))
            )
            def _():
                block = chunk // subs
                stage(
                    step, lax.rem(chunk, 2) + lax.rem(chunk, 12) // 11 * 3, chunk,
                    lax.rem(chunk, subs) * 2 * acc.shape[-1],
                    staging.at[lax.rem(block, stages)], sum_ref.at[block], acc.at[chunk],
                    core_in.at[lax.rem(chunk, slots)], [ref.at[chunk] for ref in bit_in],
                )

            @pl.when(entry == chunks + gap)
            def _():
                stage(step, 0, chunks, 0, dsmall, ssum_ref, sacc, score_in, sbit_in)

    def place_block(block, value, cols):
        for i in range(pieces):
            staging[lax.rem(block, stages), i, :, cols] = value[
                i * piece_rows : (i + 1) * piece_rows
            ]

    tile = min(256, count)
    tiles = [slice(r, r + tile) for r in range(0, count, tile)]
    gain_one = par_ref[0:1, :]
    gain_two = par_ref[1:2, :]
    shift_two, scale_two, gate_one, gate_two = (part_of(mod_ref, i, width) for i in (3, 4, 2, 5))

    def prepare():
        total = 0.0
        for rows in tiles:
            a = dot(o_ref[rows, :], wout_ref[...], ((1,), (0,)))
            branch[rows, :] = a
            x1 = x_ref[rows, :].astype(F32) + gate_one * a
            middle[rows, :] = x1
            normed, _ = normed_rows(x1)
            h2 = (normed * (gain_two * (1.0 + scale_two)) + shift_two).astype(BF)
            normed_low[rows, :] = h2
            normed_t[:, rows] = h2.T
            dm_rows = (dy_ref[rows, :].astype(F32) * gate_two).astype(BF)
            dm[rows, :] = dm_rows
            total = total + jnp.sum(dm_rows.astype(F32), axis=0, keepdims=True)
        vec[5:6, :] = total

    def hidden_units(i, rows):
        slot = 2 * lax.rem(i, 2)
        if rows is tiles[0]:
            load_up(i, slot).wait()
            load_down(i, slot + 1).wait()
        bias = par_ref[pl.ds(9 + i, 1), :]
        u = dot(normed_low[rows, :], weights[slot], ((1,), (0,))) + bias
        square = u * u
        tanh = jnp.tanh(gelu_coeff * (u + 0.044715 * u * square))
        g = (0.5 * u * (1.0 + tanh)).astype(BF)
        active[rows, :] = g
        slope[rows, :] = 0.5 * (1.0 + tanh) + (0.5 * gelu_coeff) * u * (1.0 - tanh * tanh) * (
            1.0 + (3 * 0.044715) * square
        )
        part = dot(g, weights[slot + 1], ((1,), (0,)))

        @pl.when(i == 0)
        def _():
            total_a[rows, :] = part

        @pl.when(i > 0)
        def _():
            total_a[rows, :] += part

    def down_grads(i):
        for m in range(0, width, 256):
            cols = slice(m, m + 256)
            place_block(2 * i, dot(active[...], dm[:, cols], ((0,), (0,))).astype(BF), cols)

    def hidden_units_back(i, rows):
        slot = 2 * lax.rem(i, 2)
        dg = dot(dm[rows, :], weights[slot + 1], ((1,), (1,)))
        du = (dg * slope[rows, :]).astype(BF)
        active[rows, :] = du
        total = jnp.sum(du.astype(F32), axis=0, keepdims=True)
        part = dot(du, weights[slot], ((1,), (1,)))
        line = pl.ds(i, 1)
        if rows is tiles[0]:
            dup_bias[line, :] = total
        else:
            dup_bias[line, :] += total

        @pl.when(i == 0)
        def _():
            total_b[rows, :] = part

        @pl.when(i > 0)
        def _():
            total_b[rows, :] += part

    def up_grads(i):
        slot = 2 * lax.rem(i, 2)

        @pl.when(i + 2 < folds)
        def _():
            load_up(i + 2, slot).start()
            load_down(i + 2, slot + 1).start()

        @pl.when(i == folds - 1)
        def _():
            for n in range(3):
                load_qkv(n).start()

        for m in range(0, width, 256):
            cols = slice(m, m + 256)
            place_block(2 * i + 1, dot(normed_t[...], active[:, cols], ((1,), (0,))).astype(BF), cols)

    def close_hidden(rows):
        m = total_a[rows, :] + par_ref[2:3, :]
        x1 = middle[rows, :]
        out_rows[rows, :] = (x1 + gate_two * m).astype(BF)
        dy = dy_ref[rows, :].astype(F32)
        dh = total_b[rows, :]
        n2, rscale = normed_rows(x1)
        e = dh * ((1.0 + scale_two) * gain_two)
        dx1 = dy + rscale * (
            e
            - jnp.mean(e, axis=-1, keepdims=True)
            - n2 * jnp.mean(e * n2, axis=-1, keepdims=True)
        )
        middle[rows, :] = dx1
        da = (gate_one * dx1).astype(BF)
        normed_low[rows, :] = da
        for i, value in enumerate((dx1 * branch[rows, :], dh, dh * n2, dy * m)):
            total = jnp.sum(value, axis=0, keepdims=True)
            line = slice(i, i + 1)
            vec[line, :] = total if rows is tiles[0] else vec[line, :] + total
        active[rows, :] = dot(da, wout_ref[...], ((1,), (1,))).astype(BF)

    def out_grads():
        vec[4:5, :] = vec[2:3, :] * (1.0 + scale_two)
        vec[2:3, :] = vec[2:3, :] * gain_two
        for load in loads:
            load.wait()
        for m in range(0, width, 256):
            cols = slice(m, m + 256)
            place_block(
                2 * folds, dot(ot_ref[...], normed_low[:, cols], ((1,), (0,))).astype(BF), cols
            )
        row_send_all(out_rows, tokens_ref, 0)

    copies = count // 128
    lane = lax.broadcasted_iota(jnp.int32, (1, 128), 1)
    place = pl.ds(pl.multiple_of(core * count, count), count)

    def kv_copies(p):
        cols = pl.ds(pl.multiple_of(p * 128, 128), 128)
        return [
            pltpu.make_async_remote_copy(
                src_ref=away.at[:, cols],
                dst_ref=landing.at[:, cols],
                send_sem=kv_send.at[i, p],
                recv_sem=kv_recv.at[i, p],
                device_id=core_peer,
                device_id_type=MESH,
            )
            for i, (away, landing) in enumerate(((normed_low, dk_in), (dm, dv_in)))
        ]

    def attention(p, side):
        cols = pl.ds(pl.multiple_of(p * 128, 128), 128)
        q = q_ref[:, cols]
        do = active[:, cols]
        prod = ot_ref[cols, :].astype(F32) * do.astype(F32).T
        k_ref, v_ref, b_ref, dk_ref, dv_ref = (
            (kb_ref, vb_ref, bb_ref, normed_low, dm),
            (ka_ref, va_ref, ba_ref, total_a, total_b),
        )[side]
        k = k_ref[:, cols]
        v = v_ref[:, cols]
        k_t = k.T
        dk = dv = None
        for h in range(2):
            picked = (lane // HEAD) == h
            part = slice(h * HEAD, (h + 1) * HEAD)
            qm = jnp.where(picked, q, jnp.zeros_like(q))
            dom = jnp.where(picked, do, jnp.zeros_like(do))
            delta = jnp.sum(prod[part], axis=0, keepdims=True)
            s = dot(k, qm, ((1,), (1,))) + wide_of(b_ref[...], copies)
            prob = jnp.exp(s - lse_ref[p, h : h + 1, :])
            dv_h = dot(prob.astype(BF), dom, ((1,), (0,)))
            dprob = dot(v, dom, ((1,), (1,)))
            ds = (prob * (dprob - delta)).astype(BF)
            dk_h = dot(ds, qm, ((1,), (0,)))
            dq_h = dot(k_t[part], ds, ((1,), (0,)))
            dq_t[part, :] = dq_h if side == 0 else dq_t[part, :] + dq_h
            dk = dk_h if dk is None else dk + dk_h
            dv = dv_h if dv is None else dv + dv_h
        dk_ref[:, cols] = dk.astype(dk_ref.dtype)
        dv_ref[:, cols] = dv.astype(dv_ref.dtype)
        if side == 0:
            for copy in kv_copies(p):
                copy.start()
        else:
            dq = (dq_t[...] * (HEAD**-0.5)).T
            dqkv[:, cols] = rotate(dq, cos_ref[place, :], sin_ref[place, :], -1).astype(BF)

    def join():
        normed_t[...] = h_ref[...].T

        @pl.loop(0, pairs)
        def _(p):
            for copy in kv_copies(p):
                copy.wait()
            cols = pl.ds(pl.multiple_of(p * 128, 128), 128)
            dk = total_a[:, cols] + dk_in[:, cols].astype(F32)
            dv = total_b[:, cols] + dv_in[:, cols].astype(F32)
            k_cols = pl.ds(pl.multiple_of(width + p * 128, 128), 128)
            v_cols = pl.ds(pl.multiple_of(2 * width + p * 128, 128), 128)
            dqkv[:, k_cols] = rotate(dk, cos_ref[place, :], sin_ref[place, :], -1).astype(BF)
            dqkv[:, v_cols] = dv.astype(BF)

    def project_grads(n):
        for m in range(0, width, 256):
            cols = pl.ds(pl.multiple_of(n * width + m, 256), 256)
            place_block(
                2 * folds + 1 + n,
                dot(normed_t[...], dqkv[:, cols], ((1,), (0,))).astype(BF),
                slice(m, m + 256),
            )

    def finish(rows):
        if rows is tiles[0]:
            for n in range(3):
                load_qkv(n).wait()
        scale = 1.0 + part_of(mod_ref, 1, width)
        dh = sum(
            dot(dqkv[rows, n * width : (n + 1) * width], weights[n], ((1,), (1,)))
            for n in range(3)
        )
        n1, rscale = normed_rows(x_ref[rows, :].astype(F32))
        e = dh * (scale * gain_one)
        drows[rows, :] = (
            middle[rows, :]
            + rscale
            * (
                e
                - jnp.mean(e, axis=-1, keepdims=True)
                - n1 * jnp.mean(e * n1, axis=-1, keepdims=True)
            )
        ).astype(BF)
        for i, value in enumerate((dh, dh * n1)):
            total = jnp.sum(value, axis=0, keepdims=True)
            line = slice(6 + i, 7 + i)
            vec[line, :] = total if rows is tiles[0] else vec[line, :] + total

    def small_grads():
        row_send_all(drows, grad_ref, 1)
        scale = 1.0 + part_of(mod_ref, 1, width)
        srows = dsmall.shape[1]
        seqs = wide_size * groups
        seq = (wide // 2) * ring + chip
        line = lax.broadcasted_iota(jnp.int32, (pieces * srows, width), 0)
        cond = jnp.where(core == 0, cond_ref[...], 0.0)
        high = cond.astype(BF).astype(F32)
        medium = (cond - high).astype(BF).astype(F32)
        filler = jnp.zeros((1, width - 3 * TEMB), F32)
        entries = [
            (seq, vec[6:7, :]),
            (seqs + seq, vec[7:8, :] * gain_one),
            (2 * seqs + seq, vec[0:1, :]),
            (3 * seqs + seq, vec[1:2, :]),
            (4 * seqs + seq, vec[2:3, :]),
            (5 * seqs + seq, vec[3:4, :]),
            (6 * seqs + seq, jnp.concatenate([high, medium, cond - high - medium, filler], axis=1)),
            (7 * seqs, vec[7:8, :] * scale),
            (7 * seqs + 1, vec[4:5, :]),
            (7 * seqs + 2, vec[5:6, :]),
        ] + [(7 * seqs + 3 + i, dup_bias[i : i + 1, :]) for i in range(folds)]
        value = jnp.zeros((pieces * srows, width), F32)
        for at, entry in entries:
            value = jnp.where(line == at, entry, value)
        dsmall[...] = value.reshape(pieces, srows, width).astype(BF)

    prepare()
    join_at = 6 * folds + 3 + 2 * pairs
    units = []
    for n in range(2):
        for t, rows in enumerate(tiles):
            units.append((n * 3 + t, (hidden_units, hidden_units_back)[n], rows))
        units.append((n * 3 + 2, (down_grads, up_grads)[n], None))

    @pl.loop(0, chunks + gap + 3 + offsets[-1])
    def _(tick):
        for at, unit, rows in units:

            @pl.when((tick < 6 * folds) & (lax.rem(tick, 6) == at))
            def _():
                unit(tick // 6, *(() if rows is None else (rows,)))

        for t, rows in enumerate(tiles):

            @pl.when(tick == 6 * folds + t)
            def _():
                close_hidden(rows)

            @pl.when(tick == join_at + 2 + t)
            def _():
                finish(rows)

        @pl.when(tick == 6 * folds + 2)
        def _():
            out_grads()

        for side in range(2):

            @pl.when(
                (tick >= 6 * folds + 3)
                & (tick < 6 * folds + 3 + 2 * pairs)
                & (lax.rem(tick - (6 * folds + 3), 2) == side)
            )
            def _():
                attention((tick - (6 * folds + 3)) // 2, side)

        @pl.when(tick == join_at)
        def _():
            join()

        for n in range(3):

            @pl.when(tick == join_at + 1 + subs * n)
            def _():
                project_grads(n)

        @pl.when(tick == join_at + subs + 2)
        def _():
            small_grads()

        communicate(tick)

    row_wait_all(out_rows, tokens_ref, 0)
    row_wait_all(drows, grad_ref, 1)


def rest_of_block(
    x, o, ot, dy, mod, params, cosines, sines, cond, lse, wout, q, ka, va, kb, vb, h, ba, bb,
    up, down, wqkv, groups, wide_size, ring,
    lags=(3, 6, 5, 3),
):
    count, width = x.shape
    pieces = wide_size // 2 * ring
    rows = width // pieces
    half = width // 2
    sub_half = 128
    folds = up.shape[1] // width
    subs = width // 256
    blocks = 2 * folds + 4
    chunks = blocks * subs
    pairs = width // 128
    total_bits = pieces.bit_length() - 1
    first = list(lags[:3]) + [lags[3]] * (total_bits - 2)
    lags = first + first[::-1]
    assert subs * 256 == width and subs == 3
    seqs = wide_size * groups
    srows = -(-(seqs * 7 + 3 + folds) // (pieces * 8)) * 8
    sizes = [pieces >> (i + 1) for i in range(total_bits)]
    any_space = pl.BlockSpec(memory_space=pl.ANY)
    vmem = pl.BlockSpec(memory_space=pltpu.VMEM)
    block = jax.ShapeDtypeStruct((groups, count // groups, width), BF)
    rows_low = pltpu.VMEM((count, width), BF)
    rows_full = pltpu.VMEM((count, width), F32)
    lanes = pltpu.VMEM((count, 128), F32)
    return pl.pallas_call(
        functools.partial(rest_kernel, groups, wide_size, ring, tuple(lags)),
        in_specs=[vmem] * 11 + [any_space] * 11,
        out_specs=[any_space] * 4,
        out_shape=[
            jax.ShapeDtypeStruct((blocks, pieces, rows, width), BF),
            jax.ShapeDtypeStruct((pieces, srows, width), BF),
            block,
            block,
        ],
        scratch_shapes=[rows_low] * 6
        + [lanes] * 2
        + [
            pltpu.VMEM((4, width, width), BF),
            pltpu.VMEM((4, pieces, rows, width), BF),
            pltpu.VMEM((pieces, srows, width), BF),
            rows_full,
            rows_full,
            rows_low,
            pltpu.VMEM((width, count), BF),
            rows_low,
            rows_full,
            rows_full,
            rows_low,
            rows_full,
            pltpu.VMEM((128, count), F32),
            pltpu.VMEM((8, width), F32),
            pltpu.VMEM((8, width), F32),
            rows_low,
            rows_low,
            pltpu.VMEM((count, 3 * width), BF),
            rows_low,
            rows_low,
            pltpu.VMEM((chunks, pieces, rows, sub_half), BF),
            pltpu.VMEM((pieces, srows, half), BF),
            pltpu.VMEM((2 * lags[0] + 1, pieces, rows, sub_half), BF),
            pltpu.VMEM((pieces, srows, half), BF),
            [pltpu.VMEM((chunks, n, rows, sub_half), BF) for n in sizes],
            [pltpu.VMEM((n, srows, half), BF) for n in sizes],
            DMA((8,)),
            DMA((4,)),
            DMA((chunks + 1,)),
            DMA((2 + 2 * total_bits, chunks + 1)),
            DMA((2 + 2 * total_bits, chunks + 1)),
            DMA((2, pairs)),
            DMA((2, pairs)),
            DMA((2,)),
            DMA((2, groups)),
            DMA((2, groups)),
        ],
        compiler_params=pltpu.CompilerParams(
            collective_id=0, has_side_effects=True, vmem_limit_bytes=63 << 20
        ),
        name="rest_of_block",
    )(
        x, o, ot, dy, mod, params, cosines, sines, cond, lse, wout, q, ka, va, kb, vb, h, ba, bb,
        up, down, wqkv,
    )


def spread_kernel(seqs, folds, sum_ref, small_ref, ada_ref, qkv_ref, out_ref, up_ref, down_ref,
                  ada_bias_ref, gain_one_ref, gain_two_ref, up_bias_ref, down_bias_ref):
    i = pl.program_id(0)
    width = sum_ref.shape[-1]
    value = sum_ref[0].astype(F32)

    @pl.when(i < folds)
    def _():
        down_ref[...] = value

    @pl.when((i >= folds) & (i < 2 * folds))
    def _():
        up_ref[...] = value

    @pl.when(i == 2 * folds)
    def _():
        out_ref[...] = value

    @pl.when(i > 2 * folds)
    def _():
        qkv_ref[...] = value

    @pl.when(i == 0)
    def _():
        cond = small_ref[6 * seqs : 7 * seqs, : 3 * TEMB]
        for n in range(6):
            mod = small_ref[n * seqs : (n + 1) * seqs, :]
            three = dot(mod, cond, ((0,), (0,)))
            ada_ref[n * width : (n + 1) * width, :] = (
                three[:, :TEMB] + three[:, TEMB : 2 * TEMB] + three[:, 2 * TEMB :]
            )
            ada_bias_ref[n * width : (n + 1) * width] = jnp.sum(mod.astype(F32), axis=0)
        rows = small_ref[7 * seqs : 7 * seqs + 8 * (-(-(3 + folds) // 8)), :].astype(F32)
        gain_one_ref[...] = rows[0]
        gain_two_ref[...] = rows[1]
        down_bias_ref[...] = rows[2]
        for n in range(folds):
            up_bias_ref[n * width : (n + 1) * width] = rows[3 + n]


def spread(summed, small, seqs, folds):
    chunks, width = summed.shape[0], summed.shape[-1]

    def fixed(shape):
        return pl.BlockSpec(shape, lambda i: (0,) * len(shape))

    def chunk(i):
        hidden = 2 * (i % folds) + i // folds
        return jnp.where(i < 2 * folds, hidden, i)

    def at(first, size, axis):
        def index(i):
            block = jnp.clip(i - first, 0, size - 1)
            return (block, 0) if axis == 0 else (0, block)

        return pl.BlockSpec((width, width), index)

    vectors = [(6 * width,), (width,), (width,), (folds * width,), (width,)]
    return pl.pallas_call(
        functools.partial(spread_kernel, seqs, folds),
        grid=(chunks,),
        in_specs=[pl.BlockSpec((1, width, width), lambda i: (chunk(i), 0, 0)), fixed(small.shape)],
        out_specs=[
            fixed((6 * width, TEMB)),
            at(2 * folds + 1, 3, 1),
            fixed((width, width)),
            at(folds, folds, 1),
            at(0, folds, 0),
        ]
        + [fixed(shape) for shape in vectors],
        out_shape=[
            jax.ShapeDtypeStruct(shape, F32)
            for shape in [
                (6 * width, TEMB), (width, 3 * width), (width, width), (width, folds * width),
                (folds * width, width),
            ]
            + vectors
        ],
        compiler_params=pltpu.CompilerParams(vmem_limit_bytes=56 << 20),
        name="spread",
    )(summed, small)


def local(
    tokens, step_ids, prefix, keep_bits, ada_weight, ada_bias, norm1_gain, qkv_weight, out_weight,
    norm2_gain, up_weight, up_bias, down_weight, down_bias, cotangent,
):
    wide_size = lax.axis_size("wide")
    ring = lax.axis_size("narrow")
    groups, span, width = tokens.shape
    assert ring == 2 * groups and wide_size % 2 == 0
    length = ring * span
    hidden = up_weight.shape[1]
    folds = hidden // width
    seqs = wide_size * groups

    allowed = (jnp.arange(length, dtype=jnp.int32)[None, :] < prefix[:, None]) | (keep_bits == 1)
    info = jnp.concatenate(
        [jax.nn.silu(time_embed(step_ids)), jnp.where(allowed, 0.0, masked_score)], axis=1
    )[:, None, :]
    params = jnp.concatenate([norm1_gain, norm2_gain, down_bias, ada_bias, up_bias]).reshape(
        -1, width
    )
    cosines, sines = rope_tables(length)
    x, dy, h, q, ka, va, kb, vb, o, ot, lse, mod, ba, bb, cond = front(
        tokens, cotangent, qkv_weight, ada_weight, info, params, cosines, sines, ring
    )
    summed, small, outputs, input_grad = rest_of_block(
        x, o, ot, dy, mod, params, cosines, sines, cond, lse, out_weight, q, ka, va, kb, vb, h,
        ba, bb, up_weight, down_weight, qkv_weight, groups, wide_size, ring,
    )
    ada, qkv, out, up, down, ada_bias_grad, gain_one, gain_two, up_bias_grad, down_bias_grad = (
        spread(summed.reshape(-1, width, width), small.reshape(-1, width), seqs, folds)
    )
    return (
        outputs, input_grad, ada, ada_bias_grad, gain_one, qkv, out, gain_two, up, up_bias_grad,
        down, down_bias_grad,
    )


def solution(mesh):
    split = P("wide", "narrow", None)
    in_specs = (
        (split, P("wide"), P("wide"), P("wide", None)) + (P(),) * 10 + (split,)
    )
    out_specs = (split, split) + (P(),) * 10
    return jax.shard_map(local, mesh=mesh, in_specs=in_specs, out_specs=out_specs, check_vma=False)
```

time: 289 us -> 268 us (0.927)
  other arithmetic: 18.9 us -> 1.66 us
  local copies, waits for them, and re-layouts: 18.8 us -> 6.53 us
  Pallas kernels: 247 us -> 258 us
    convert_element_type x6 -> x0, other arithmetic: 15 us -> none  [the longest x2 7.51 us: untile(): jnp.concatenate([array[i] for i in range(array.shape[0])], axis=1)]
    pallas_call x2, Pallas kernels: 207 us -> 218 us  [the longest x1 197 us: rest_of_block(): pl.pallas_call(functools.partial(rest_kernel, groups, wide_size, ring, tu...]
    slice x6 -> x0, local copies, waits for them, and re-layouts: 9.26 us -> none  [the longest x1 4.13 us: untile(): array[i]]
    broadcast_in_dim x4 -> x0, local copies, waits for them, and re-layouts: 5.16 us -> none  [the longest x1 1.35 us: local(): ada_bias[None]]
where the time goes in v3:
time: 268 us; the launch traced here: 267 us
  Pallas kernels  258 us (96%)
  local copies, waits for them, and re-layouts  6.53 us (2%)
    pallas_call x1, Pallas kernels, rest_of_block(): pl.pallas_call(functools.partial(rest_kernel, groups, wide_size, ring, tu...  197 us
    pallas_call x1, Pallas kernels, front(): pl.pallas_call(functools.partial(front_kernel, groups, ring), in_specs=[a...  39.9 us
    pallas_call x1, Pallas kernels, spread(): pl.pallas_call(functools.partial(spread_kernel, seqs, folds), grid=(chunk...  20.7 us

profile of v3, /device:TPU:1, one launch (start us, length us, event | category | flops | bytes accessed | tf_op | source)
XLA Modules:
  0.0 266.8 jit_solution(1536082637846089996)
XLA Ops:
  0.6 0.7 convert_element_type.3
  1.3 0.1 multiply_cosine_fusion
  1.4 0.1 divide_multiply_fusion
  1.5 0.8 or_select_fusion
  2.3 0.6 broadcast_in_dim.17.info_ref
  2.9 0.7 constant_dynamic-update-slice_fusion.4
  3.6 0.7 constant_dynamic-update-slice_fusion.3
  4.3 0.7 constant_dynamic-update-slice_fusion.2
  5.0 0.7 constant_dynamic-update-slice_fusion.1
  5.7 0.7 constant_dynamic-update-slice_fusion
  6.4 0.6 reshape.40.par_ref
  7.1 39.9 %front.1 = (bf16[512,768]{1,0:T(8,128)(2,1)}, bf16[512,768]{1,0:T(8,128)(2,1)}, bf16[512,768]{1,0:T(8,128)(2,1)}, bf16[512,768]{1,0:T(8,128)(2,1)}, bf16[512,768...) custom-call(bf16[2,256,768]{2,1,0:T(8,128)(2,1)} %tok_ref.1, ...), custom_call_target="tpu_custom_call" | custom-call | tf_op jit(solution)/shard_map/front/pallas_call | solution.py:275
  47.0 197.3 %rest_of_block.1 = (bf16[12,16,48,768]{3,2,1,0:T(8,128)(2,1)}, bf16[16,8,768]{2,1,0:T(8,128)(2,1)}, bf16[2,256,768]{2,1,0:T(8,128)(2,1)}, bf16[2,256,768]{2,1,0:T(8,128)(2,1)}) custom-call(bf16[512,768]{1,0:T(8,128)(2,1)} %get-tuple-element.41.x_ref, bf16[512,768]{1,0:T(8,128)(2,1)} %get-tuple-element.42.o_ref, bf16[768,512]{1,0:T(8,128)(2,1)} %get-tuple-element.43.ot_ref, ...), custom_call_target="tpu_custom_call" | custom-call | tf_op jit(solution)/shard_map/rest_of_block/pallas_call | solution.py:910
  244.3 0.0 copy-start.1
  244.3 0.0 copy-start
  244.3 20.7 %spread.1 = (f32[4608,128]{1,0:T(8,128)}, f32[768,2304]{1,0:T(8,128)}, f32[768,768]{1,0:T(8,128)}, f32[768,3072]{1,0:T(8,128)}, f32[3072,768]{1,0:T(8,128)}, /*i...) custom-call(bf16[12,768,768]{2,1,0:T(8,128)(2,1)} %bitcast.2, bf16[128,768]{1,0:T(8,128)(2,1)} %bitcast.3), custom_call_target="tpu_custom_call" | custom-call | tf_op jit(solution)/shard_map/spread/pallas_call | solution.py:1028
  265.0 0.0 copy-done.1
  265.0 0.9 copy.36
  265.9 0.0 copy-done
  265.9 0.9 copy.37
  (3 shorter events, 0.0 us)
Async XLA Ops:
  244.3 20.7 %copy-start.1 = (bf16[2,256,768]{2,1,0:T(8,128)(2,1)S(1)}, bf16[2,256,768]{2,1,0:T(8,128)(2,1)}, u32[]{:S(2)}) copy-start(bf16[2,256,768]{2,1,0:T(8,128)(2,1)} %get-tuple-element.84) | copy-start | bytes 2359300
  244.3 21.6 %copy-start = (bf16[2,256,768]{2,1,0:T(8,128)(2,1)S(1)}, bf16[2,256,768]{2,1,0:T(8,128)(2,1)}, u32[]{:S(2)}) copy-start(bf16[2,256,768]{2,1,0:T(8,128)(2,1)} %get-tuple-element.85) | copy-start | bytes 2359300

commit v4 on v3

--- a/solution.py
+++ b/solution.py
@@ -70,50 +70,100 @@
     return jnp.concatenate([block] * copies, axis=1)
 
 
-def front_kernel(
-    groups, ring,
-    tok_ref, cot_ref, wqkv_ref, ada_ref, info_ref, par_ref, cos_ref, sin_ref,
-    x_ref, dy_ref, h_ref, q_ref, ka_ref, va_ref, kb_ref, vb_ref, o_ref, ot_ref, lse_ref,
-    mod_ref, ba_ref, bb_ref, cond_ref,
-    wqkv, ada, table,
-    load_sem, self_sem, info_send, info_recv, send_sem, recv_sem, kv_send, kv_recv,
+def block_kernel(
+    groups, wide_size, ring, lags,
+    tok_ref, cot_ref, wqkv_ref, ada_ref, wout_ref, up_ref, down_ref,
+    info_ref, gain_one_ref, gain_two_ref, down_bias_ref, ada_bias_ref, up_bias_ref, cos_ref,
+    sin_ref,
+    sum_ref, ssum_ref, tokens_ref, grad_ref,
+    x_ref, dy_ref, h_ref, q_ref, ka_ref, va_ref, kb_ref, vb_ref, o_ref, ot_ref, lse_ref, mod_ref,
+    ba_ref, bb_ref, cond_ref, table, par_ref, wout,
+    weights, staging, dsmall, middle, branch, normed_low, normed_t, dm, total_a, total_b, active,
+    slope, dq_t, deltas, vec, dup_bias, out_rows, drows, dqkv, dk_in, dv_in,
+    acc, sacc, core_in, score_in, bit_in, sbit_in,
+    load_sem, weight_sem, take_self, info_send, info_recv, take_send, take_recv, swap_send,
+    swap_recv, copy_sem, send_sem, recv_sem, kv_send, kv_recv, self_sem, row_send, row_recv,
 ):
-    span, width = tok_ref.shape[1:]
-    count = groups * span
+    chunks, pieces, piece_rows = acc.shape[:3]
+    slots = core_in.shape[0]
+    stages = staging.shape[0]
+    outer = (wide_size // 2).bit_length() - 1
+    inner = ring.bit_length() - 1
+    total_bits = outer + inner
+    count, width = x_ref.shape
+    subs = width // (2 * acc.shape[-1])
+    span = count // groups
+    pairs = width // 128
+    folds = up_ref.shape[1] // width
+    early = (2 * folds + 1) * subs
     wide = lax.axis_index("wide")
     chip = lax.axis_index("narrow")
     core = lax.rem(wide, 2)
     base = wide - core
-    peer = (base + 1 - core, chip)
-
-    load_w = pltpu.make_async_copy(wqkv_ref, wqkv, load_sem.at[0])
-    load_a = pltpu.make_async_copy(ada_ref, ada, load_sem.at[1])
-    load_a.start()
-    load_w.start()
+    core_peer = (base + 1 - core, chip)
+    dims = []
+    for b in range(outer):
+        bit = lax.rem(wide // (2 << b), 2)
+        dims.append((bit, wide + (1 - 2 * bit) * (2 << b), chip))
+    for b in range(inner):
+        bit = lax.rem(chip // (1 << b), 2)
+        dims.append((bit, wide, chip + (1 - 2 * bit) * (1 << b)))
+    up = list(range(outer))
+    rest = list(range(outer, total_bits))
+    orders = (up + rest, up[::-1] + rest, rest + up)
+
+    def load_up(i, slot):
+        cols = pl.ds(pl.multiple_of(i * width, width), width)
+        return pltpu.make_async_copy(up_ref.at[:, cols], weights.at[slot], weight_sem.at[slot])
+
+    def load_down(i, slot):
+        rows = pl.ds(pl.multiple_of(i * width, width), width)
+        return pltpu.make_async_copy(down_ref.at[rows], weights.at[slot], weight_sem.at[slot])
+
+    def load_qkv(n):
+        cols = pl.ds(n * width, width)
+        return pltpu.make_async_copy(wqkv_ref.at[:, cols], weights.at[n], weight_sem.at[n])
+
+    load_ada = [
+        pltpu.make_async_copy(
+            ada_ref.at[pl.ds(n * width, width)],
+            weights.at[3, :, pl.ds(n * TEMB, TEMB)],
+            load_sem.at[1 + n],
+        )
+        for n in range(6)
+    ]
+    load_out = pltpu.make_async_copy(wout_ref, wout, load_sem.at[0])
 
     barrier = pltpu.get_barrier_semaphore()
+    for d in dims[:outer]:
+        pl.semaphore_signal(barrier, inc=1, device_id=d[1:], device_id_type=MESH)
     for c in range(2):
         for d in range(ring):
             if c or d:
                 other = (base + lax.rem(core + c, 2), lax.rem(chip + d, ring))
                 pl.semaphore_signal(barrier, inc=1, device_id=other, device_id_type=MESH)
-    pl.semaphore_wait(barrier, 2 * ring - 1)
+    for load in load_ada:
+        load.start()
+    for n in range(3):
+        load_qkv(n).start()
+    load_out.start()
+    pl.semaphore_wait(barrier, outer + 2 * ring - 1)
 
     slot = lax.rem(chip, groups)
-    to_core = chip // groups
+    home = chip // groups
     rows_out = pl.ds(pl.multiple_of(slot * span, span), span)
 
     def move(src, dst, kind, g):
         remote = pltpu.make_async_remote_copy(
             src_ref=src.at[g],
             dst_ref=dst.at[rows_out],
-            send_sem=send_sem.at[kind, g],
-            recv_sem=recv_sem.at[kind, slot],
-            device_id=(base + to_core, core * groups + g),
+            send_sem=take_send.at[kind, g],
+            recv_sem=take_recv.at[kind, slot],
+            device_id=(base + home, core * groups + g),
             device_id_type=MESH,
         )
-        here = pltpu.make_async_copy(src.at[g], dst.at[rows_out], self_sem.at[kind])
-        own = (to_core == core) & (slot == g)
+        here = pltpu.make_async_copy(src.at[g], dst.at[rows_out], take_self.at[kind])
+        own = (home == core) & (slot == g)
         return remote, here, own
 
     def send(src, dst, kind):
@@ -138,36 +188,43 @@
 
     def arrive(src, dst, kind, j):
         rows = pl.ds(j * span, span)
-        own = (to_core == core) & (slot == j)
+        own = (home == core) & (slot == j)
 
         @pl.when(own)
         def _():
-            pltpu.make_async_copy(src.at[0], dst.at[rows], self_sem.at[kind]).wait()
+            pltpu.make_async_copy(src.at[0], dst.at[rows], take_self.at[kind]).wait()
 
         @pl.when(jnp.logical_not(own))
         def _():
             pltpu.make_async_remote_copy(
                 src_ref=src.at[0],
                 dst_ref=dst.at[rows],
-                send_sem=send_sem.at[kind, 0],
-                recv_sem=recv_sem.at[kind, j],
-                device_id=peer,
+                send_sem=take_send.at[kind, 0],
+                recv_sem=take_recv.at[kind, j],
+                device_id=core_peer,
                 device_id_type=MESH,
             ).wait_recv()
 
     send(tok_ref, x_ref, 0)
+    par_ref[0:1, :] = gain_one_ref[...].reshape(1, width)
+    par_ref[1:2, :] = gain_two_ref[...].reshape(1, width)
+    par_ref[2:3, :] = down_bias_ref[...].reshape(1, width)
+    for i in range(6):
+        par_ref[3 + i : 4 + i, :] = ada_bias_ref[i * width : (i + 1) * width].reshape(1, width)
+    for i in range(folds):
+        par_ref[9 + i : 10 + i, :] = up_bias_ref[i * width : (i + 1) * width].reshape(1, width)
     table[core] = info_ref[...]
     swap_info = pltpu.make_async_remote_copy(
         src_ref=info_ref,
         dst_ref=table.at[core],
         send_sem=info_send,
         recv_sem=info_recv,
-        device_id=peer,
+        device_id=core_peer,
         device_id_type=MESH,
     )
     swap_info.start()
     swap_info.wait()
-    row = table[chip // groups, lax.rem(chip, groups)]
+    row = table[home, pl.ds(slot, 1), :]
     length = row.shape[1] - TEMB
     cond_ref[...] = row[:, :TEMB]
     bias = jnp.where(core == 0, row[:, TEMB : TEMB + count], row[:, TEMB + count : TEMB + length])
@@ -177,23 +234,25 @@
 
     cond = jnp.broadcast_to(row[:, :TEMB], (16, TEMB))
     high = cond.astype(BF).astype(F32)
-    middle = (cond - high).astype(BF).astype(F32)
-    low = cond - high - middle
+    medium = (cond - high).astype(BF).astype(F32)
+    low = cond - high - medium
     line = lax.broadcasted_iota(jnp.int32, (16, TEMB), 0)
     three = jnp.where(
-        line == 0, high, jnp.where(line == 1, middle, jnp.where(line == 2, low, 0.0))
+        line == 0, high, jnp.where(line == 1, medium, jnp.where(line == 2, low, 0.0))
     ).astype(BF)
-    load_a.wait()
+    for load in load_ada:
+        load.wait()
     for i in range(6):
         cols = slice(i * width, (i + 1) * width)
         mod_ref[:, cols] = (
-            jnp.sum(dot(three, ada[cols, :], ((1,), (1,))), axis=0, keepdims=True)
+            jnp.sum(dot(three, weights[3, :, i * TEMB : (i + 1) * TEMB], ((1,), (1,))), axis=0, keepdims=True)
             + par_ref[3 + i : 4 + i, :]
         )
     shift = part_of(mod_ref, 0, width)
     scale = par_ref[0:1, :] * (1.0 + part_of(mod_ref, 1, width))
 
-    load_w.wait()
+    for n in range(3):
+        load_qkv(n).wait()
     swaps = []
     for j in range(groups):
         rows = pl.ds(j * span, span)
@@ -209,8 +268,8 @@
         for n in (2, 1, 0):
             target = (q_ref, ka_ref, va_ref)[n]
             for m in range(width // step):
-                cols = pl.ds(n * width + m * step, step)
-                block = dot(h_ref[rows, :], wqkv[:, cols], ((1,), (0,)))
+                cols = slice(m * step, (m + 1) * step)
+                block = dot(h_ref[rows, :], weights[n, :, cols], ((1,), (0,)))
                 if n < 2:
                     block = rotate(block, cosines, sines, 1)
                 if n == 0:
@@ -220,13 +279,16 @@
                 swap = pltpu.make_async_remote_copy(
                     src_ref=target.at[rows],
                     dst_ref=(kb_ref, vb_ref)[n - 1].at[rows],
-                    send_sem=kv_send.at[n - 1, j],
-                    recv_sem=kv_recv.at[n - 1, j],
-                    device_id=peer,
+                    send_sem=swap_send.at[n - 1, j],
+                    recv_sem=swap_recv.at[n - 1, j],
+                    device_id=core_peer,
                     device_id_type=MESH,
                 )
                 swap.start()
                 swaps.append(swap)
+    for i in range(2):
+        load_up(i, 2 * i).start()
+        load_down(i, 2 * i + 1).start()
     for swap in swaps:
         swap.wait()
 
@@ -263,145 +325,29 @@
     sent(tok_ref, x_ref, 0)
     for j in range(groups):
         arrive(cot_ref, dy_ref, 1, j)
-    sent(cot_ref, dy_ref, 1)
-
-
-def front(tokens, cotangent, wqkv, ada, info, params, cosines, sines, ring):
-    groups, span, width = tokens.shape
-    count = groups * span
-    any_space = pl.BlockSpec(memory_space=pl.ANY)
-    vmem = pl.BlockSpec(memory_space=pltpu.VMEM)
-    rows = jax.ShapeDtypeStruct((count, width), BF)
-    return pl.pallas_call(
-        functools.partial(front_kernel, groups, ring),
-        in_specs=[any_space] * 4 + [vmem] * 4,
-        out_specs=[vmem] * 15,
-        out_shape=[rows] * 9
-        + [
-            jax.ShapeDtypeStruct((width, count), BF),
-            jax.ShapeDtypeStruct((width // 128, 8, count), F32),
-            jax.ShapeDtypeStruct((1, 6 * width), F32),
-            jax.ShapeDtypeStruct((count, 128), F32),
-            jax.ShapeDtypeStruct((count, 128), F32),
-            jax.ShapeDtypeStruct((1, TEMB), F32),
-        ],
-        scratch_shapes=[
-            pltpu.VMEM(wqkv.shape, BF),
-            pltpu.VMEM(ada.shape, BF),
-            pltpu.VMEM((2,) + info.shape, F32),
-            DMA((2,)),
-            DMA((2,)),
-            DMA,
-            DMA,
-            DMA((2, groups)),
-            DMA((2, groups)),
-            DMA((2, groups)),
-            DMA((2, groups)),
-        ],
-        compiler_params=pltpu.CompilerParams(
-            collective_id=1, has_side_effects=True, vmem_limit_bytes=56 << 20
-        ),
-        name="front",
-    )(tokens, cotangent, wqkv, ada, info, params, cosines, sines)
-
-
-def rest_kernel(
-    groups, wide_size, ring, lags,
-    x_ref, o_ref, ot_ref, dy_ref, mod_ref, par_ref, cos_ref, sin_ref, cond_ref, lse_ref, wout_ref,
-    q_in, ka_in, va_in, kb_in, vb_in, h_in, ba_in, bb_in, up_ref, down_ref, wqkv_ref,
-    sum_ref, ssum_ref, tokens_ref, grad_ref,
-    q_ref, ka_ref, va_ref, kb_ref, vb_ref, h_ref, ba_ref, bb_ref,
-    weights, staging, dsmall, middle, branch, normed_low, normed_t, dm, total_a, total_b, active,
-    slope, dq_t, vec, dup_bias, out_rows, drows, dqkv, dk_in, dv_in,
-    acc, sacc, core_in, score_in, bit_in, sbit_in,
-    load_sem, weight_sem, copy_sem, send_sem, recv_sem, kv_send, kv_recv, self_sem, row_send,
-    row_recv,
-):
-    chunks, pieces, piece_rows = acc.shape[:3]
-    slots = core_in.shape[0]
-    subs = x_ref.shape[1] // (2 * acc.shape[-1])
-    stages = staging.shape[0]
-    outer = (wide_size // 2).bit_length() - 1
-    inner = ring.bit_length() - 1
-    total_bits = outer + inner
-    count, width = x_ref.shape
-    span = count // groups
-    pairs = width // 128
-    folds = up_ref.shape[1] // width
-    early = (2 * folds + 1) * subs
-    gap = 2 * pairs - subs + 2
-    wide = lax.axis_index("wide")
-    chip = lax.axis_index("narrow")
-    core = lax.rem(wide, 2)
-    base = wide - core
-    core_peer = (base + 1 - core, chip)
-    dims = []
-    for b in range(outer):
-        bit = lax.rem(wide // (2 << b), 2)
-        dims.append((bit, wide + (1 - 2 * bit) * (2 << b), chip))
-    for b in range(inner):
-        bit = lax.rem(chip // (1 << b), 2)
-        dims.append((bit, wide, chip + (1 - 2 * bit) * (1 << b)))
-    up = list(range(outer))
-    rest = list(range(outer, total_bits))
-    orders = (up + rest, up[::-1] + rest, rest + up)
-
-    def load_up(i, slot):
-        cols = pl.ds(pl.multiple_of(i * width, width), width)
-        return pltpu.make_async_copy(up_ref.at[:, cols], weights.at[slot], weight_sem.at[slot])
-
-    def load_down(i, slot):
-        rows = pl.ds(pl.multiple_of(i * width, width), width)
-        return pltpu.make_async_copy(down_ref.at[rows], weights.at[slot], weight_sem.at[slot])
-
-    def load_qkv(n):
-        cols = pl.ds(n * width, width)
-        return pltpu.make_async_copy(wqkv_ref.at[:, cols], weights.at[n], weight_sem.at[n])
-
-    for i in range(2):
-        load_up(i, 2 * i).start()
-        load_down(i, 2 * i + 1).start()
-    loads = [
-        pltpu.make_async_copy(src, dst, load_sem.at[i])
-        for i, (src, dst) in enumerate(
-            (
-                (q_in, q_ref), (ka_in, ka_ref), (va_in, va_ref), (kb_in, kb_ref), (vb_in, vb_ref),
-                (h_in, h_ref), (ba_in, ba_ref), (bb_in, bb_ref),
-            )
-        )
-    ]
-    for load in loads:
-        load.start()
-    barrier = pltpu.get_barrier_semaphore()
-    for d in dims[:outer]:
-        pl.semaphore_signal(barrier, inc=1, device_id=d[1:], device_id_type=MESH)
-    for c in range(2):
-        for d in range(ring):
-            if c or d:
-                other = (base + lax.rem(core + c, 2), lax.rem(chip + d, ring))
-                pl.semaphore_signal(barrier, inc=1, device_id=other, device_id_type=MESH)
-    pl.semaphore_wait(barrier, outer + 2 * ring - 1)
-
-    slot = lax.rem(chip, groups)
-    home = chip // groups
-
-    def row_move(src, dst, kind, j):
-        rows = pl.ds(j * span, span)
+    load_out.wait()
+
+    parts = 8
+    part_rows = span // parts
+
+    def row_move(src, dst, kind, j, q):
+        rows = pl.ds(pl.multiple_of(j * span + q * part_rows, part_rows), part_rows)
+        place = dst.at[slot, pl.ds(pl.multiple_of(q * part_rows, part_rows), part_rows)]
         remote = pltpu.make_async_remote_copy(
             src_ref=src.at[rows],
-            dst_ref=dst.at[slot],
-            send_sem=row_send.at[kind, j],
-            recv_sem=row_recv.at[kind, slot],
+            dst_ref=place,
+            send_sem=row_send.at[kind, j, q],
+            recv_sem=row_recv.at[kind, slot, q],
             device_id=(base + home, core * groups + j),
             device_id_type=MESH,
         )
-        here = pltpu.make_async_copy(src.at[rows], dst.at[slot], self_sem.at[kind])
+        here = pltpu.make_async_copy(src.at[rows], place, self_sem.at[kind, q])
         own = (home == core) & (slot == j)
         return remote, here, own
 
-    def row_send_all(src, dst, kind):
+    def row_send_part(src, dst, kind, q):
         for j in range(groups):
-            remote, here, own = row_move(src, dst, kind, j)
+            remote, here, own = row_move(src, dst, kind, j, q)
 
             @pl.when(own)
             def _():
@@ -411,9 +357,9 @@
             def _():
                 remote.start()
 
-    def row_wait_all(src, dst, kind):
+    def row_wait_part(src, dst, kind, q):
         for j in range(groups):
-            remote, here, own = row_move(src, dst, kind, j)
+            remote, here, own = row_move(src, dst, kind, j, q)
 
             @pl.when(own)
             def _():
@@ -423,16 +369,17 @@
             def _():
                 remote.wait_send()
 
+        rows = pl.ds(pl.multiple_of(q * part_rows, part_rows), part_rows)
         for g in range(groups):
             own = (home == core) & (slot == g)
 
             @pl.when(jnp.logical_not(own))
             def _():
                 pltpu.make_async_remote_copy(
-                    src_ref=src.at[pl.ds(0, span)],
-                    dst_ref=dst.at[g],
-                    send_sem=row_send.at[kind, 0],
-                    recv_sem=row_recv.at[kind, g],
+                    src_ref=src.at[rows],
+                    dst_ref=dst.at[g, rows],
+                    send_sem=row_send.at[kind, 0, q],
+                    recv_sem=row_recv.at[kind, g, q],
                     device_id=core_peer,
                     device_id_type=MESH,
                 ).wait_recv()
@@ -532,28 +479,37 @@
             core_back().wait()
 
     last = 2 * total_bits + 2
-
     offsets = [sum(lags[:step]) for step in range(last + 1)]
+    turn = 2 * (pairs // subs) + subs
+    lead = 6 * folds + 3
+    late = lead + turn - 2
+    closing = lead + subs * turn + 1
 
     def communicate(tick):
         for step in range(last, -1, -1):
-            entry = tick - offsets[step] - 2
-            chunk = entry - gap * (entry // (early + gap))
-
-            @pl.when(
-                ((entry >= 0) & (entry < early))
-                | ((entry >= early + gap) & (entry < chunks + gap))
-            )
-            def _():
-                block = chunk // subs
+            at = tick - offsets[step]
+
+            def move_on(chunk, block, sub):
                 stage(
                     step, lax.rem(chunk, 2) + lax.rem(chunk, 12) // 11 * 3, chunk,
-                    lax.rem(chunk, subs) * 2 * acc.shape[-1],
+                    sub * 2 * acc.shape[-1],
                     staging.at[lax.rem(block, stages)], sum_ref.at[block], acc.at[chunk],
                     core_in.at[lax.rem(chunk, slots)], [ref.at[chunk] for ref in bit_in],
                 )
 
-            @pl.when(entry == chunks + gap)
+            @pl.when((at >= 2) & (at < 2 + early))
+            def _():
+                move_on(at - 2, (at - 2) // subs, lax.rem(at - 2, subs))
+
+            since = at - late
+            part = lax.rem(since, turn)
+
+            @pl.when((since >= 0) & (since < subs * turn) & (part < 3))
+            def _():
+                group = since // turn
+                move_on(early + group * 3 + part, 2 * folds + 1 + part, group)
+
+            @pl.when(at == closing + 2)
             def _():
                 stage(step, 0, chunks, 0, dsmall, ssum_ref, sacc, score_in, sbit_in)
 
@@ -572,7 +528,7 @@
     def prepare():
         total = 0.0
         for rows in tiles:
-            a = dot(o_ref[rows, :], wout_ref[...], ((1,), (0,)))
+            a = dot(o_ref[rows, :], wout[...], ((1,), (0,)))
             branch[rows, :] = a
             x1 = x_ref[rows, :].astype(F32) + gate_one * a
             middle[rows, :] = x1
@@ -672,22 +628,17 @@
             total = jnp.sum(value, axis=0, keepdims=True)
             line = slice(i, i + 1)
             vec[line, :] = total if rows is tiles[0] else vec[line, :] + total
-        active[rows, :] = dot(da, wout_ref[...], ((1,), (1,))).astype(BF)
+        active[rows, :] = dot(da, wout[...], ((1,), (1,))).astype(BF)
 
     def out_grads():
         vec[4:5, :] = vec[2:3, :] * (1.0 + scale_two)
         vec[2:3, :] = vec[2:3, :] * gain_two
-        for load in loads:
-            load.wait()
         for m in range(0, width, 256):
             cols = slice(m, m + 256)
             place_block(
                 2 * folds, dot(ot_ref[...], normed_low[:, cols], ((1,), (0,))).astype(BF), cols
             )
-        row_send_all(out_rows, tokens_ref, 0)
-
-    copies = count // 128
-    lane = lax.broadcasted_iota(jnp.int32, (1, 128), 1)
+
     place = pl.ds(pl.multiple_of(core * count, count), count)
 
     def kv_copies(p):
@@ -708,7 +659,8 @@
         cols = pl.ds(pl.multiple_of(p * 128, 128), 128)
         q = q_ref[:, cols]
         do = active[:, cols]
-        prod = ot_ref[cols, :].astype(F32) * do.astype(F32).T
+        if side == 0:
+            prod = ot_ref[cols, :].astype(F32) * do.astype(F32).T
         k_ref, v_ref, b_ref, dk_ref, dv_ref = (
             (kb_ref, vb_ref, bb_ref, normed_low, dm),
             (ka_ref, va_ref, ba_ref, total_a, total_b),
@@ -722,7 +674,9 @@
             part = slice(h * HEAD, (h + 1) * HEAD)
             qm = jnp.where(picked, q, jnp.zeros_like(q))
             dom = jnp.where(picked, do, jnp.zeros_like(do))
-            delta = jnp.sum(prod[part], axis=0, keepdims=True)
+            if side == 0:
+                deltas[h : h + 1, :] = jnp.sum(prod[part], axis=0, keepdims=True)
+            delta = deltas[h : h + 1, :]
             s = dot(k, qm, ((1,), (1,))) + wide_of(b_ref[...], copies)
             prob = jnp.exp(s - lse_ref[p, h : h + 1, :])
             dv_h = dot(prob.astype(BF), dom, ((1,), (0,)))
@@ -742,11 +696,9 @@
             dq = (dq_t[...] * (HEAD**-0.5)).T
             dqkv[:, cols] = rotate(dq, cos_ref[place, :], sin_ref[place, :], -1).astype(BF)
 
-    def join():
-        normed_t[...] = h_ref[...].T
-
-        @pl.loop(0, pairs)
-        def _(p):
+    def join(group):
+        for i in range(pairs // subs):
+            p = group * (pairs // subs) + i
             for copy in kv_copies(p):
                 copy.wait()
             cols = pl.ds(pl.multiple_of(p * 128, 128), 128)
@@ -757,14 +709,12 @@
             dqkv[:, k_cols] = rotate(dk, cos_ref[place, :], sin_ref[place, :], -1).astype(BF)
             dqkv[:, v_cols] = dv.astype(BF)
 
-    def project_grads(n):
-        for m in range(0, width, 256):
-            cols = pl.ds(pl.multiple_of(n * width + m, 256), 256)
-            place_block(
-                2 * folds + 1 + n,
-                dot(normed_t[...], dqkv[:, cols], ((1,), (0,))).astype(BF),
-                slice(m, m + 256),
-            )
+    def project_grads(group, n):
+        cols = pl.ds(pl.multiple_of(n * width + group * 256, 256), 256)
+        value = dot(normed_t[...], dqkv[:, cols], ((1,), (0,))).astype(BF)
+        place_block(
+            2 * folds + 1 + n, value, pl.ds(pl.multiple_of(group * 256, 256), 256)
+        )
 
     def finish(rows):
         if rows is tiles[0]:
@@ -792,7 +742,6 @@
             vec[line, :] = total if rows is tiles[0] else vec[line, :] + total
 
     def small_grads():
-        row_send_all(drows, grad_ref, 1)
         scale = 1.0 + part_of(mod_ref, 1, width)
         srows = dsmall.shape[1]
         seqs = wide_size * groups
@@ -820,14 +769,13 @@
         dsmall[...] = value.reshape(pieces, srows, width).astype(BF)
 
     prepare()
-    join_at = 6 * folds + 3 + 2 * pairs
     units = []
     for n in range(2):
         for t, rows in enumerate(tiles):
             units.append((n * 3 + t, (hidden_units, hidden_units_back)[n], rows))
         units.append((n * 3 + 2, (down_grads, up_grads)[n], None))
 
-    @pl.loop(0, chunks + gap + 3 + offsets[-1])
+    @pl.loop(0, closing + 3 + offsets[-1])
     def _(tick):
         for at, unit, rows in units:
 
@@ -841,54 +789,70 @@
             def _():
                 close_hidden(rows)
 
-            @pl.when(tick == join_at + 2 + t)
+            @pl.when(tick == closing + t)
             def _():
                 finish(rows)
 
         @pl.when(tick == 6 * folds + 2)
         def _():
             out_grads()
-
-        for side in range(2):
-
-            @pl.when(
-                (tick >= 6 * folds + 3)
-                & (tick < 6 * folds + 3 + 2 * pairs)
-                & (lax.rem(tick - (6 * folds + 3), 2) == side)
-            )
-            def _():
-                attention((tick - (6 * folds + 3)) // 2, side)
-
-        @pl.when(tick == join_at)
+            normed_t[...] = h_ref[...].T
+
+        since = tick - lead
+        part = lax.rem(since, turn)
+        for at in range(2 * (pairs // subs)):
+
+            @pl.when((since >= 0) & (since < subs * turn) & (part == at))
+            def _():
+                attention(since // turn * (pairs // subs) + at // 2, at % 2)
+
+        back = tick - late + 1
+        back_part = lax.rem(back, turn)
+
+        @pl.when((back >= 0) & (back < subs * turn) & (back_part == 0))
         def _():
-            join()
+            join(back // turn)
 
         for n in range(3):
 
-            @pl.when(tick == join_at + 1 + subs * n)
-            def _():
-                project_grads(n)
-
-        @pl.when(tick == join_at + subs + 2)
+            @pl.when((back >= 0) & (back < subs * turn) & (back_part == 1 + n))
+            def _():
+                project_grads(back // turn, n)
+
+        @pl.when(tick == closing + 2)
         def _():
             small_grads()
 
+        for kind, (src, dst, first) in enumerate(
+            ((out_rows, tokens_ref, 6 * folds + 2), (drows, grad_ref, closing + 2))
+        ):
+
+            @pl.when(
+                (tick >= first) & (tick < first + 2 * parts) & (lax.rem(tick - first, 2) == 0)
+            )
+            def _():
+                row_send_part(src, dst, kind, (tick - first) // 2)
+
         communicate(tick)
 
-    row_wait_all(out_rows, tokens_ref, 0)
-    row_wait_all(drows, grad_ref, 1)
-
-
-def rest_of_block(
-    x, o, ot, dy, mod, params, cosines, sines, cond, lse, wout, q, ka, va, kb, vb, h, ba, bb,
-    up, down, wqkv, groups, wide_size, ring,
-    lags=(3, 6, 5, 3),
+    sent(cot_ref, dy_ref, 1)
+
+    @pl.loop(0, parts)
+    def _(q):
+        row_wait_part(out_rows, tokens_ref, 0, q)
+        row_wait_part(drows, grad_ref, 1, q)
+
+
+def whole_block(
+    tokens, cotangent, wqkv, ada, wout, up, down, info, gain_one, gain_two, down_bias, ada_bias,
+    up_bias, cosines, sines, wide_size, ring,
+    lags=(2, 4, 3, 2),
 ):
-    count, width = x.shape
+    groups, span, width = tokens.shape
+    count = groups * span
     pieces = wide_size // 2 * ring
     rows = width // pieces
     half = width // 2
-    sub_half = 128
     folds = up.shape[1] // width
     subs = width // 256
     blocks = 2 * folds + 4
@@ -896,20 +860,22 @@
     pairs = width // 128
     total_bits = pieces.bit_length() - 1
     first = list(lags[:3]) + [lags[3]] * (total_bits - 2)
-    lags = first + first[::-1]
-    assert subs * 256 == width and subs == 3
+    lags = tuple(first + first[::-1])
+    assert subs * 256 == width and subs == 3 and sum(lags) > 16
     seqs = wide_size * groups
     srows = -(-(seqs * 7 + 3 + folds) // (pieces * 8)) * 8
     sizes = [pieces >> (i + 1) for i in range(total_bits)]
     any_space = pl.BlockSpec(memory_space=pl.ANY)
     vmem = pl.BlockSpec(memory_space=pltpu.VMEM)
-    block = jax.ShapeDtypeStruct((groups, count // groups, width), BF)
+    block = jax.ShapeDtypeStruct((groups, span, width), BF)
     rows_low = pltpu.VMEM((count, width), BF)
     rows_full = pltpu.VMEM((count, width), F32)
     lanes = pltpu.VMEM((count, 128), F32)
+    turned = pltpu.VMEM((width, count), BF)
+    vectors = pltpu.VMEM((8, width), F32)
     return pl.pallas_call(
-        functools.partial(rest_kernel, groups, wide_size, ring, tuple(lags)),
-        in_specs=[vmem] * 11 + [any_space] * 11,
+        functools.partial(block_kernel, groups, wide_size, ring, lags),
+        in_specs=[any_space] * 7 + [vmem] * 8,
         out_specs=[any_space] * 4,
         out_shape=[
             jax.ShapeDtypeStruct((blocks, pieces, rows, width), BF),
@@ -917,135 +883,141 @@
             block,
             block,
         ],
-        scratch_shapes=[rows_low] * 6
-        + [lanes] * 2
+        scratch_shapes=[rows_low] * 9
         + [
+            turned,
+            pltpu.VMEM((pairs, 8, count), F32),
+            pltpu.VMEM((1, 6 * width), F32),
+            lanes,
+            lanes,
+            pltpu.VMEM((1, TEMB), F32),
+            pltpu.VMEM((2,) + info.shape, F32),
+            pltpu.VMEM((-(-(9 + folds) // 8) * 8, width), F32),
+            pltpu.VMEM((width, width), BF),
             pltpu.VMEM((4, width, width), BF),
             pltpu.VMEM((4, pieces, rows, width), BF),
             pltpu.VMEM((pieces, srows, width), BF),
             rows_full,
             rows_full,
             rows_low,
-            pltpu.VMEM((width, count), BF),
+            turned,
             rows_low,
             rows_full,
             rows_full,
             rows_low,
             rows_full,
             pltpu.VMEM((128, count), F32),
-            pltpu.VMEM((8, width), F32),
-            pltpu.VMEM((8, width), F32),
+            pltpu.VMEM((8, count), F32),
+            vectors,
+            vectors,
             rows_low,
             rows_low,
             pltpu.VMEM((count, 3 * width), BF),
             rows_low,
             rows_low,
-            pltpu.VMEM((chunks, pieces, rows, sub_half), BF),
+            pltpu.VMEM((chunks, pieces, rows, 128), BF),
             pltpu.VMEM((pieces, srows, half), BF),
-            pltpu.VMEM((2 * lags[0] + 1, pieces, rows, sub_half), BF),
+            pltpu.VMEM((2 * lags[0] + 1, pieces, rows, 128), BF),
             pltpu.VMEM((pieces, srows, half), BF),
-            [pltpu.VMEM((chunks, n, rows, sub_half), BF) for n in sizes],
+            [pltpu.VMEM((chunks, n, rows, 128), BF) for n in sizes],
             [pltpu.VMEM((n, srows, half), BF) for n in sizes],
-            DMA((8,)),
+            DMA((7,)),
             DMA((4,)),
+            DMA((2,)),
+            DMA,
+            DMA,
+            DMA((2, groups)),
+            DMA((2, groups)),
+            DMA((2, groups)),
+            DMA((2, groups)),
             DMA((chunks + 1,)),
             DMA((2 + 2 * total_bits, chunks + 1)),
             DMA((2 + 2 * total_bits, chunks + 1)),
             DMA((2, pairs)),
             DMA((2, pairs)),
-            DMA((2,)),
-            DMA((2, groups)),
-            DMA((2, groups)),
+            DMA((2, 8)),
+            DMA((2, groups, 8)),
+            DMA((2, groups, 8)),
         ],
         compiler_params=pltpu.CompilerParams(
             collective_id=0, has_side_effects=True, vmem_limit_bytes=63 << 20
         ),
-        name="rest_of_block",
+        name="whole_block",
     )(
-        x, o, ot, dy, mod, params, cosines, sines, cond, lse, wout, q, ka, va, kb, vb, h, ba, bb,
-        up, down, wqkv,
+        tokens, cotangent, wqkv, ada, wout, up, down, info, gain_one, gain_two, down_bias, ada_bias,
+        up_bias, cosines, sines,
     )
 
 
-def spread_kernel(seqs, folds, sum_ref, small_ref, ada_ref, qkv_ref, out_ref, up_ref, down_ref,
-                  ada_bias_ref, gain_one_ref, gain_two_ref, up_bias_ref, down_bias_ref):
-    i = pl.program_id(0)
-    width = sum_ref.shape[-1]
-    value = sum_ref[0].astype(F32)
-
-    @pl.when(i < folds)
-    def _():
-        down_ref[...] = value
-
-    @pl.when((i >= folds) & (i < 2 * folds))
-    def _():
-        up_ref[...] = value
-
-    @pl.when(i == 2 * folds)
-    def _():
-        out_ref[...] = value
-
-    @pl.when(i > 2 * folds)
-    def _():
-        qkv_ref[...] = value
-
-    @pl.when(i == 0)
-    def _():
-        cond = small_ref[6 * seqs : 7 * seqs, : 3 * TEMB]
-        for n in range(6):
-            mod = small_ref[n * seqs : (n + 1) * seqs, :]
-            three = dot(mod, cond, ((0,), (0,)))
-            ada_ref[n * width : (n + 1) * width, :] = (
-                three[:, :TEMB] + three[:, TEMB : 2 * TEMB] + three[:, 2 * TEMB :]
-            )
-            ada_bias_ref[n * width : (n + 1) * width] = jnp.sum(mod.astype(F32), axis=0)
-        rows = small_ref[7 * seqs : 7 * seqs + 8 * (-(-(3 + folds) // 8)), :].astype(F32)
-        gain_one_ref[...] = rows[0]
-        gain_two_ref[...] = rows[1]
-        down_bias_ref[...] = rows[2]
-        for n in range(folds):
-            up_bias_ref[n * width : (n + 1) * width] = rows[3 + n]
+def spread_kernel(
+    seqs, folds,
+    sum_ref, small_ref,
+    ada_ref, qkv_ref, out_ref, up_ref, down_ref,
+    ada_bias_ref, gain_one_ref, gain_two_ref, up_bias_ref, down_bias_ref,
+    taken, wide, take_sem, give_sem,
+):
+    blocks, width = sum_ref.shape[0], sum_ref.shape[-1]
+    order = list(range(blocks))
+    takes = [pltpu.make_async_copy(sum_ref.at[n], taken.at[n], take_sem.at[n]) for n in order]
+    for take in takes:
+        take.start()
+    cond = small_ref[6 * seqs : 7 * seqs, : 3 * TEMB]
+    for n in range(6):
+        mod = small_ref[n * seqs : (n + 1) * seqs, :]
+        three = dot(mod, cond, ((0,), (0,)))
+        ada_ref[n * width : (n + 1) * width, :] = (
+            three[:, :TEMB] + three[:, TEMB : 2 * TEMB] + three[:, 2 * TEMB :]
+        )
+        ada_bias_ref[n * width : (n + 1) * width] = jnp.sum(mod.astype(F32), axis=0)
+    rows = small_ref[7 * seqs : 7 * seqs + 8 * (-(-(3 + folds) // 8)), :].astype(F32)
+    gain_one_ref[...] = rows[0]
+    gain_two_ref[...] = rows[1]
+    down_bias_ref[...] = rows[2]
+    for n in range(folds):
+        up_bias_ref[n * width : (n + 1) * width] = rows[3 + n]
+
+    gives = []
+    for n in order:
+        if n < 2 * folds:
+            whole = pl.ds(n // 2 * width, width)
+            place = up_ref.at[:, whole] if n % 2 else down_ref.at[whole]
+        elif n == 2 * folds:
+            place = out_ref
+        else:
+            place = qkv_ref.at[:, pl.ds((n - 2 * folds - 1) * width, width)]
+        gives.append(pltpu.make_async_copy(wide.at[n], place, give_sem.at[n]))
+        takes[n].wait()
+
+        @pl.loop(0, width // 32)
+        def _(r):
+            lines = pl.ds(pl.multiple_of(r * 32, 32), 32)
+            wide[n, lines, :] = taken[n, lines, :].astype(F32)
+
+        gives[n].start()
+    for give in gives:
+        give.wait()
 
 
 def spread(summed, small, seqs, folds):
-    chunks, width = summed.shape[0], summed.shape[-1]
-
-    def fixed(shape):
-        return pl.BlockSpec(shape, lambda i: (0,) * len(shape))
-
-    def chunk(i):
-        hidden = 2 * (i % folds) + i // folds
-        return jnp.where(i < 2 * folds, hidden, i)
-
-    def at(first, size, axis):
-        def index(i):
-            block = jnp.clip(i - first, 0, size - 1)
-            return (block, 0) if axis == 0 else (0, block)
-
-        return pl.BlockSpec((width, width), index)
-
-    vectors = [(6 * width,), (width,), (width,), (folds * width,), (width,)]
+    blocks, width = summed.shape[0], summed.shape[-1]
+    any_space = pl.BlockSpec(memory_space=pl.ANY)
+    vmem = pl.BlockSpec(memory_space=pltpu.VMEM)
+    shapes = [
+        (6 * width, TEMB), (width, 3 * width), (width, width), (width, folds * width),
+        (folds * width, width), (6 * width,), (width,), (width,), (folds * width,), (width,),
+    ]
     return pl.pallas_call(
         functools.partial(spread_kernel, seqs, folds),
-        grid=(chunks,),
-        in_specs=[pl.BlockSpec((1, width, width), lambda i: (chunk(i), 0, 0)), fixed(small.shape)],
-        out_specs=[
-            fixed((6 * width, TEMB)),
-            at(2 * folds + 1, 3, 1),
-            fixed((width, width)),
-            at(folds, folds, 1),
-            at(0, folds, 0),
-        ]
-        + [fixed(shape) for shape in vectors],
-        out_shape=[
-            jax.ShapeDtypeStruct(shape, F32)
-            for shape in [
-                (6 * width, TEMB), (width, 3 * width), (width, width), (width, folds * width),
-                (folds * width, width),
-            ]
-            + vectors
+        in_specs=[any_space, vmem],
+        out_specs=[vmem] + [any_space] * 4 + [vmem] * 5,
+        out_shape=[jax.ShapeDtypeStruct(shape, F32) for shape in shapes],
+        scratch_shapes=[
+            pltpu.VMEM((blocks, width, width), BF),
+            pltpu.VMEM((blocks, width, width), F32),
+            DMA((blocks,)),
+            DMA((blocks,)),
         ],
-        compiler_params=pltpu.CompilerParams(vmem_limit_bytes=56 << 20),
+        compiler_params=pltpu.CompilerParams(vmem_limit_bytes=60 << 20),
         name="spread",
     )(summed, small)
 
@@ -1066,17 +1038,11 @@
     allowed = (jnp.arange(length, dtype=jnp.int32)[None, :] < prefix[:, None]) | (keep_bits == 1)
     info = jnp.concatenate(
         [jax.nn.silu(time_embed(step_ids)), jnp.where(allowed, 0.0, masked_score)], axis=1
-    )[:, None, :]
-    params = jnp.concatenate([norm1_gain, norm2_gain, down_bias, ada_bias, up_bias]).reshape(
-        -1, width
     )
     cosines, sines = rope_tables(length)
-    x, dy, h, q, ka, va, kb, vb, o, ot, lse, mod, ba, bb, cond = front(
-        tokens, cotangent, qkv_weight, ada_weight, info, params, cosines, sines, ring
-    )
-    summed, small, outputs, input_grad = rest_of_block(
-        x, o, ot, dy, mod, params, cosines, sines, cond, lse, out_weight, q, ka, va, kb, vb, h,
-        ba, bb, up_weight, down_weight, qkv_weight, groups, wide_size, ring,
+    summed, small, outputs, input_grad = whole_block(
+        tokens, cotangent, qkv_weight, ada_weight, out_weight, up_weight, down_weight, info,
+        norm1_gain, norm2_gain, down_bias, ada_bias, up_bias, cosines, sines, wide_size, ring,
     )
     ada, qkv, out, up, down, ada_bias_grad, gain_one, gain_two, up_bias_grad, down_bias_grad = (
         spread(summed.reshape(-1, width, width), small.reshape(-1, width), seqs, folds)

time: 268 us -> 246 us (0.918)
  Pallas kernels: 258 us -> 241 us
  local copies, waits for them, and re-layouts: 6.53 us -> 1.77 us
    pallas_call x3 -> x2, Pallas kernels: 258 us -> 241 us  [the longest x1 225 us: whole_block(): pl.pallas_call(functools.partial(block_kernel, groups, wide_size, ring, l...]
    unnamed x10 -> x6, local copies, waits for them, and re-layouts: 4.58 us -> 1.77 us
where the time goes in v4:
time: 246 us
  Pallas kernels  241 us (98%)
    pallas_call x1, Pallas kernels, whole_block(): pl.pallas_call(functools.partial(block_kernel, groups, wide_size, ring, l...  225 us
    pallas_call x1, Pallas kernels, spread(): pl.pallas_call(functools.partial(spread_kernel, seqs, folds), in_specs=[a...  16 us

profile of v4, /device:TPU:1, one launch (start us, length us, event | category | flops | bytes accessed | tf_op | source)
XLA Modules:
  0.0 245.8 jit_solution(18292662462500043964)
XLA Ops:
  0.6 0.7 convert_element_type.3
  1.3 0.1 multiply_cosine_fusion
  1.4 0.1 divide_multiply_fusion
  1.5 0.8 or_select_fusion
  2.3 0.6 pad_maximum_fusion.info_ref
  2.9 225.1 %whole_block.1 = (bf16[12,16,48,768]{3,2,1,0:T(8,128)(2,1)}, bf16[16,8,768]{2,1,0:T(8,128)(2,1)}, bf16[2,256,768]{2,1,0:T(8,128)(2,1)}, bf16[2,256,768]{2,1,0:T(8,128)(2,1)}) custom-call(bf16[2,256,768]{2,1,0:T(8,128)(2,1)} %tok_ref.1, bf16[2,256,768]{2,1,0:T(8,128)(2,1)} %cot_ref.1, bf16[768,2304]{1,0:T(8,128)(2,1)} %wqkv_ref.1, bf16[4608,128]{1,0:T(8,128)(2,1)} %ada_ref.1, ...), custom_call_target="tpu_custom_call" | custom-call | tf_op jit(solution)/shard_map/whole_block/pallas_call | solution.py:876
  228.0 0.0 copy-start.1
  228.0 0.0 copy-start
  228.0 16.0 %spread.1 = (f32[4608,128]{1,0:T(8,128)}, f32[768,2304]{1,0:T(8,128)}, f32[768,768]{1,0:T(8,128)}, f32[768,3072]{1,0:T(8,128)}, f32[3072,768]{1,0:T(8,128)}, /*i...) custom-call(bf16[12,768,768]{2,1,0:T(8,128)(2,1)} %bitcast.2, bf16[128,768]{1,0:T(8,128)(2,1)} %bitcast.3), custom_call_target="tpu_custom_call" | custom-call | tf_op jit(solution)/shard_map/spread/pallas_call | solution.py:1009
  244.0 0.0 copy-done.1
  244.1 0.9 copy.31
  244.9 0.0 copy-done
  244.9 0.9 copy.32
  (1 shorter events, 0.0 us)
Async XLA Ops:
  228.0 16.0 %copy-start.1 = (bf16[2,256,768]{2,1,0:T(8,128)(2,1)S(1)}, bf16[2,256,768]{2,1,0:T(8,128)(2,1)}, u32[]{:S(2)}) copy-start(bf16[2,256,768]{2,1,0:T(8,128)(2,1)} %get-tuple-element.54) | copy-start | bytes 2359300
  228.0 16.9 %copy-start = (bf16[2,256,768]{2,1,0:T(8,128)(2,1)S(1)}, bf16[2,256,768]{2,1,0:T(8,128)(2,1)}, u32[]{:S(2)}) copy-start(bf16[2,256,768]{2,1,0:T(8,128)(2,1)} %get-tuple-element.55) | copy-start | bytes 2359300

commit v5 on v4

--- a/solution.py
+++ b/solution.py
@@ -19,6 +19,8 @@
 norm_epsilon = 1e-05
 gelu_coeff = 0.7978845608028654
 masked_score = -1e30
+EARLY = (2, 6, 5, 5, 3)
+LATE = (2, 4, 3)
 
 
 def time_embed(step_ids):
@@ -71,7 +73,7 @@
 
 
 def block_kernel(
-    groups, wide_size, ring, lags,
+    groups, wide_size, ring, early_lags, late_lags,
     tok_ref, cot_ref, wqkv_ref, ada_ref, wout_ref, up_ref, down_ref,
     info_ref, gain_one_ref, gain_two_ref, down_bias_ref, ada_bias_ref, up_bias_ref, cos_ref,
     sin_ref,
@@ -80,22 +82,18 @@
     ba_ref, bb_ref, cond_ref, table, par_ref, wout,
     weights, staging, dsmall, middle, branch, normed_low, normed_t, dm, total_a, total_b, active,
     slope, dq_t, deltas, vec, dup_bias, out_rows, drows, dqkv, dk_in, dv_in,
-    acc, sacc, core_in, score_in, bit_in, sbit_in,
+    early_buffers, late_buffers, small_buffers,
     load_sem, weight_sem, take_self, info_send, info_recv, take_send, take_recv, swap_send,
-    swap_recv, copy_sem, send_sem, recv_sem, kv_send, kv_recv, self_sem, row_send, row_recv,
+    swap_recv, copy_sem, send_sem, recv_sem, ring_send, ring_recv, gather_send, gather_recv, kv_send, kv_recv, self_sem, row_send, row_recv,
 ):
-    chunks, pieces, piece_rows = acc.shape[:3]
-    slots = core_in.shape[0]
+    early, subs, pieces, piece_rows = early_buffers[0].shape[:4]
+    late_count = late_buffers[0].shape[0]
     stages = staging.shape[0]
     outer = (wide_size // 2).bit_length() - 1
-    inner = ring.bit_length() - 1
-    total_bits = outer + inner
     count, width = x_ref.shape
-    subs = width // (2 * acc.shape[-1])
     span = count // groups
     pairs = width // 128
     folds = up_ref.shape[1] // width
-    early = (2 * folds + 1) * subs
     wide = lax.axis_index("wide")
     chip = lax.axis_index("narrow")
     core = lax.rem(wide, 2)
@@ -105,12 +103,6 @@
     for b in range(outer):
         bit = lax.rem(wide // (2 << b), 2)
         dims.append((bit, wide + (1 - 2 * bit) * (2 << b), chip))
-    for b in range(inner):
-        bit = lax.rem(chip // (1 << b), 2)
-        dims.append((bit, wide, chip + (1 - 2 * bit) * (1 << b)))
-    up = list(range(outer))
-    rest = list(range(outer, total_bits))
-    orders = (up + rest, up[::-1] + rest, rest + up)
 
     def load_up(i, slot):
         cols = pl.ds(pl.multiple_of(i * width, width), width)
@@ -384,28 +376,21 @@
                     device_id_type=MESH,
                 ).wait_recv()
 
-    def plan(kind):
-        late = kind // 4
-        odd = lax.rem(kind, 2) * (1 - late)
+    last = 2 * outer + 4
+
+    def stage(step, odd, sem, pick, source, out, total, core_slot, ring_slot, bit_slots):
         low = 0
         size = pieces
         steps = []
-        for i in range(total_bits):
-            bit, peer_wide, peer_here = (
-                a + odd * (b - a) + late * (c - a)
-                for a, b, c in zip(*(dims[order[i]] for order in orders))
-            )
+        for i in range(outer):
+            (bit, peer_wide, _), (other_bit, other_wide, _) = dims[i], dims[outer - 1 - i]
+            bit = bit + odd * (other_bit - bit)
+            peer_wide = peer_wide + odd * (other_wide - peer_wide)
             size //= 2
             before = low
             low = low + bit * size
-            steps.append((before + (1 - bit) * size, low, size, (peer_wide, peer_here)))
-        return steps
-
-    def stage(step, kind, sem, lane_base, big, out, total, core_slot, bit_slots):
-        cols = total.shape[-1]
-        mine = pl.ds(pl.multiple_of(lane_base + core * cols, 128), cols)
-        other = pl.ds(pl.multiple_of(lane_base + (1 - core) * cols, 128), cols)
-        steps = plan(kind)
+            steps.append((before + (1 - bit) * size, low, size, (peer_wide, chip)))
+        final = low + chip
 
         def remote(src, dst, index, peer):
             return pltpu.make_async_remote_copy(
@@ -418,36 +403,60 @@
             )
 
         def core_copy():
-            return remote(big.at[:, :, other], core_slot, 0, core_peer)
+            return remote(source(1 - core), core_slot, 0, core_peer)
 
         def own_copy():
-            return pltpu.make_async_copy(big.at[:, :, mine], total, copy_sem.at[sem])
+            return pltpu.make_async_copy(source(core), total, copy_sem.at[sem])
 
         def bit_copy(i):
             away, _, size, peer = steps[i]
-            return remote(total.at[pl.ds(away, size)], bit_slots[i], 1 + i, peer)
+            return remote(pick(total, away, size), bit_slots[i], 1 + i, peer)
+
+        def ring_copies():
+            copies = []
+            for d in range(1, ring):
+                target = lax.rem(chip + d, ring)
+                copies.append(
+                    pltpu.make_async_remote_copy(
+                        src_ref=pick(total, low + target, 1),
+                        dst_ref=ring_slot.at[d - 1],
+                        send_sem=ring_send.at[d - 1, sem],
+                        recv_sem=ring_recv.at[d - 1, sem],
+                        device_id=(wide, target),
+                        device_id_type=MESH,
+                    )
+                )
+            return copies
+
+        def gather_copies():
+            return [
+                pltpu.make_async_remote_copy(
+                    src_ref=pick(total, final, 1),
+                    dst_ref=pick(out(core), final, 1),
+                    send_sem=gather_send.at[d - 1, sem],
+                    recv_sem=gather_recv.at[d - 1, sem],
+                    device_id=(wide, lax.rem(chip + d, ring)),
+                    device_id_type=MESH,
+                )
+                for d in range(1, ring)
+            ]
+
+        def keep_copy():
+            return pltpu.make_async_copy(
+                pick(total, final, 1), pick(out(core), final, 1), copy_sem.at[sem]
+            )
 
         def back_copy(i):
             _, keep, size, peer = steps[i]
-            place = out.at[pl.ds(keep, size), :, mine]
-            if i == total_bits - 1:
-                return remote(total.at[pl.ds(keep, size)], place, 1 + total_bits + i, peer)
-            return remote(place, place, 1 + total_bits + i, peer)
-
-        def keep_copy():
-            _, keep, size, _ = steps[-1]
-            return pltpu.make_async_copy(
-                total.at[pl.ds(keep, size)], out.at[pl.ds(keep, size), :, mine], copy_sem.at[sem]
-            )
+            place = pick(out(core), keep, size)
+            return remote(place, place, 1 + outer + i, peer)
 
         def core_back():
-            place = out.at[:, :, mine]
-            return remote(place, place, 1 + 2 * total_bits, core_peer)
-
-        def add(start, size, from_slot):
-            @pl.loop(0, size)
-            def _(j):
-                total[start + j] = (total[start + j].astype(F32) + from_slot[j].astype(F32)).astype(BF)
+            return remote(out(core), out(core), 1 + 2 * outer, core_peer)
+
+        def add(start, size, slot):
+            place = pick(total, start, size)
+            place[...] = place[...] + slot[...]
 
         if step == 0:
             core_copy().start()
@@ -455,69 +464,113 @@
         elif step == 1:
             own_copy().wait()
             core_copy().wait()
-            add(0, pieces, core_slot)
+            total[...] = total[...] + core_slot[...]
             bit_copy(0).start()
-        elif step <= total_bits + 1:
+        elif step <= outer + 1:
             i = step - 2
             bit_copy(i).wait()
             add(steps[i][1], steps[i][2], bit_slots[i])
-            if step <= total_bits:
+            if step <= outer:
                 bit_copy(i + 1).start()
             else:
-                keep_copy().start()
-                back_copy(i).start()
-        elif step <= 2 * total_bits:
-            i = 2 * total_bits + 1 - step
-            if i == total_bits - 1:
-                keep_copy().wait()
-            back_copy(i).wait()
-            back_copy(i - 1).start()
-        elif step == 2 * total_bits + 1:
+                for copy in ring_copies():
+                    copy.start()
+        elif step == outer + 2:
+            for copy in ring_copies():
+                copy.wait()
+            place = pick(total, final, 1)
+            value = place[...].astype(F32)
+            for d in range(1, ring):
+                value = value + ring_slot[d - 1].astype(F32)
+            place[...] = value.astype(BF)
+            keep_copy().start()
+            for copy in gather_copies():
+                copy.start()
+        elif step == outer + 3:
+            keep_copy().wait()
+            for copy in gather_copies():
+                copy.wait()
+            back_copy(outer - 1).start()
+        elif step <= 2 * outer + 2:
+            i = 2 * outer + 2 - step
+            back_copy(i + 1).wait()
+            back_copy(i).start()
+        elif step == 2 * outer + 3:
             back_copy(0).wait()
             core_back().start()
         else:
             core_back().wait()
 
-    last = 2 * total_bits + 2
-    offsets = [sum(lags[:step]) for step in range(last + 1)]
+    early_at = [2 + sum(early_lags[:step]) for step in range(last + 1)]
+    late_at = [sum(late_lags[:step]) for step in range(last + 1)]
     turn = 2 * (pairs // subs) + subs
     lead = 6 * folds + 3
     late = lead + turn - 2
     closing = lead + subs * turn + 1
 
-    def communicate(tick):
+    def pick_early(ref, start, size):
+        return ref.at[:, pl.ds(start, size)]
+
+    def pick_late(ref, start, size):
+        return ref.at[pl.ds(start, size)]
+
+    early_end = 3 * early + early_at[-1]
+
+    def move_early(tick):
+        turn_now = lax.rem(tick, 3)
         for step in range(last, -1, -1):
-            at = tick - offsets[step]
-
-            def move_on(chunk, block, sub):
+            since = tick - early_at[step]
+
+            @pl.when(
+                (since >= 0) & (since < 3 * early) & (turn_now == early_at[step] % 3)
+            )
+            def _():
+                chunk = lax.div(since, 3)
+                total, core_slots, ring_slots, bit_slots = early_buffers
                 stage(
-                    step, lax.rem(chunk, 2) + lax.rem(chunk, 12) // 11 * 3, chunk,
-                    sub * 2 * acc.shape[-1],
-                    staging.at[lax.rem(block, stages)], sum_ref.at[block], acc.at[chunk],
-                    core_in.at[lax.rem(chunk, slots)], [ref.at[chunk] for ref in bit_in],
+                    step, lax.rem(chunk, 2), chunk, pick_early,
+                    lambda half: staging.at[lax.rem(chunk, stages), :, half],
+                    lambda half: sum_ref.at[chunk, :, half],
+                    total.at[chunk], core_slots.at[lax.rem(chunk, 2)], ring_slots.at[chunk],
+                    [ref.at[chunk] for ref in bit_slots],
                 )
 
-            @pl.when((at >= 2) & (at < 2 + early))
-            def _():
-                move_on(at - 2, (at - 2) // subs, lax.rem(at - 2, subs))
-
-            since = at - late
-            part = lax.rem(since, turn)
-
-            @pl.when((since >= 0) & (since < subs * turn) & (part < 3))
-            def _():
-                group = since // turn
-                move_on(early + group * 3 + part, 2 * folds + 1 + part, group)
-
-            @pl.when(at == closing + 2)
-            def _():
-                stage(step, 0, chunks, 0, dsmall, ssum_ref, sacc, score_in, sbit_in)
-
-    def place_block(block, value, cols):
-        for i in range(pieces):
-            staging[lax.rem(block, stages), i, :, cols] = value[
-                i * piece_rows : (i + 1) * piece_rows
-            ]
+    def move_late(tick):
+        turn_now = lax.rem(tick, turn)
+        for step in range(last, -1, -1):
+            at = tick - late_at[step] - late
+            zero = (late_at[step] + late) % turn
+            on = [turn_now == (zero + n) % turn for n in range(3)]
+
+            @pl.when((at >= 0) & (at < subs * turn) & (on[0] | on[1] | on[2]))
+            def _():
+                group = lax.div(at, turn)
+                part = at - group * turn
+                chunk = group * 3 + part
+                block = early + part
+                total, core_slots, ring_slots, bit_slots = late_buffers
+                stage(
+                    step, lax.rem(chunk, 2), early + chunk, pick_late,
+                    lambda half: staging.at[lax.rem(block, stages), group, half],
+                    lambda half: sum_ref.at[block, group, half],
+                    total.at[chunk], core_slots.at[lax.rem(chunk, core_slots.shape[0])],
+                    ring_slots.at[chunk], [ref.at[chunk] for ref in bit_slots],
+                )
+
+            @pl.when(tick == closing + 2 + late_at[step])
+            def _():
+                stage(
+                    step, 0, early + late_count, pick_late,
+                    lambda half: dsmall.at[half], lambda half: ssum_ref.at[half], *small_buffers
+                )
+
+    def place_block(block, part, value):
+        for half in range(2):
+            lanes = slice(half * 128, (half + 1) * 128)
+            for i in range(pieces):
+                staging[lax.rem(block, stages), part, half, i] = value[
+                    i * piece_rows : (i + 1) * piece_rows, lanes
+                ]
 
     tile = min(256, count)
     tiles = [slice(r, r + tile) for r in range(0, count, tile)]
@@ -529,7 +582,7 @@
         total = 0.0
         for rows in tiles:
             a = dot(o_ref[rows, :], wout[...], ((1,), (0,)))
-            branch[rows, :] = a
+            branch[rows, :] = a.astype(BF)
             x1 = x_ref[rows, :].astype(F32) + gate_one * a
             middle[rows, :] = x1
             normed, _ = normed_rows(x1)
@@ -568,7 +621,9 @@
     def down_grads(i):
         for m in range(0, width, 256):
             cols = slice(m, m + 256)
-            place_block(2 * i, dot(active[...], dm[:, cols], ((0,), (0,))).astype(BF), cols)
+            place_block(
+                2 * i, m // 256, dot(active[...], dm[:, cols], ((0,), (0,))).astype(BF)
+            )
 
     def hidden_units_back(i, rows):
         slot = 2 * lax.rem(i, 2)
@@ -606,7 +661,9 @@
 
         for m in range(0, width, 256):
             cols = slice(m, m + 256)
-            place_block(2 * i + 1, dot(normed_t[...], active[:, cols], ((1,), (0,))).astype(BF), cols)
+            place_block(
+                2 * i + 1, m // 256, dot(normed_t[...], active[:, cols], ((1,), (0,))).astype(BF)
+            )
 
     def close_hidden(rows):
         m = total_a[rows, :] + par_ref[2:3, :]
@@ -624,7 +681,7 @@
         middle[rows, :] = dx1
         da = (gate_one * dx1).astype(BF)
         normed_low[rows, :] = da
-        for i, value in enumerate((dx1 * branch[rows, :], dh, dh * n2, dy * m)):
+        for i, value in enumerate((dx1 * branch[rows, :].astype(F32), dh, dh * n2, dy * m)):
             total = jnp.sum(value, axis=0, keepdims=True)
             line = slice(i, i + 1)
             vec[line, :] = total if rows is tiles[0] else vec[line, :] + total
@@ -636,7 +693,7 @@
         for m in range(0, width, 256):
             cols = slice(m, m + 256)
             place_block(
-                2 * folds, dot(ot_ref[...], normed_low[:, cols], ((1,), (0,))).astype(BF), cols
+                2 * folds, m // 256, dot(ot_ref[...], normed_low[:, cols], ((1,), (0,))).astype(BF)
             )
 
     place = pl.ds(pl.multiple_of(core * count, count), count)
@@ -712,9 +769,7 @@
     def project_grads(group, n):
         cols = pl.ds(pl.multiple_of(n * width + group * 256, 256), 256)
         value = dot(normed_t[...], dqkv[:, cols], ((1,), (0,))).astype(BF)
-        place_block(
-            2 * folds + 1 + n, value, pl.ds(pl.multiple_of(group * 256, 256), 256)
-        )
+        place_block(early + n, group, value)
 
     def finish(rows):
         if rows is tiles[0]:
@@ -743,7 +798,7 @@
 
     def small_grads():
         scale = 1.0 + part_of(mod_ref, 1, width)
-        srows = dsmall.shape[1]
+        srows = dsmall.shape[2]
         seqs = wide_size * groups
         seq = (wide // 2) * ring + chip
         line = lax.broadcasted_iota(jnp.int32, (pieces * srows, width), 0)
@@ -766,7 +821,9 @@
         value = jnp.zeros((pieces * srows, width), F32)
         for at, entry in entries:
             value = jnp.where(line == at, entry, value)
-        dsmall[...] = value.reshape(pieces, srows, width).astype(BF)
+        for half in range(2):
+            lanes = slice(half * (width // 2), (half + 1) * (width // 2))
+            dsmall[half] = value[:, lanes].reshape(pieces, srows, width // 2).astype(BF)
 
     prepare()
     units = []
@@ -775,53 +832,69 @@
             units.append((n * 3 + t, (hidden_units, hidden_units_back)[n], rows))
         units.append((n * 3 + 2, (down_grads, up_grads)[n], None))
 
-    @pl.loop(0, closing + 3 + offsets[-1])
+    @pl.loop(0, closing + 3 + late_at[-1])
     def _(tick):
-        for at, unit, rows in units:
-
-            @pl.when((tick < 6 * folds) & (lax.rem(tick, 6) == at))
-            def _():
-                unit(tick // 6, *(() if rows is None else (rows,)))
-
-        for t, rows in enumerate(tiles):
-
-            @pl.when(tick == 6 * folds + t)
-            def _():
-                close_hidden(rows)
-
-            @pl.when(tick == closing + t)
-            def _():
-                finish(rows)
-
-        @pl.when(tick == 6 * folds + 2)
-        def _():
-            out_grads()
-            normed_t[...] = h_ref[...].T
-
-        since = tick - lead
-        part = lax.rem(since, turn)
-        for at in range(2 * (pairs // subs)):
-
-            @pl.when((since >= 0) & (since < subs * turn) & (part == at))
-            def _():
-                attention(since // turn * (pairs // subs) + at // 2, at % 2)
-
-        back = tick - late + 1
-        back_part = lax.rem(back, turn)
-
-        @pl.when((back >= 0) & (back < subs * turn) & (back_part == 0))
-        def _():
-            join(back // turn)
-
-        for n in range(3):
-
-            @pl.when((back >= 0) & (back < subs * turn) & (back_part == 1 + n))
-            def _():
-                project_grads(back // turn, n)
-
-        @pl.when(tick == closing + 2)
-        def _():
-            small_grads()
+        @pl.when(tick < 6 * folds)
+        def _():
+            i = lax.div(tick, 6)
+            turn_now = tick - 6 * i
+            for at, unit, rows in units:
+
+                @pl.when(turn_now == at)
+                def _():
+                    unit(i, *(() if rows is None else (rows,)))
+
+        @pl.when((tick >= 6 * folds) & (tick < lead))
+        def _():
+            for t, rows in enumerate(tiles):
+
+                @pl.when(tick == 6 * folds + t)
+                def _():
+                    close_hidden(rows)
+
+            @pl.when(tick == 6 * folds + 2)
+            def _():
+                out_grads()
+                normed_t[...] = h_ref[...].T
+
+        @pl.when((tick >= lead) & (tick < lead + subs * turn))
+        def _():
+            since = tick - lead
+            group = lax.div(since, turn)
+            part = since - group * turn
+            for at in range(2 * (pairs // subs)):
+
+                @pl.when(part == at)
+                def _():
+                    attention(group * (pairs // subs) + at // 2, at % 2)
+
+        @pl.when((tick >= late - 1) & (tick < late - 1 + subs * turn))
+        def _():
+            since = tick - late + 1
+            group = lax.div(since, turn)
+            part = since - group * turn
+
+            @pl.when(part == 0)
+            def _():
+                join(group)
+
+            for n in range(3):
+
+                @pl.when(part == 1 + n)
+                def _():
+                    project_grads(group, n)
+
+        @pl.when((tick >= closing) & (tick < closing + 3))
+        def _():
+            for t, rows in enumerate(tiles):
+
+                @pl.when(tick == closing + t)
+                def _():
+                    finish(rows)
+
+            @pl.when(tick == closing + 2)
+            def _():
+                small_grads()
 
         for kind, (src, dst, first) in enumerate(
             ((out_rows, tokens_ref, 6 * folds + 2), (drows, grad_ref, closing + 2))
@@ -833,7 +906,13 @@
             def _():
                 row_send_part(src, dst, kind, (tick - first) // 2)
 
-        communicate(tick)
+        @pl.when(tick < early_end)
+        def _():
+            move_early(tick)
+
+        @pl.when(tick >= late)
+        def _():
+            move_late(tick)
 
     sent(cot_ref, dy_ref, 1)
 
@@ -846,7 +925,6 @@
 def whole_block(
     tokens, cotangent, wqkv, ada, wout, up, down, info, gain_one, gain_two, down_bias, ada_bias,
     up_bias, cosines, sines, wide_size, ring,
-    lags=(2, 4, 3, 2),
 ):
     groups, span, width = tokens.shape
     count = groups * span
@@ -855,16 +933,21 @@
     half = width // 2
     folds = up.shape[1] // width
     subs = width // 256
-    blocks = 2 * folds + 4
-    chunks = blocks * subs
+    early = 2 * folds + 1
+    blocks = early + 3
+    late = 3 * subs
     pairs = width // 128
-    total_bits = pieces.bit_length() - 1
-    first = list(lags[:3]) + [lags[3]] * (total_bits - 2)
-    lags = tuple(first + first[::-1])
-    assert subs * 256 == width and subs == 3 and sum(lags) > 16
+    outer = (wide_size // 2).bit_length() - 1
+    bits = EARLY[1:2] + EARLY[2:3] * (outer - 1)
+    early_lags = EARLY[:1] + bits + EARLY[3:4] * 2 + bits[::-1] + EARLY[4:]
+    late_lags = LATE[:1] + LATE[1:2] * (2 * outer + 2) + LATE[2:]
+    assert subs * 256 == width and subs == 3 and sum(late_lags) > 16
+    assert 26 + sum(early_lags) < 50 + sum(late_lags)
     seqs = wide_size * groups
     srows = -(-(seqs * 7 + 3 + folds) // (pieces * 8)) * 8
-    sizes = [pieces >> (i + 1) for i in range(total_bits)]
+    sizes = [pieces >> (i + 1) for i in range(outer)]
+    tail = (rows, 128)
+    small = (srows, half)
     any_space = pl.BlockSpec(memory_space=pl.ANY)
     vmem = pl.BlockSpec(memory_space=pltpu.VMEM)
     block = jax.ShapeDtypeStruct((groups, span, width), BF)
@@ -874,12 +957,12 @@
     turned = pltpu.VMEM((width, count), BF)
     vectors = pltpu.VMEM((8, width), F32)
     return pl.pallas_call(
-        functools.partial(block_kernel, groups, wide_size, ring, lags),
+        functools.partial(block_kernel, groups, wide_size, ring, early_lags, late_lags),
         in_specs=[any_space] * 7 + [vmem] * 8,
         out_specs=[any_space] * 4,
         out_shape=[
-            jax.ShapeDtypeStruct((blocks, pieces, rows, width), BF),
-            jax.ShapeDtypeStruct((pieces, srows, width), BF),
+            jax.ShapeDtypeStruct((blocks, subs, 2, pieces, rows, 128), BF),
+            jax.ShapeDtypeStruct((2, pieces, srows, half), BF),
             block,
             block,
         ],
@@ -895,10 +978,10 @@
             pltpu.VMEM((-(-(9 + folds) // 8) * 8, width), F32),
             pltpu.VMEM((width, width), BF),
             pltpu.VMEM((4, width, width), BF),
-            pltpu.VMEM((4, pieces, rows, width), BF),
-            pltpu.VMEM((pieces, srows, width), BF),
+            pltpu.VMEM((4, subs, 2, pieces, rows, 128), BF),
+            pltpu.VMEM((2, pieces, srows, half), BF),
             rows_full,
-            rows_full,
+            rows_low,
             rows_low,
             turned,
             rows_low,
@@ -915,12 +998,24 @@
             pltpu.VMEM((count, 3 * width), BF),
             rows_low,
             rows_low,
-            pltpu.VMEM((chunks, pieces, rows, 128), BF),
-            pltpu.VMEM((pieces, srows, half), BF),
-            pltpu.VMEM((2 * lags[0] + 1, pieces, rows, 128), BF),
-            pltpu.VMEM((pieces, srows, half), BF),
-            [pltpu.VMEM((chunks, n, rows, 128), BF) for n in sizes],
-            [pltpu.VMEM((n, srows, half), BF) for n in sizes],
+            [
+                pltpu.VMEM((early, subs, pieces) + tail, BF),
+                pltpu.VMEM((2, subs, pieces) + tail, BF),
+                pltpu.VMEM((early, ring - 1, subs, 1) + tail, BF),
+                [pltpu.VMEM((early, subs, n) + tail, BF) for n in sizes],
+            ],
+            [
+                pltpu.VMEM((late, pieces) + tail, BF),
+                pltpu.VMEM((2 * LATE[0] + 1, pieces) + tail, BF),
+                pltpu.VMEM((late, ring - 1, 1) + tail, BF),
+                [pltpu.VMEM((late, n) + tail, BF) for n in sizes],
+            ],
+            [
+                pltpu.VMEM((pieces,) + small, BF),
+                pltpu.VMEM((pieces,) + small, BF),
+                pltpu.VMEM((ring - 1, 1) + small, BF),
+                [pltpu.VMEM((n,) + small, BF) for n in sizes],
+            ],
             DMA((7,)),
             DMA((4,)),
             DMA((2,)),
@@ -930,9 +1025,13 @@
             DMA((2, groups)),
             DMA((2, groups)),
             DMA((2, groups)),
-            DMA((chunks + 1,)),
-            DMA((2 + 2 * total_bits, chunks + 1)),
-            DMA((2 + 2 * total_bits, chunks + 1)),
+            DMA((early + late + 1,)),
+            DMA((2 + 2 * outer, early + late + 1)),
+            DMA((2 + 2 * outer, early + late + 1)),
+            DMA((ring - 1, early + late + 1)),
+            DMA((ring - 1, early + late + 1)),
+            DMA((ring - 1, early + late + 1)),
+            DMA((ring - 1, early + late + 1)),
             DMA((2, pairs)),
             DMA((2, pairs)),
             DMA((2, 8)),
@@ -956,20 +1055,21 @@
     ada_bias_ref, gain_one_ref, gain_two_ref, up_bias_ref, down_bias_ref,
     taken, wide, take_sem, give_sem,
 ):
-    blocks, width = sum_ref.shape[0], sum_ref.shape[-1]
+    blocks, subs, _, width, _ = sum_ref.shape
+    small = jnp.concatenate([small_ref[0], small_ref[1]], axis=1)
     order = list(range(blocks))
     takes = [pltpu.make_async_copy(sum_ref.at[n], taken.at[n], take_sem.at[n]) for n in order]
     for take in takes:
         take.start()
-    cond = small_ref[6 * seqs : 7 * seqs, : 3 * TEMB]
+    cond = small[6 * seqs : 7 * seqs, : 3 * TEMB]
     for n in range(6):
-        mod = small_ref[n * seqs : (n + 1) * seqs, :]
+        mod = small[n * seqs : (n + 1) * seqs, :]
         three = dot(mod, cond, ((0,), (0,)))
         ada_ref[n * width : (n + 1) * width, :] = (
             three[:, :TEMB] + three[:, TEMB : 2 * TEMB] + three[:, 2 * TEMB :]
         )
         ada_bias_ref[n * width : (n + 1) * width] = jnp.sum(mod.astype(F32), axis=0)
-    rows = small_ref[7 * seqs : 7 * seqs + 8 * (-(-(3 + folds) // 8)), :].astype(F32)
+    rows = small[7 * seqs : 7 * seqs + 8 * (-(-(3 + folds) // 8)), :].astype(F32)
     gain_one_ref[...] = rows[0]
     gain_two_ref[...] = rows[1]
     down_bias_ref[...] = rows[2]
@@ -991,7 +1091,10 @@
         @pl.loop(0, width // 32)
         def _(r):
             lines = pl.ds(pl.multiple_of(r * 32, 32), 32)
-            wide[n, lines, :] = taken[n, lines, :].astype(F32)
+            for m in range(subs):
+                for half in range(2):
+                    lanes = slice((2 * m + half) * 128, (2 * m + half + 1) * 128)
+                    wide[n, lines, lanes] = taken[n, m, half, lines].astype(F32)
 
         gives[n].start()
     for give in gives:
@@ -999,7 +1102,7 @@
 
 
 def spread(summed, small, seqs, folds):
-    blocks, width = summed.shape[0], summed.shape[-1]
+    blocks, _, _, width, _ = summed.shape
     any_space = pl.BlockSpec(memory_space=pl.ANY)
     vmem = pl.BlockSpec(memory_space=pltpu.VMEM)
     shapes = [
@@ -1012,7 +1115,7 @@
         out_specs=[vmem] + [any_space] * 4 + [vmem] * 5,
         out_shape=[jax.ShapeDtypeStruct(shape, F32) for shape in shapes],
         scratch_shapes=[
-            pltpu.VMEM((blocks, width, width), BF),
+            pltpu.VMEM(summed.shape, BF),
             pltpu.VMEM((blocks, width, width), F32),
             DMA((blocks,)),
             DMA((blocks,)),
@@ -1045,7 +1148,10 @@
         norm1_gain, norm2_gain, down_bias, ada_bias, up_bias, cosines, sines, wide_size, ring,
     )
     ada, qkv, out, up, down, ada_bias_grad, gain_one, gain_two, up_bias_grad, down_bias_grad = (
-        spread(summed.reshape(-1, width, width), small.reshape(-1, width), seqs, folds)
+        spread(
+            summed.reshape(-1, width // 256, 2, width, 128), small.reshape(2, -1, width // 2), seqs,
+            folds,
+        )
     )
     return (
         outputs, input_grad, ada, ada_bias_grad, gain_one, qkv, out, gain_two, up, up_bias_grad,

time: 246 us -> 226 us (0.919)
  Pallas kernels: 241 us -> 221 us
    pallas_call x1, Pallas kernels: 225 us -> 205 us  [whole_block(): pl.pallas_call(functools.partial(block_kernel, groups, wide_size, ring, e...]
where the time goes in v5:
time: 226 us
  Pallas kernels  221 us (98%)
    pallas_call x1, Pallas kernels, whole_block(): pl.pallas_call(functools.partial(block_kernel, groups, wide_size, ring, e...  205 us
    pallas_call x1, Pallas kernels, spread(): pl.pallas_call(functools.partial(spread_kernel, seqs, folds), in_specs=[a...  16 us

profile of v5, /device:TPU:1, one launch (start us, length us, event | category | flops | bytes accessed | tf_op | source)
XLA Modules:
  0.0 226.1 jit_solution(17696700492847631100)
XLA Ops:
  0.6 0.7 convert_element_type.3
  1.3 0.1 multiply_cosine_fusion
  1.4 0.1 divide_multiply_fusion
  1.5 0.8 or_select_fusion
  2.3 0.6 pad_maximum_fusion.info_ref
  2.9 205.4 %whole_block.1 = (bf16[12,3,2,16,48,128]{5,4,3,2,1,0:T(8,128)(2,1)}, bf16[2,16,8,384]{3,2,1,0:T(8,128)(2,1)}, bf16[2,256,768]{2,1,0:T(8,128)(2,1)}, bf16[2,256,768]{2,1,0:T(8,128)(2,1)}) custom-call(bf16[2,256,768]{2,1,0:T(8,128)(2,1)} %tok_ref.1, bf16[2,256,768]{2,1,0:T(8,128)(2,1)} %cot_ref.1, bf16[768,2304]{1,0:T(8,128)(2,1)} %wqkv_ref.1, ...), custom_call_target="tpu_custom_call" | custom-call | tf_op jit(solution)/shard_map/whole_block/pallas_call | solution.py:959
  208.3 0.0 copy-start.1
  208.3 0.0 copy-start
  208.3 16.0 %spread.1 = (f32[4608,128]{1,0:T(8,128)}, f32[768,2304]{1,0:T(8,128)}, f32[768,768]{1,0:T(8,128)}, f32[768,3072]{1,0:T(8,128)}, f32[3072,768]{1,0:T(8,128)}, /*i...) custom-call(bf16[12,3,2,768,128]{4,3,2,1,0:T(8,128)(2,1)} %bitcast.2, ...), custom_call_target="tpu_custom_call" | custom-call | tf_op jit(solution)/shard_map/spread/pallas_call | solution.py:1112
  224.3 0.0 copy-done.1
  224.3 0.9 copy.31
  225.2 0.0 copy-done
  225.2 0.9 copy.32
  (1 shorter events, 0.0 us)
Async XLA Ops:
  208.3 16.1 %copy-start.1 = (bf16[2,256,768]{2,1,0:T(8,128)(2,1)S(1)}, bf16[2,256,768]{2,1,0:T(8,128)(2,1)}, u32[]{:S(2)}) copy-start(bf16[2,256,768]{2,1,0:T(8,128)(2,1)} %get-tuple-element.54) | copy-start | bytes 2359300
  208.3 16.9 %copy-start = (bf16[2,256,768]{2,1,0:T(8,128)(2,1)S(1)}, bf16[2,256,768]{2,1,0:T(8,128)(2,1)}, u32[]{:S(2)}) copy-start(bf16[2,256,768]{2,1,0:T(8,128)(2,1)} %get-tuple-element.55) | copy-start | bytes 2359300

commit v6 on v5

--- a/solution.py
+++ b/solution.py
@@ -81,7 +81,7 @@
     x_ref, dy_ref, h_ref, q_ref, ka_ref, va_ref, kb_ref, vb_ref, o_ref, ot_ref, lse_ref, mod_ref,
     ba_ref, bb_ref, cond_ref, table, par_ref, wout,
     weights, staging, dsmall, middle, branch, normed_low, normed_t, dm, total_a, total_b, active,
-    slope, dq_t, deltas, vec, dup_bias, out_rows, drows, dqkv, dk_in, dv_in,
+    slope, dq_t, deltas, vec, dup_bias, out_rows, dqkv, dk_in, dv_in,
     early_buffers, late_buffers, small_buffers,
     load_sem, weight_sem, take_self, info_send, info_recv, take_send, take_recv, swap_send,
     swap_recv, copy_sem, send_sem, recv_sem, ring_send, ring_recv, gather_send, gather_recv, kv_send, kv_recv, self_sem, row_send, row_recv,
@@ -503,10 +503,10 @@
 
     early_at = [2 + sum(early_lags[:step]) for step in range(last + 1)]
     late_at = [sum(late_lags[:step]) for step in range(last + 1)]
-    turn = 2 * (pairs // subs) + subs
+    per_group = pairs // subs
+    turn = 2 * per_group + 2
     lead = 6 * folds + 3
-    late = lead + turn - 2
-    closing = lead + subs * turn + 1
+    closing = lead + subs * turn
 
     def pick_early(ref, start, size):
         return ref.at[:, pl.ds(start, size)]
@@ -514,55 +514,57 @@
     def pick_late(ref, start, size):
         return ref.at[pl.ds(start, size)]
 
-    early_end = 3 * early + early_at[-1]
-
-    def move_early(tick):
-        turn_now = lax.rem(tick, 3)
+    def early_stage(step, chunk, odd):
+        total, core_slots, ring_slots, bit_slots = early_buffers
+        stage(
+            step, odd, chunk, pick_early,
+            lambda half: staging.at[chunk % stages, :, half],
+            lambda half: sum_ref.at[chunk, :, half],
+            total.at[chunk], core_slots.at[odd], ring_slots.at[chunk],
+            [ref.at[chunk] for ref in bit_slots],
+        )
+
+    def late_stage(step, group, part):
+        chunk = group * 3 + part
+        total, core_slots, ring_slots, bit_slots = late_buffers
+        stage(
+            step, (group + part) % 2, early + chunk, pick_late,
+            lambda half: staging.at[(early + part) % stages, group, half],
+            lambda half: sum_ref.at[early + part, group, half],
+            total.at[chunk], core_slots.at[chunk % core_slots.shape[0]],
+            ring_slots.at[chunk], [ref.at[chunk] for ref in bit_slots],
+        )
+
+    def small_stage(step):
+        stage(
+            step, 0, early + late_count, pick_late,
+            lambda half: dsmall.at[half], lambda half: ssum_ref.at[half], *small_buffers
+        )
+
+    def move_on(tick, turns, repeat, period):
         for step in range(last, -1, -1):
             since = tick - early_at[step]
-
-            @pl.when(
-                (since >= 0) & (since < 3 * early) & (turn_now == early_at[step] % 3)
-            )
-            def _():
-                chunk = lax.div(since, 3)
-                total, core_slots, ring_slots, bit_slots = early_buffers
-                stage(
-                    step, lax.rem(chunk, 2), chunk, pick_early,
-                    lambda half: staging.at[lax.rem(chunk, stages), :, half],
-                    lambda half: sum_ref.at[chunk, :, half],
-                    total.at[chunk], core_slots.at[lax.rem(chunk, 2)], ring_slots.at[chunk],
-                    [ref.at[chunk] for ref in bit_slots],
-                )
-
-    def move_late(tick):
-        turn_now = lax.rem(tick, turn)
+            first = since // 3
+            if since % 3 == 0 and first + (turns - 1) * period // 3 >= 0 and first < early:
+                chunk = first + repeat * (period // 3)
+                one = functools.partial(early_stage, step, chunk, first % 2)
+                if first >= 0 and first + (turns - 1) * period // 3 < early:
+                    one()
+                else:
+                    pl.when((chunk >= 0) & (chunk < early))(one)
         for step in range(last, -1, -1):
-            at = tick - late_at[step] - late
-            zero = (late_at[step] + late) % turn
-            on = [turn_now == (zero + n) % turn for n in range(3)]
-
-            @pl.when((at >= 0) & (at < subs * turn) & (on[0] | on[1] | on[2]))
-            def _():
-                group = lax.div(at, turn)
-                part = at - group * turn
-                chunk = group * 3 + part
-                block = early + part
-                total, core_slots, ring_slots, bit_slots = late_buffers
-                stage(
-                    step, lax.rem(chunk, 2), early + chunk, pick_late,
-                    lambda half: staging.at[lax.rem(block, stages), group, half],
-                    lambda half: sum_ref.at[block, group, half],
-                    total.at[chunk], core_slots.at[lax.rem(chunk, core_slots.shape[0])],
-                    ring_slots.at[chunk], [ref.at[chunk] for ref in bit_slots],
-                )
-
-            @pl.when(tick == closing + 2 + late_at[step])
-            def _():
-                stage(
-                    step, 0, early + late_count, pick_late,
-                    lambda half: dsmall.at[half], lambda half: ssum_ref.at[half], *small_buffers
-                )
+            for part in range(3):
+                since = tick - (lead + 2 * per_group + part) - late_at[step]
+                first = since // turn
+                if since % turn == 0 and first + (turns - 1) * period // turn >= 0 and first < subs:
+                    group = first + repeat * (period // turn)
+                    one = functools.partial(late_stage, step, group, part)
+                    if first >= 0 and first + (turns - 1) * period // turn < subs:
+                        one()
+                    else:
+                        pl.when((group >= 0) & (group < subs))(one)
+            if turns == 1 and tick == closing + 2 + late_at[step]:
+                small_stage(step)
 
     def place_block(block, part, value):
         for half in range(2):
@@ -605,9 +607,10 @@
         tanh = jnp.tanh(gelu_coeff * (u + 0.044715 * u * square))
         g = (0.5 * u * (1.0 + tanh)).astype(BF)
         active[rows, :] = g
-        slope[rows, :] = 0.5 * (1.0 + tanh) + (0.5 * gelu_coeff) * u * (1.0 - tanh * tanh) * (
-            1.0 + (3 * 0.044715) * square
-        )
+        slope[rows, :] = (
+            0.5 * (1.0 + tanh)
+            + (0.5 * gelu_coeff) * u * (1.0 - tanh * tanh) * (1.0 + (3 * 0.044715) * square)
+        ).astype(BF)
         part = dot(g, weights[slot + 1], ((1,), (0,)))
 
         @pl.when(i == 0)
@@ -628,7 +631,7 @@
     def hidden_units_back(i, rows):
         slot = 2 * lax.rem(i, 2)
         dg = dot(dm[rows, :], weights[slot + 1], ((1,), (1,)))
-        du = (dg * slope[rows, :]).astype(BF)
+        du = (dg * slope[rows, :].astype(F32)).astype(BF)
         active[rows, :] = du
         total = jnp.sum(du.astype(F32), axis=0, keepdims=True)
         part = dot(du, weights[slot], ((1,), (1,)))
@@ -665,7 +668,7 @@
                 2 * i + 1, m // 256, dot(normed_t[...], active[:, cols], ((1,), (0,))).astype(BF)
             )
 
-    def close_hidden(rows):
+    def close_hidden_rows(rows):
         m = total_a[rows, :] + par_ref[2:3, :]
         x1 = middle[rows, :]
         out_rows[rows, :] = (x1 + gate_two * m).astype(BF)
@@ -686,6 +689,10 @@
             line = slice(i, i + 1)
             vec[line, :] = total if rows is tiles[0] else vec[line, :] + total
         active[rows, :] = dot(da, wout[...], ((1,), (1,))).astype(BF)
+
+    def close_hidden(all_tiles):
+        for rows in all_tiles:
+            close_hidden_rows(rows)
 
     def out_grads():
         vec[4:5, :] = vec[2:3, :] * (1.0 + scale_two)
@@ -782,7 +789,7 @@
         )
         n1, rscale = normed_rows(x_ref[rows, :].astype(F32))
         e = dh * (scale * gain_one)
-        drows[rows, :] = (
+        active[rows, :] = (
             middle[rows, :]
             + rscale
             * (
@@ -826,100 +833,62 @@
             dsmall[half] = value[:, lanes].reshape(pieces, srows, width // 2).astype(BF)
 
     prepare()
-    units = []
-    for n in range(2):
-        for t, rows in enumerate(tiles):
-            units.append((n * 3 + t, (hidden_units, hidden_units_back)[n], rows))
-        units.append((n * 3 + 2, (down_grads, up_grads)[n], None))
-
-    @pl.loop(0, closing + 3 + late_at[-1])
-    def _(tick):
-        @pl.when(tick < 6 * folds)
-        def _():
-            i = lax.div(tick, 6)
-            turn_now = tick - 6 * i
-            for at, unit, rows in units:
-
-                @pl.when(turn_now == at)
+
+    @pl.loop(0, folds)
+    def _(i):
+        for u in range(6):
+            unit = (hidden_units, hidden_units_back)[u // 3]
+            if u % 3 == 2:
+                (down_grads, up_grads)[u // 3](i)
+            else:
+                for rows in tiles[u % 3 :: 2]:
+                    unit(i, rows)
+            move_on(u, folds, i, 6)
+
+    close_hidden(tiles)
+    move_on(lead - 3, 1, 0, 0)
+    move_on(lead - 2, 1, 0, 0)
+    out_grads()
+    normed_t[...] = h_ref[...].T
+    move_on(lead - 1, 1, 0, 0)
+
+    @pl.loop(0, subs)
+    def _(group):
+        for u in range(turn):
+            if u < 2 * per_group:
+                attention(group * per_group + u // 2, u % 2)
+            elif u == 2 * per_group:
+                join(group)
+                project_grads(group, 0)
+            else:
+                project_grads(group, 1)
+                project_grads(group, 2)
+            if u % 2 == 0:
+                part = group * (turn // 2) + u // 2
+
+                @pl.when(part < parts)
                 def _():
-                    unit(i, *(() if rows is None else (rows,)))
-
-        @pl.when((tick >= 6 * folds) & (tick < lead))
-        def _():
-            for t, rows in enumerate(tiles):
-
-                @pl.when(tick == 6 * folds + t)
-                def _():
-                    close_hidden(rows)
-
-            @pl.when(tick == 6 * folds + 2)
-            def _():
-                out_grads()
-                normed_t[...] = h_ref[...].T
-
-        @pl.when((tick >= lead) & (tick < lead + subs * turn))
-        def _():
-            since = tick - lead
-            group = lax.div(since, turn)
-            part = since - group * turn
-            for at in range(2 * (pairs // subs)):
-
-                @pl.when(part == at)
-                def _():
-                    attention(group * (pairs // subs) + at // 2, at % 2)
-
-        @pl.when((tick >= late - 1) & (tick < late - 1 + subs * turn))
-        def _():
-            since = tick - late + 1
-            group = lax.div(since, turn)
-            part = since - group * turn
-
-            @pl.when(part == 0)
-            def _():
-                join(group)
-
-            for n in range(3):
-
-                @pl.when(part == 1 + n)
-                def _():
-                    project_grads(group, n)
-
-        @pl.when((tick >= closing) & (tick < closing + 3))
-        def _():
-            for t, rows in enumerate(tiles):
-
-                @pl.when(tick == closing + t)
-                def _():
-                    finish(rows)
-
-            @pl.when(tick == closing + 2)
-            def _():
-                small_grads()
-
-        for kind, (src, dst, first) in enumerate(
-            ((out_rows, tokens_ref, 6 * folds + 2), (drows, grad_ref, closing + 2))
-        ):
-
-            @pl.when(
-                (tick >= first) & (tick < first + 2 * parts) & (lax.rem(tick - first, 2) == 0)
-            )
-            def _():
-                row_send_part(src, dst, kind, (tick - first) // 2)
-
-        @pl.when(tick < early_end)
-        def _():
-            move_early(tick)
-
-        @pl.when(tick >= late)
-        def _():
-            move_late(tick)
+                    row_send_part(out_rows, tokens_ref, 0, part)
+
+            move_on(lead + u, subs, group, turn)
+
+    for tick in range(closing, closing + 3 + late_at[-1]):
+        if tick < closing + 2:
+            for rows in tiles[tick - closing :: 2]:
+                finish(rows)
+        elif tick == closing + 2:
+            small_grads()
+        part = tick - closing - 2
+        if part >= 0 and part % 2 == 0 and part // 2 < parts:
+            row_send_part(active, grad_ref, 1, part // 2)
+        move_on(tick, 1, 0, 0)
 
     sent(cot_ref, dy_ref, 1)
 
     @pl.loop(0, parts)
     def _(q):
         row_wait_part(out_rows, tokens_ref, 0, q)
-        row_wait_part(drows, grad_ref, 1, q)
+        row_wait_part(active, grad_ref, 1, q)
 
 
 def whole_block(
@@ -942,7 +911,7 @@
     early_lags = EARLY[:1] + bits + EARLY[3:4] * 2 + bits[::-1] + EARLY[4:]
     late_lags = LATE[:1] + LATE[1:2] * (2 * outer + 2) + LATE[2:]
     assert subs * 256 == width and subs == 3 and sum(late_lags) > 16
-    assert 26 + sum(early_lags) < 50 + sum(late_lags)
+    assert 26 + sum(early_lags) < 48 + sum(late_lags) and folds % 2 == 0
     seqs = wide_size * groups
     srows = -(-(seqs * 7 + 3 + folds) // (pieces * 8)) * 8
     sizes = [pieces >> (i + 1) for i in range(outer)]
@@ -988,12 +957,11 @@
             rows_full,
             rows_full,
             rows_low,
-            rows_full,
+            rows_low,
             pltpu.VMEM((128, count), F32),
             pltpu.VMEM((8, count), F32),
             vectors,
             vectors,
-            rows_low,
             rows_low,
             pltpu.VMEM((count, 3 * width), BF),
             rows_low,

time: 226 us -> 217 us (0.960)
  Pallas kernels: 221 us -> 212 us
    pallas_call x1, Pallas kernels: 205 us -> 195 us  [whole_block(): pl.pallas_call(functools.partial(block_kernel, groups, wide_size, ring, e...]
where the time goes in v6:
time: 217 us; the launch traced here: 216 us
  Pallas kernels  212 us (98%)
  other arithmetic  2.25 us (1%)
    pallas_call x1, Pallas kernels, whole_block(): pl.pallas_call(functools.partial(block_kernel, groups, wide_size, ring, e...  195 us
    pallas_call x1, Pallas kernels, spread(): pl.pallas_call(functools.partial(spread_kernel, seqs, folds), in_specs=[a...  16 us

profile of v6, /device:TPU:1, one launch (start us, length us, event | category | flops | bytes accessed | tf_op | source)
XLA Modules:
  0.0 216.2 jit_solution(11551874009495832676)
XLA Ops:
  0.6 0.7 convert_element_type.3
  1.3 0.1 multiply_cosine_fusion
  1.4 0.1 divide_multiply_fusion
  1.5 0.8 or_select_fusion
  2.3 0.6 pad_maximum_fusion.info_ref
  2.9 195.5 %whole_block.1 = (bf16[12,3,2,16,48,128]{5,4,3,2,1,0:T(8,128)(2,1)}, bf16[2,16,8,384]{3,2,1,0:T(8,128)(2,1)}, bf16[2,256,768]{2,1,0:T(8,128)(2,1)}, bf16[2,256,768]{2,1,0:T(8,128)(2,1)}) custom-call(bf16[2,256,768]{2,1,0:T(8,128)(2,1)} %tok_ref.1, bf16[2,256,768]{2,1,0:T(8,128)(2,1)} %cot_ref.1, bf16[768,2304]{1,0:T(8,128)(2,1)} %wqkv_ref.1, ...), custom_call_target="tpu_custom_call" | custom-call | tf_op jit(solution)/shard_map/whole_block/pallas_call | solution.py:928
  198.4 0.0 copy-start.1
  198.4 0.0 copy-start
  198.4 16.0 %spread.1 = (f32[4608,128]{1,0:T(8,128)}, f32[768,2304]{1,0:T(8,128)}, f32[768,768]{1,0:T(8,128)}, f32[768,3072]{1,0:T(8,128)}, f32[3072,768]{1,0:T(8,128)}, /*i...) custom-call(bf16[12,3,2,768,128]{4,3,2,1,0:T(8,128)(2,1)} %bitcast.2, ...), custom_call_target="tpu_custom_call" | custom-call | tf_op jit(solution)/shard_map/spread/pallas_call | solution.py:1080
  214.5 0.0 copy-done.1
  214.5 0.9 copy.31
  215.3 0.0 copy-done
  215.3 0.9 copy.32
  (1 shorter events, 0.0 us)
Async XLA Ops:
  198.4 16.1 %copy-start.1 = (bf16[2,256,768]{2,1,0:T(8,128)(2,1)S(1)}, bf16[2,256,768]{2,1,0:T(8,128)(2,1)}, u32[]{:S(2)}) copy-start(bf16[2,256,768]{2,1,0:T(8,128)(2,1)} %get-tuple-element.54) | copy-start | bytes 2359300
  198.4 16.9 %copy-start = (bf16[2,256,768]{2,1,0:T(8,128)(2,1)S(1)}, bf16[2,256,768]{2,1,0:T(8,128)(2,1)}, u32[]{:S(2)}) copy-start(bf16[2,256,768]{2,1,0:T(8,128)(2,1)} %get-tuple-element.55) | copy-start | bytes 2359300

commit v7 on v6

--- a/solution.py
+++ b/solution.py
@@ -879,8 +879,8 @@
         elif tick == closing + 2:
             small_grads()
         part = tick - closing - 2
-        if part >= 0 and part % 2 == 0 and part // 2 < parts:
-            row_send_part(active, grad_ref, 1, part // 2)
+        if part >= 0 and part % 3 == 0 and part // 3 < parts:
+            row_send_part(active, grad_ref, 1, part // 3)
         move_on(tick, 1, 0, 0)
 
     sent(cot_ref, dy_ref, 1)

time: 217 us -> 216 us (level)
  no operation moved by 1% of the time
where the time goes in v7:
time: 216 us
  Pallas kernels  211 us (98%)
  other arithmetic  2.25 us (1%)
    pallas_call x1, Pallas kernels, whole_block(): pl.pallas_call(functools.partial(block_kernel, groups, wide_size, ring, e...  195 us
    pallas_call x1, Pallas kernels, spread(): pl.pallas_call(functools.partial(spread_kernel, seqs, folds), in_specs=[a...  16 us

profile of v7, /device:TPU:1, one launch (start us, length us, event | category | flops | bytes accessed | tf_op | source)
XLA Modules:
  0.0 216.0 jit_solution(1570173237982681101)
XLA Ops:
  0.6 0.7 convert_element_type.3
  1.3 0.1 multiply_cosine_fusion
  1.4 0.1 divide_multiply_fusion
  1.5 0.8 or_select_fusion
  2.3 0.6 pad_maximum_fusion.info_ref
  2.9 195.3 %whole_block.1 = (bf16[12,3,2,16,48,128]{5,4,3,2,1,0:T(8,128)(2,1)}, bf16[2,16,8,384]{3,2,1,0:T(8,128)(2,1)}, bf16[2,256,768]{2,1,0:T(8,128)(2,1)}, bf16[2,256,768]{2,1,0:T(8,128)(2,1)}) custom-call(bf16[2,256,768]{2,1,0:T(8,128)(2,1)} %tok_ref.1, bf16[2,256,768]{2,1,0:T(8,128)(2,1)} %cot_ref.1, bf16[768,2304]{1,0:T(8,128)(2,1)} %wqkv_ref.1, ...), custom_call_target="tpu_custom_call" | custom-call | tf_op jit(solution)/shard_map/whole_block/pallas_call | solution.py:928
  198.2 0.0 copy-start.1
  198.2 0.0 copy-start
  198.2 16.0 %spread.1 = (f32[4608,128]{1,0:T(8,128)}, f32[768,2304]{1,0:T(8,128)}, f32[768,768]{1,0:T(8,128)}, f32[768,3072]{1,0:T(8,128)}, f32[3072,768]{1,0:T(8,128)}, /*i...) custom-call(bf16[12,3,2,768,128]{4,3,2,1,0:T(8,128)(2,1)} %bitcast.2, ...), custom_call_target="tpu_custom_call" | custom-call | tf_op jit(solution)/shard_map/spread/pallas_call | solution.py:1080
  214.2 0.0 copy-done.1
  214.2 0.9 copy.31
  215.1 0.0 copy-done
  215.1 0.9 copy.32
  (1 shorter events, 0.0 us)
Async XLA Ops:
  198.2 16.1 %copy-start.1 = (bf16[2,256,768]{2,1,0:T(8,128)(2,1)S(1)}, bf16[2,256,768]{2,1,0:T(8,128)(2,1)}, u32[]{:S(2)}) copy-start(bf16[2,256,768]{2,1,0:T(8,128)(2,1)} %get-tuple-element.54) | copy-start | bytes 2359300
  198.2 16.9 %copy-start = (bf16[2,256,768]{2,1,0:T(8,128)(2,1)S(1)}, bf16[2,256,768]{2,1,0:T(8,128)(2,1)}, u32[]{:S(2)}) copy-start(bf16[2,256,768]{2,1,0:T(8,128)(2,1)} %get-tuple-element.55) | copy-start | bytes 2359300
